TPU v7x, 256 devices: a whole 4x4x8 slice. The times are simulated.
256 devices in a mesh: seq: 64 (over z, x, core), tp: 4 (over y).
Axes of the slice: x: 4, y: 4, z: 8, core: 2. Of those that a mesh axis runs over, the one named last changes fastest.
Arguments:
- tokens: bfloat16 [32768, 2048], P('seq', 'tp'), may hold values from -6 to 6
- norm_gain: float32 [2048], replicated, may hold values from 0.1 to 1.9
- w_query: bfloat16 [2048, 2048], P(None, 'tp'), may hold values from -0.125 to 0.125
- w_keyval: bfloat16 [2048, 256], replicated, may hold values from -0.125 to 0.125
- w_out: bfloat16 [2048, 2048], P('tp'), may hold values from -0.5 to 0.5
- span_lens: int32 [64], P('seq'), may hold values from 1 to 512, 24576 in all
- cached_lens: int32 [64], P('seq'), may hold values from 1 to 1536, 49152 in all
- old_table: int32 [64, 64], P('seq'), may hold values from 0 to 63, each once within a row
- new_table: int32 [64, 64], P('seq'), may hold values from 0 to 63, each once within a row
- old_cache: bfloat16 [4096, 32, 256], P('seq', 'tp'), may hold values from -720 to 720
Outputs:
- mixed: bfloat16 [32768, 2048], P('seq', 'tp')
- new_cache: bfloat16 [4096, 32, 256], P('seq', 'tp')
Inputs may be any that keep to these rules, and one draw needn't show every extreme that they name: Request r's new tokens are the first span_lens[r] of its 512 rows. `old_table`: each row names every device once: each device holds exactly one block of every request. `new_table`: each row names every device once: each device receives exactly one block of every request.
All inputs are finite; a program needn't handle non-finite values. No bound on the sum of `span_lens` or of `cached_lens` on one device may be relied on, other than what follows from the above.
Results may differ from a plain program's by a relative error of at most 0.012.
The roundings to bfloat16 on the way count: a program that leaves them out, or rounds other values in their place, can miss the bound.
Values may be sent and summed in bfloat16 or wider, within the bound.
A program may use at most 128 MiB of HBM per device.

v0:
```python
import jax
import jax.numpy as jnp
from jax import lax
from jax.sharding import PartitionSpec as P

EPSILON = 1e-05
MASKED = -1e30


def normalize(rows, norm_gain):
    values = rows.astype(jnp.float32)
    average = jnp.mean(values, axis=1, keepdims=True)
    centred = values - average
    spread = jnp.mean(centred * centred, axis=1, keepdims=True)
    return (centred * lax.rsqrt(spread + EPSILON) * norm_gain).astype(jnp.bfloat16)


def body(
    tokens,
    norm_gain,
    w_query,
    w_keyval,
    w_out,
    span_lens,
    cached_lens,
    old_table,
    new_table,
    old_cache,
):
    full_rows = lax.all_gather(tokens, "tp", axis=1, tiled=True)
    normed = normalize(full_rows, norm_gain)
    query = jnp.dot(normed, w_query, preferred_element_type=jnp.float32).astype(jnp.bfloat16)
    keyval = jnp.dot(normed, w_keyval, preferred_element_type=jnp.float32).astype(jnp.bfloat16)
    groups = lax.axis_size("seq")
    tp_count = lax.axis_size("tp")
    holders = old_table[0]
    pooled = lax.all_gather(old_cache, "tp", axis=1, tiled=True)
    arrived = lax.all_to_all(pooled, "seq", split_axis=0, concat_axis=0, tiled=True)
    ordered = jnp.take(arrived, holders, axis=0)
    block_rows = ordered.shape[1]
    width = ordered.shape[2]
    capacity = groups * block_rows
    cached = ordered.reshape(capacity, width)
    held_len = cached_lens[0]
    span_len = span_lens[0]
    tok_rows = tokens.shape[0]
    share = block_rows // tp_count
    targets = new_table[0]
    device_ids = lax.broadcasted_iota(jnp.int32, (groups, groups), 0)
    block_ids = lax.broadcasted_iota(jnp.int32, (groups, groups), 1)
    matches = targets[None, :] == device_ids
    sources = jnp.sum(jnp.where(matches, block_ids, 0), axis=1)
    positions = lax.broadcasted_iota(jnp.int32, (capacity, 1), 0)
    placed = lax.dynamic_update_slice(cached, keyval, (held_len, jnp.int32(0)))
    fresh = jnp.where(positions < held_len + span_len, placed, jnp.zeros_like(placed))
    head_size = width // 2
    keys = fresh[:, :head_size]
    values = fresh[:, head_size:]
    local_heads = query.shape[1] // head_size
    query3 = query.reshape(tok_rows, local_heads, head_size)
    scores = jnp.einsum(
        "thd,kd->htk", query3, keys, preferred_element_type=jnp.float32
    ) * head_size ** (-0.5)
    row_pos = lax.broadcasted_iota(jnp.int32, (tok_rows, 1), 0)
    key_pos = lax.broadcasted_iota(jnp.int32, (1, capacity), 1)
    allowed = key_pos <= held_len + row_pos
    scores = jnp.where(allowed[None], scores, MASKED)
    top = jnp.max(scores, axis=2, keepdims=True)
    weights = jnp.exp(scores - top)
    probs = (weights / jnp.sum(weights, axis=2, keepdims=True)).astype(jnp.bfloat16)
    context = jnp.einsum("htk,kd->thd", probs, values, preferred_element_type=jnp.float32).astype(
        jnp.bfloat16
    )
    context = context.reshape(tok_rows, local_heads * head_size)
    partial_out = jnp.dot(context, w_out, preferred_element_type=jnp.float32)
    summed = lax.psum_scatter(
        partial_out.astype(jnp.bfloat16), "tp", scatter_dimension=1, tiled=True
    ).astype(jnp.float32)
    total = tokens.astype(jnp.float32) + summed
    mixed = jnp.where(row_pos < span_len, total, jnp.zeros_like(total)).astype(jnp.bfloat16)
    mine_part = lax.dynamic_slice_in_dim(
        fresh.reshape(groups, block_rows, width), lax.axis_index("tp") * share, share, 1
    )
    new_cache = lax.all_to_all(
        jnp.take(mine_part, sources, axis=0), "seq", split_axis=0, concat_axis=0, tiled=True
    )
    return (mixed, new_cache)


def solution(mesh):
    in_specs = (
        P("seq", "tp"),
        P(),
        P(None, "tp"),
        P(),
        P("tp", None),
        P("seq"),
        P("seq"),
        P("seq", None),
        P("seq", None),
        P("seq", "tp", None),
    )
    out_specs = (P("seq", "tp"), P("seq", "tp", None))
    return jax.shard_map(body, mesh=mesh, in_specs=in_specs, out_specs=out_specs, check_vma=False)
```

profile of v0, /device:TPU:1, one launch (start us, length us, event | category | flops | bytes accessed | tf_op | source)
XLA Modules:
  0.0 154.8 jit_solution(5848110831717273681)
XLA Ops:
  7.2 0.0 copy-start
  7.2 0.0 copy-start.4
  7.2 0.0 all-gather.3.cloned.1.call-start
  7.2 0.7 all-gather.3.cloned.1.call-update
  7.9 0.0 all-gather.5.cloned.1.call-start
  8.0 0.7 all-gather.5.cloned.1.call-update
  9.3 0.7 compare_and_fusion.1
  10.0 0.1 broadcast_in_dim.70
  10.1 0.1 broadcast_in_dim.71
  10.8 0.7 fusion.15
  11.5 1.8 %iota_compare_fusion = pred[512,2048]{0,1:T(8,128)(4,1)} fusion(s32[512]{0:T(512)S(1)} %iota_add_fusion), kind=kLoop, calls=%fused_computation.18 | loop fusion | flops 1048576 | bytes 1050624 | tf_op jit(solution)/shard_map/le | solution.py:66
  13.3 27.9 %all-gather.3.cloned.1.call-done = bf16[64,32,256]{2,1,0:T(8,128)(2,1)} async-done(((bf16[64,8,256]{2,1,0:T(8,128)(2,1)}), bf16[64,32,256]{2,1,0:T(8,128)(2,1)}) %all-gather.3.cloned.1.call-update) | async-done | bytes 1048592 | tf_op jit(solution)/shard_map/all_gather | solution.py:37
  41.2 11.5 %all-to-all-start = ((bf16[64,32,256]{2,1,0:T(8,128)(2,1)}), bf16[64,32,256]{2,1,0:T(8,128)(2,1)S(1)}, u32[]{:S(2)}, u32[]{:S(2)}) async-start(bf16[64,32,256]{2,1,0:T(8,128)(2,1)} %all-gather.3.cloned.1.call-done), calls=%async_computation | async-start | bytes 2097152 | tf_op jit(solution)/shard_map/all_to_all | solution.py:38
  52.8 0.0 reduce-scatter.2.cloned.1.call-start
  52.8 25.5 %all-gather.5.cloned.1.call-done = bf16[512,2048]{1,0:T(8,128)(2,1)} async-done(((bf16[512,512]{1,0:T(8,128)(2,1)}), bf16[512,2048]{1,0:T(8,128)(2,1)}) %all-gather.5.cloned.1.call-update) | async-done | bytes 2097168 | tf_op jit(solution)/shard_map/all_gather | solution.py:30
  78.3 0.0 copy-start.1
  78.3 0.0 copy-start.6
  78.3 2.1 %convert_reduce_fusion = f32[512]{0:T(512)S(1)} fusion(bf16[512,2048]{1,0:T(8,128)(2,1)} %all-gather.5.cloned.1.call-done), kind=kLoop, calls=%fused_computation.12 | loop fusion | flops 2096640 | bytes 2099200 | tf_op jit(solution)/shard_map/reduce_sum | solution.py:12
  80.4 2.3 %fusion.8 = f32[512]{0:T(512)S(1)} fusion(bf16[512,2048]{1,0:T(8,128)(2,1)} %all-gather.5.cloned.1.call-done, f32[512]{0:T(512)S(1)} %broadcast_multiply_fusion), kind=kLoop, calls=%fused_computation.15 | loop fusion | flops 4193792 | bytes 2101248 | tf_op jit(solution)/shard_map/reduce_sum | solution.py:14
  82.7 0.0 copy-start.5
  82.7 0.0 copy-done.4
  82.8 0.0 copy-done.1
  82.8 0.7 fusion.10
  83.5 0.0 copy-done.6
  83.5 0.7 convolution_convert_fusion.2
  84.2 0.1 copy-done.5
  84.3 2.1 %convolution_convert_fusion.1 = bf16[512,512]{0,1:T(8,128)(2,1)} fusion(bf16[512,2048]{1,0:T(8,128)(2,1)S(1)} %fusion.10, bf16[2048,512]{1,0:T(8,128)(2,1)S(1)} %copy-done.5), kind=kOutput, calls=%fused_computation.21 | convolution fusion | flops 1074003968 | bytes 4718592 | tf_op jit(solution)/shard_map/dot_general | solution.py:32
  86.4 0.0 all-to-all-done
  86.4 1.6 %gather_fusion = bf16[64,32,256]{2,1,0:T(8,128)(2,1)} fusion(bf16[64,32,256]{2,1,0:T(8,128)(2,1)S(1)} %all-to-all-done, s32[1024]{0:T(1024)S(1)} %pad_clamp_fusion.1), kind=kCustom, calls=%fused_computation | custom fusion | bytes 2097408 | tf_op jit(solution)/shard_map/jit(_take)/gather | solution.py:39
  88.0 1.5 bitcast_select_fusion.4
  89.5 1.9 %dynamic_update_slice.3 = bf16[2048,256]{1,0:T(8,128)(2,1)S(1)} dynamic-update-slice(bf16[2048,256]{1,0:T(8,128)(2,1)S(1)} %bitcast_select_fusion.4, bf16[512,256]{1,0:T(8,128)(2,1)S(1)} %convolution_convert_fusion.2, s32[]{:T(128)S(6)} %select_n.65, s32[]{:T(128)} %constant.15.clone.1) | dynamic-update-slice | bytes 524292 | tf_op jit(solution)/shard_map/dynamic_update_slice | solution.py:54
  91.4 1.2 broadcast_select_fusion
  92.6 0.0 copy-start.3
  92.6 10.7 %fusion.19 = (f32[4,512]{1,0:T(4,128)S(1)}, f32[4,512,2048]{1,2,0:T(8,128)}) fusion(pred[512,2048]{0,1:T(8,128)(4,1)} %iota_compare_fusion, bf16[512,4,128]{0,2,1:T(8,128)(2,1)} %bitcast.63, bf16[2048,256]{1,0:T(8,128)(2,1)} %broadcast_select_fusion), kind=kOutput, calls=%fused_computation.51 | convolution fusion | flops 1090521088 | bytes 18882560 | tf_op jit(solution)/shard_map/sub | solution.py:69
  103.3 0.0 copy-done.3
  103.4 7.0 %fusion.13 = bf16[128,4,512]{2,0,1:T(8,128)(2,1)S(1)} fusion(f32[4,512,2048]{1,2,0:T(8,128)} %get-tuple-element.3, f32[4,512]{1,0:T(4,128)S(1)} %get-tuple-element.2, bf16[2048,256]{1,0:T(8,128)(2,1)S(1)} %copy-done.3), kind=kOutput, calls=%fused_computation.22 | convolution fusion | flops 1082392576 | bytes 17833984 | tf_op jit(solution)/shard_map/htk,kd->thd/dot_general | solution.py:71
  110.4 0.0 copy-start.7
  110.4 0.0 copy-done
  110.4 0.0 copy-start.2
  110.4 2.6 %convolution_convert_fusion = bf16[512,2048]{1,0:T(8,128)(2,1)} fusion(bf16[512,512]{0,1:T(8,128)(2,1)S(1)} %bitcast.64, bf16[512,2048]{1,0:T(8,128)(2,1)S(1)} %copy-done), kind=kOutput, calls=%fused_computation.19 | convolution fusion | flops 1074790400 | bytes 4718592 | tf_op jit(solution)/shard_map/dot_general | solution.py:75
  113.1 0.0 reduce-scatter.2.cloned.1.call-update
  113.1 0.0 copy-done.7
  113.1 0.1 select_reduce_fusion
  113.2 1.0 constant_dynamic-slice_fusion
  114.2 0.6 gather_fusion.1
  114.8 0.8 broadcast_select_fusion.1
  115.7 10.6 %all-to-all-start.1 = ((bf16[64,8,256]{2,1,0:T(8,128)(2,1)}), bf16[64,8,256]{2,1,0:T(8,128)(2,1)S(1)}, u32[]{:S(2)}, u32[]{:S(2)}) async-start(bf16[64,8,256]{2,1,0:T(8,128)(2,1)} %broadcast_select_fusion.1), calls=%async_computation.2 | async-start | bytes 524288 | tf_op jit(solution)/shard_map/all_to_all | solution.py:84
  126.3 13.1 %all-to-all-done.1 = bf16[64,8,256]{2,1,0:T(8,128)(2,1)S(1)} async-done(((bf16[64,8,256]{2,1,0:T(8,128)(2,1)}), bf16[64,8,256]{2,1,0:T(8,128)(2,1)S(1)}, u32[]{:S(2)}, u32[]{:S(2)}) %all-to-all-start.1) | async-done | bytes 262176 | tf_op jit(solution)/shard_map/all_to_all | solution.py:84
  139.5 6.1 %reduce-scatter.2.cloned.1.call-done = bf16[512,512]{1,0:T(8,128)(2,1)} async-done(((bf16[512,2048]{1,0:T(8,128)(2,1)}), bf16[512,512]{1,0:T(8,128)(2,1)}) %reduce-scatter.2.cloned.1.call-update) | async-done | bytes 524304 | tf_op jit(solution)/shard_map/reduce_scatter | solution.py:76
  145.6 0.0 copy-done.2
  145.6 2.0 %select_convert_fusion = bf16[512,512]{1,0:T(8,128)(2,1)} fusion(bf16[512,512]{1,0:T(8,128)(2,1)} %reduce-scatter.2.cloned.1.call-done, bf16[512,512]{1,0:T(8,128)(2,1)S(1)} %copy-done.2, pred[512]{0:T(512)(128)(4,1)S(1)} %iota_compare_fusion.3), kind=kLoop, calls=%fused_computation.25 | loop fusion | flops 1310720 | bytes 1573376 | tf_op jit(solution)/shard_map/convert_element_type | solution.py:80
  147.6 0.7 copy.29
  (9 shorter events, 0.1 us)
Async XLA Ops:
  7.2 103.3 %copy-start = (bf16[512,2048]{1,0:T(8,128)(2,1)S(1)}, bf16[512,2048]{1,0:T(8,128)(2,1)}, u32[]{:S(2)}) copy-start(bf16[512,2048]{1,0:T(8,128)(2,1)} %param.14) | copy-start | bytes 6291460
  7.2 75.6 %copy-start.4 = (f32[2048]{0:T(1024)S(1)}, f32[2048]{0:T(1024)}, u32[]{:S(2)}) copy-start(f32[2048]{0:T(1024)} %param.11) | copy-start | bytes 24580
  7.2 34.0 %all-gather.3.cloned.1.call-start = ((), (), s32[]{:S(2)}) async-start(), calls=%async_computation.3 | async-start | bytes 1310720 | tf_op jit(solution)/shard_map/all_gather | solution.py:37
  7.9 70.4 %all-gather.5.cloned.1.call-start = ((), (), s32[]{:S(2)}) async-start(), calls=%async_computation.4 | async-start | bytes 2621440 | tf_op jit(solution)/shard_map/all_gather | solution.py:30
  41.2 45.2 %all-to-all-start = ((bf16[64,32,256]{2,1,0:T(8,128)(2,1)}), bf16[64,32,256]{2,1,0:T(8,128)(2,1)S(1)}, u32[]{:S(2)}, u32[]{:S(2)}) async-start(bf16[64,32,256]{2,1,0:T(8,128)(2,1)} %all-gather.3.cloned.1.call-done), calls=%async_computation | async-start | bytes 2097152 | tf_op jit(solution)/shard_map/all_to_all | solution.py:38
  52.8 92.8 %reduce-scatter.2.cloned.1.call-start = ((), (), s32[]{:S(2)}) async-start(), calls=%async_computation.5 | async-start | bytes 2621440 | tf_op jit(solution)/shard_map/reduce_scatter | solution.py:76
  78.3 4.4 %copy-start.1 = (bf16[512,2048]{1,0:T(8,128)(2,1)S(1)}, bf16[512,2048]{1,0:T(8,128)(2,1)}, u32[]{:S(2)}) copy-start(bf16[512,2048]{1,0:T(8,128)(2,1)} %all-gather.5.cloned.1.call-done) | copy-start | bytes 6291460
  78.3 5.1 %copy-start.6 = (bf16[2048,256]{1,0:T(8,128)(2,1)S(1)}, bf16[2048,256]{1,0:T(8,128)(2,1)}, u32[]{:S(2)}) copy-start(bf16[2048,256]{1,0:T(8,128)(2,1)} %param.13) | copy-start | bytes 3145732
  82.7 1.6 %copy-start.5 = (bf16[2048,512]{1,0:T(8,128)(2,1)S(1)}, bf16[2048,512]{1,0:T(8,128)(2,1)}, u32[]{:S(2)}) copy-start(bf16[2048,512]{1,0:T(8,128)(2,1)} %param.12) | copy-start | bytes 6291460
  92.6 10.7 %copy-start.3 = (bf16[2048,256]{1,0:T(8,128)(2,1)S(1)}, bf16[2048,256]{1,0:T(8,128)(2,1)}, u32[]{:S(2)}) copy-start(bf16[2048,256]{1,0:T(8,128)(2,1)} %broadcast_select_fusion) | copy-start | bytes 3145732
  110.4 2.7 %copy-start.7 = (s32[1,64]{1,0:T(1,128)S(1)}, s32[1,64]{1,0:T(1,128)}, u32[]{:S(2)}) copy-start(s32[1,64]{1,0:T(1,128)} %param.18) | copy-start | bytes 772
  110.4 35.1 %copy-start.2 = (bf16[512,512]{1,0:T(8,128)(2,1)S(1)}, bf16[512,512]{1,0:T(8,128)(2,1)}, u32[]{:S(2)}) copy-start(bf16[512,512]{1,0:T(8,128)(2,1)} %param.10) | copy-start | bytes 1572868
  115.7 23.8 %all-to-all-start.1 = ((bf16[64,8,256]{2,1,0:T(8,128)(2,1)}), bf16[64,8,256]{2,1,0:T(8,128)(2,1)S(1)}, u32[]{:S(2)}, u32[]{:S(2)}) async-start(bf16[64,8,256]{2,1,0:T(8,128)(2,1)} %broadcast_select_fusion.1), calls=%async_computation.2 | async-start | bytes 524288 | tf_op jit(solution)/shard_map/all_to_all | solution.py:84
Sparse Core Ops, SparseCore 0:
  9.8 31.3 all-gather.2
  43.0 35.2 all-gather.4
  113.2 32.3 reduce-scatter.1
where the time goes:
time: 155 us
  waiting for transfers between devices  74.1 us (48%)
  matrix products  23.2 us (15%)
  starting transfers between devices  22.3 us (14%)
  between operations  15.3 us (10%)
  other arithmetic  13.9 us (9%)
  local copies, waits for them, and re-layouts  6.07 us (4%)
    all_gather x1, waiting for transfers between devices, body(): pooled = lax.all_gather(old_cache, 'tp', axis=1, tiled=True)  27.9 us
    all_gather x1, waiting for transfers between devices, body(): full_rows = lax.all_gather(tokens, 'tp', axis=1, tiled=True)  25.5 us
    all_to_all x1, waiting for transfers between devices, body(): lax.all_to_all(jnp.take(mine_part, sources, axis=0), 'seq', split_axis=0,...  13.1 us
    all_to_all x1, starting transfers between devices, body(): lax.all_to_all(pooled, 'seq', split_axis=0, concat_axis=0, tiled=True)  11.5 us
    sub x1, matrix products, body(): weights = jnp.exp(scores - top)  10.7 us
    all_to_all x1, starting transfers between devices, body(): lax.all_to_all(jnp.take(mine_part, sources, axis=0), 'seq', split_axis=0,...  10.6 us
    dot_general x1, matrix products, body(): jnp.einsum('htk,kd->thd', probs, values, preferred_element_type=jnp.float32)  7.05 us
    reduce_scatter x1, waiting for transfers between devices, body(): lax.psum_scatter(partial_out.astype(jnp.bfloat16), 'tp', scatter_dimensio...  6.08 us
  transfers between devices with their start and end apart: 5, of which 4 were waited for; matrix products, arithmetic and copies ran while one was open for 9% of the time, Pallas kernels for 0%

commit v1 on v0

--- a/solution.py
+++ b/solution.py
@@ -27,32 +27,58 @@
     new_table,
     old_cache,
 ):
+    groups = lax.axis_size("seq")
+    tp_count = lax.axis_size("tp")
+    tp_index = lax.axis_index("tp")
+    holders = old_table[0]
+    held_len = cached_lens[0]
+    span_len = span_lens[0]
+    tok_rows = tokens.shape[0]
+    share = old_cache.shape[1]
+    width = old_cache.shape[2]
+    block_rows = share * tp_count
+    capacity = groups * block_rows
+
+    arrived = lax.all_to_all(old_cache, "seq", split_axis=0, concat_axis=0, tiled=True)
+    cache_share = jnp.take(arrived, holders, axis=0)
+
     full_rows = lax.all_gather(tokens, "tp", axis=1, tiled=True)
     normed = normalize(full_rows, norm_gain)
     query = jnp.dot(normed, w_query, preferred_element_type=jnp.float32).astype(jnp.bfloat16)
     keyval = jnp.dot(normed, w_keyval, preferred_element_type=jnp.float32).astype(jnp.bfloat16)
-    groups = lax.axis_size("seq")
-    tp_count = lax.axis_size("tp")
-    holders = old_table[0]
-    pooled = lax.all_gather(old_cache, "tp", axis=1, tiled=True)
-    arrived = lax.all_to_all(pooled, "seq", split_axis=0, concat_axis=0, tiled=True)
-    ordered = jnp.take(arrived, holders, axis=0)
-    block_rows = ordered.shape[1]
-    width = ordered.shape[2]
-    capacity = groups * block_rows
-    cached = ordered.reshape(capacity, width)
-    held_len = cached_lens[0]
-    span_len = span_lens[0]
-    tok_rows = tokens.shape[0]
-    share = block_rows // tp_count
+
+    shifted = lax.dynamic_update_slice(
+        jnp.zeros((capacity, width), jnp.bfloat16), keyval, (held_len, jnp.int32(0))
+    )
+    shifted_share = lax.dynamic_slice_in_dim(
+        shifted.reshape(groups, block_rows, width), tp_index * share, share, 1
+    )
+    share_pos = (
+        lax.broadcasted_iota(jnp.int32, (groups, share, 1), 0) * block_rows
+        + tp_index * share
+        + lax.broadcasted_iota(jnp.int32, (groups, share, 1), 1)
+    )
+    fresh_share = jnp.where(
+        share_pos < held_len,
+        cache_share,
+        jnp.where(share_pos < held_len + span_len, shifted_share, jnp.zeros_like(shifted_share)),
+    )
     targets = new_table[0]
     device_ids = lax.broadcasted_iota(jnp.int32, (groups, groups), 0)
     block_ids = lax.broadcasted_iota(jnp.int32, (groups, groups), 1)
     matches = targets[None, :] == device_ids
     sources = jnp.sum(jnp.where(matches, block_ids, 0), axis=1)
+    new_cache = lax.all_to_all(
+        jnp.take(fresh_share, sources, axis=0), "seq", split_axis=0, concat_axis=0, tiled=True
+    )
+
+    cached = lax.all_gather(cache_share, "tp", axis=1, tiled=True).reshape(capacity, width)
     positions = lax.broadcasted_iota(jnp.int32, (capacity, 1), 0)
-    placed = lax.dynamic_update_slice(cached, keyval, (held_len, jnp.int32(0)))
-    fresh = jnp.where(positions < held_len + span_len, placed, jnp.zeros_like(placed))
+    fresh = jnp.where(
+        positions < held_len,
+        cached,
+        jnp.where(positions < held_len + span_len, shifted, jnp.zeros_like(shifted)),
+    )
     head_size = width // 2
     keys = fresh[:, :head_size]
     values = fresh[:, head_size:]
@@ -78,12 +104,6 @@
     ).astype(jnp.float32)
     total = tokens.astype(jnp.float32) + summed
     mixed = jnp.where(row_pos < span_len, total, jnp.zeros_like(total)).astype(jnp.bfloat16)
-    mine_part = lax.dynamic_slice_in_dim(
-        fresh.reshape(groups, block_rows, width), lax.axis_index("tp") * share, share, 1
-    )
-    new_cache = lax.all_to_all(
-        jnp.take(mine_part, sources, axis=0), "seq", split_axis=0, concat_axis=0, tiled=True
-    )
     return (mixed, new_cache)
 
 

time: 155 us -> 154 us (level)
  waiting for transfers between devices: 74.1 us -> 65.4 us
  other arithmetic: 13.9 us -> 17 us
  starting transfers between devices: 22.3 us -> 24.8 us
  matrix products: 23.2 us -> 25.4 us
    all_gather x1, waiting for transfers between devices: 25.5 us -> 11.7 us  [body(): full_rows = lax.all_gather(tokens, 'tp', axis=1, tiled=True)]
    all_to_all x2, waiting for transfers between devices: 13.2 us -> 23.5 us  [the longest x1 13.1 us: body(): lax.all_to_all(jnp.take(fresh_share, sources, axis=0), 'seq', split_axis=...]
    all_gather x1, waiting for transfers between devices: 27.9 us -> 21.4 us  [body(): lax.all_gather(cache_share, 'tp', axis=1, tiled=True)]
    select_n x5, other arithmetic: 4.24 us -> 7.21 us  [the longest x1 3.78 us: body(): jnp.where(positions < held_len, cached, jnp.where(positions < held_len +...]
    all_to_all x2, starting transfers between devices: 22.2 us -> 24.5 us  [the longest x1 13 us: body(): lax.all_to_all(old_cache, 'seq', split_axis=0, concat_axis=0, tiled=True)]
    dot_general x1, matrix products: 2.1 us -> 4.31 us  [body(): jnp.dot(normed, w_query, preferred_element_type=jnp.float32)]
    reduce_scatter x1, waiting for transfers between devices: 6.08 us -> 8.03 us  [body(): lax.psum_scatter(partial_out.astype(jnp.bfloat16), 'tp', scatter_dimensio...]
  transfers between devices with their start and end apart: 5 -> 5, of which waited for: 4 -> 5; matrix products, arithmetic and copies ran while one was open for 9% -> 7% of each run, Pallas kernels for 0% -> 0%
where the time goes in v1:
time: 154 us; the launch traced here: 153 us
  waiting for transfers between devices  65.4 us (42%)
  matrix products  25.4 us (16%)
  starting transfers between devices  24.8 us (16%)
  other arithmetic  17 us (11%)
  between operations  15.3 us (10%)
  local copies, waits for them, and re-layouts  5.21 us (3%)
    all_gather x1, waiting for transfers between devices, body(): lax.all_gather(cache_share, 'tp', axis=1, tiled=True)  21.4 us
    all_to_all x1, waiting for transfers between devices, body(): lax.all_to_all(jnp.take(fresh_share, sources, axis=0), 'seq', split_axis=...  13.1 us
    all_to_all x1, starting transfers between devices, body(): lax.all_to_all(old_cache, 'seq', split_axis=0, concat_axis=0, tiled=True)  13 us
    all_gather x1, waiting for transfers between devices, body(): full_rows = lax.all_gather(tokens, 'tp', axis=1, tiled=True)  11.7 us
    all_to_all x1, starting transfers between devices, body(): lax.all_to_all(jnp.take(fresh_share, sources, axis=0), 'seq', split_axis=...  11.5 us
    sub x1, matrix products, body(): weights = jnp.exp(scores - top)  10.7 us
    all_to_all x1, waiting for transfers between devices, body(): lax.all_to_all(old_cache, 'seq', split_axis=0, concat_axis=0, tiled=True)  10.4 us
    reduce_scatter x1, waiting for transfers between devices, body(): lax.psum_scatter(partial_out.astype(jnp.bfloat16), 'tp', scatter_dimensio...  8.03 us
  transfers between devices with their start and end apart: 5, of which 5 were waited for; matrix products, arithmetic and copies ran while one was open for 7% of the time, Pallas kernels for 0%

profile of v1, /device:TPU:1, one launch (start us, length us, event | category | flops | bytes accessed | tf_op | source)
XLA Modules:
  0.0 153.1 jit_solution(9230389170875504754)
XLA Ops:
  7.2 0.0 copy-start
  7.2 0.0 copy-start.5
  7.2 0.0 all-gather.5.cloned.1.call-start
  7.2 0.7 all-gather.5.cloned.1.call-update
  7.9 13.0 %all-to-all-start = ((bf16[64,8,256]{2,1,0:T(8,128)(2,1)}), bf16[64,8,256]{2,1,0:T(8,128)(2,1)S(1)}, u32[]{:S(2)}, u32[]{:S(2)}) async-start(bf16[64,8,256]{2,1,0:T(8,128)(2,1)} %param.21), calls=%async_computation | async-start | bytes 524288 | tf_op jit(solution)/shard_map/all_to_all | solution.py:42
  20.9 0.0 all-gather.3.cloned.1.call-start
  22.3 0.7 compare_select_fusion.1
  23.0 0.7 compare_and_fusion.1
  23.6 0.1 fusion.16
  23.7 10.4 %all-to-all-done = bf16[64,8,256]{2,1,0:T(8,128)(2,1)S(1)} async-done(((bf16[64,8,256]{2,1,0:T(8,128)(2,1)}), bf16[64,8,256]{2,1,0:T(8,128)(2,1)S(1)}, u32[]{:S(2)}, u32[]{:S(2)}) %all-to-all-start) | async-done | bytes 262176 | tf_op jit(solution)/shard_map/all_to_all | solution.py:42
  34.1 1.3 gather_fusion
  35.4 11.7 %all-gather.5.cloned.1.call-done = bf16[512,2048]{1,0:T(8,128)(2,1)} async-done(((bf16[512,512]{1,0:T(8,128)(2,1)}), bf16[512,2048]{1,0:T(8,128)(2,1)}) %all-gather.5.cloned.1.call-update) | async-done | bytes 2097168 | tf_op jit(solution)/shard_map/all_gather | solution.py:45
  47.1 0.0 copy-start.1
  47.1 0.0 copy-start.6
  47.1 2.1 %convert_reduce_fusion = f32[512]{0:T(512)S(1)} fusion(bf16[512,2048]{1,0:T(8,128)(2,1)} %all-gather.5.cloned.1.call-done), kind=kLoop, calls=%fused_computation.12 | loop fusion | flops 2096640 | bytes 2099200 | tf_op jit(solution)/shard_map/reduce_sum | solution.py:12
  49.2 2.3 %fusion.8 = f32[512]{0:T(512)S(1)} fusion(bf16[512,2048]{1,0:T(8,128)(2,1)} %all-gather.5.cloned.1.call-done, f32[512]{0:T(512)S(1)} %broadcast_multiply_fusion), kind=kLoop, calls=%fused_computation.15 | loop fusion | flops 4193792 | bytes 2101248 | tf_op jit(solution)/shard_map/reduce_sum | solution.py:14
  51.5 0.0 copy-done.5
  51.5 0.0 copy-done.1
  51.5 0.7 fusion.10
  52.2 0.0 copy-done.6
  52.3 0.0 copy-start.2
  52.3 0.7 convolution_convert_fusion.2
  53.0 0.6 copy-done.2
  53.6 0.1 broadcast.104
  53.7 1.9 %dynamic_update_slice.3 = bf16[2048,256]{1,0:T(8,128)(2,1)S(1)} dynamic-update-slice(bf16[2048,256]{1,0:T(8,128)(2,1)S(1)} %broadcast.104, bf16[512,256]{1,0:T(8,128)(2,1)S(1)} %convolution_convert_fusion.2, s32[]{:T(128)S(6)} %select_n.39, s32[]{:T(128)} %constant.9.clone.1) | dynamic-update-slice | bytes 524292 | tf_op jit(solution)/shard_map/dynamic_update_slice | solution.py:50
  55.6 1.9 %select_select_fusion = (bf16[64,8,256]{2,1,0:T(8,128)(2,1)S(1)}, bf16[64,8,256]{2,1,0:T(8,128)(2,1)}) fusion(bf16[64,32,256]{2,1,0:T(8,128)(2,1)S(1)} %bitcast.57, s32[]{:T(128)S(6)} %select_n.44, pred[64,8]{1,0:T(8,128)(4,1)S(1)} %get-tuple-element.6, pred[64,8]{1,0:T(8,128)(4,1)S(1)} %get-tuple-element.5, bf16[64,8,256]{2,1,0:T(8,128)(2,1)} %gather_fusion, ...), kind=kLoop, calls=%fused_computation.29 | loop fusion | flops 393216 | bytes 1049668 | tf_op jit(solution)/shard_map/jit(_where)/select_n | solution.py:61
  57.5 0.0 all-gather.3.cloned.1.call-update
  57.5 0.2 reduce-scatter.2.cloned.1.call-start
  57.8 1.8 %iota_compare_fusion = pred[512,2048]{0,1:T(8,128)(4,1)} fusion(s32[512]{0:T(512)S(1)} %iota_add_fusion.1), kind=kLoop, calls=%fused_computation.18 | loop fusion | flops 1048576 | bytes 1050624 | tf_op jit(solution)/shard_map/le | solution.py:92
  59.6 4.3 %convolution_convert_fusion.1 = bf16[512,512]{0,1:T(8,128)(2,1)} fusion(bf16[512,2048]{1,0:T(8,128)(2,1)} %copy-done.2, bf16[2048,512]{1,0:T(8,128)(2,1)} %param.14), kind=kOutput, calls=%fused_computation.21 | convolution fusion | flops 1074003968 | bytes 4718592 | tf_op jit(solution)/shard_map/dot_general | solution.py:47
  63.9 21.4 %all-gather.3.cloned.1.call-done = bf16[64,32,256]{2,1,0:T(8,128)(2,1)} async-done(((bf16[64,8,256]{2,1,0:T(8,128)(2,1)}), bf16[64,32,256]{2,1,0:T(8,128)(2,1)}) %all-gather.3.cloned.1.call-update) | async-done | bytes 1048592 | tf_op jit(solution)/shard_map/all_gather | solution.py:75
  85.3 3.8 %bitcast_select_fusion.4 = bf16[2048,256]{1,0:T(8,128)(2,1)} fusion(bf16[64,32,256]{2,1,0:T(8,128)(2,1)} %all-gather.3.cloned.1.call-done, bf16[2048,256]{1,0:T(8,128)(2,1)S(1)} %dynamic_update_slice.3, pred[2048]{0:T(1024)(128)(4,1)S(1)} %get-tuple-element.9, pred[2048]{0:T(1024)(128)(4,1)S(1)} %get-tuple-element.10), kind=kLoop, calls=%fused_computation.24 | loop fusion | flops 1048576 | bytes 3149824 | tf_op jit(solution)/shard_map/jit(_where)/select_n | solution.py:77
  89.1 0.0 copy-start.4
  89.1 10.7 %fusion.19 = (f32[4,512]{1,0:T(4,128)S(1)}, f32[4,512,2048]{1,2,0:T(8,128)}) fusion(pred[512,2048]{0,1:T(8,128)(4,1)} %iota_compare_fusion, bf16[512,4,128]{0,2,1:T(8,128)(2,1)} %bitcast.59, bf16[2048,256]{1,0:T(8,128)(2,1)} %bitcast_select_fusion.4), kind=kOutput, calls=%fused_computation.52 | convolution fusion | flops 1090521088 | bytes 18882560 | tf_op jit(solution)/shard_map/sub | solution.py:95
  99.8 0.0 copy-done.4
  99.8 7.0 %fusion.13 = bf16[128,4,512]{2,0,1:T(8,128)(2,1)S(1)} fusion(f32[4,512,2048]{1,2,0:T(8,128)} %get-tuple-element.8, f32[4,512]{1,0:T(4,128)S(1)} %get-tuple-element.7, bf16[2048,256]{1,0:T(8,128)(2,1)S(1)} %copy-done.4), kind=kOutput, calls=%fused_computation.22 | convolution fusion | flops 1082392576 | bytes 17833984 | tf_op jit(solution)/shard_map/htk,kd->thd/dot_general | solution.py:97
  106.8 0.0 copy-start.7
  106.8 0.0 copy-done
  106.9 0.0 copy-start.3
  106.9 2.6 %convolution_convert_fusion = bf16[512,2048]{1,0:T(8,128)(2,1)} fusion(bf16[512,512]{0,1:T(8,128)(2,1)S(1)} %bitcast.60, bf16[512,2048]{1,0:T(8,128)(2,1)S(1)} %copy-done), kind=kOutput, calls=%fused_computation.19 | convolution fusion | flops 1074790400 | bytes 4718592 | tf_op jit(solution)/shard_map/dot_general | solution.py:101
  109.5 0.0 reduce-scatter.2.cloned.1.call-update
  109.5 0.0 copy-done.7
  109.5 0.1 select_reduce_fusion
  109.7 0.6 gather_fusion.1
  110.3 0.8 broadcast_select_fusion
  111.1 11.5 %all-to-all-start.1 = ((bf16[64,8,256]{2,1,0:T(8,128)(2,1)}), bf16[64,8,256]{2,1,0:T(8,128)(2,1)S(1)}, u32[]{:S(2)}, u32[]{:S(2)}) async-start(bf16[64,8,256]{2,1,0:T(8,128)(2,1)} %broadcast_select_fusion), calls=%async_computation.2 | async-start | bytes 524288 | tf_op jit(solution)/shard_map/all_to_all | solution.py:71
  122.7 13.1 %all-to-all-done.1 = bf16[64,8,256]{2,1,0:T(8,128)(2,1)S(1)} async-done(((bf16[64,8,256]{2,1,0:T(8,128)(2,1)}), bf16[64,8,256]{2,1,0:T(8,128)(2,1)S(1)}, u32[]{:S(2)}, u32[]{:S(2)}) %all-to-all-start.1) | async-done | bytes 262176 | tf_op jit(solution)/shard_map/all_to_all | solution.py:71
  135.8 8.0 %reduce-scatter.2.cloned.1.call-done = bf16[512,512]{1,0:T(8,128)(2,1)} async-done(((bf16[512,2048]{1,0:T(8,128)(2,1)}), bf16[512,512]{1,0:T(8,128)(2,1)}) %reduce-scatter.2.cloned.1.call-update) | async-done | bytes 524304 | tf_op jit(solution)/shard_map/reduce_scatter | solution.py:102
  143.8 0.0 copy-done.3
  143.8 2.0 %select_convert_fusion = bf16[512,512]{1,0:T(8,128)(2,1)} fusion(bf16[512,512]{1,0:T(8,128)(2,1)} %reduce-scatter.2.cloned.1.call-done, bf16[512,512]{1,0:T(8,128)(2,1)S(1)} %copy-done.3, pred[512]{0:T(512)(128)(4,1)S(1)} %iota_compare_fusion.4), kind=kLoop, calls=%fused_computation.25 | loop fusion | flops 1310720 | bytes 1573376 | tf_op jit(solution)/shard_map/convert_element_type | solution.py:106
  145.9 0.7 copy.29
  (10 shorter events, 0.1 us)
Async XLA Ops:
  7.2 99.7 %copy-start = (bf16[512,2048]{1,0:T(8,128)(2,1)S(1)}, bf16[512,2048]{1,0:T(8,128)(2,1)}, u32[]{:S(2)}) copy-start(bf16[512,2048]{1,0:T(8,128)(2,1)} %param.16) | copy-start | bytes 6291460
  7.2 44.3 %copy-start.5 = (f32[2048]{0:T(1024)S(1)}, f32[2048]{0:T(1024)}, u32[]{:S(2)}) copy-start(f32[2048]{0:T(1024)} %param.13) | copy-start | bytes 24580
  7.2 39.9 %all-gather.5.cloned.1.call-start = ((), (), s32[]{:S(2)}) async-start(), calls=%async_computation.4 | async-start | bytes 2621440 | tf_op jit(solution)/shard_map/all_gather | solution.py:45
  7.9 26.2 %all-to-all-start = ((bf16[64,8,256]{2,1,0:T(8,128)(2,1)}), bf16[64,8,256]{2,1,0:T(8,128)(2,1)S(1)}, u32[]{:S(2)}, u32[]{:S(2)}) async-start(bf16[64,8,256]{2,1,0:T(8,128)(2,1)} %param.21), calls=%async_computation | async-start | bytes 524288 | tf_op jit(solution)/shard_map/all_to_all | solution.py:42
  20.9 64.3 %all-gather.3.cloned.1.call-start = ((), (), s32[]{:S(2)}) async-start(), calls=%async_computation.3 | async-start | bytes 1310720 | tf_op jit(solution)/shard_map/all_gather | solution.py:75
  47.1 4.4 %copy-start.1 = (bf16[512,2048]{1,0:T(8,128)(2,1)S(1)}, bf16[512,2048]{1,0:T(8,128)(2,1)}, u32[]{:S(2)}) copy-start(bf16[512,2048]{1,0:T(8,128)(2,1)} %all-gather.5.cloned.1.call-done) | copy-start | bytes 6291460
  47.1 5.1 %copy-start.6 = (bf16[2048,256]{1,0:T(8,128)(2,1)S(1)}, bf16[2048,256]{1,0:T(8,128)(2,1)}, u32[]{:S(2)}) copy-start(bf16[2048,256]{1,0:T(8,128)(2,1)} %param.15) | copy-start | bytes 3145732
  52.3 1.3 copy-start.2
  57.5 86.3 %reduce-scatter.2.cloned.1.call-start = ((), (), s32[]{:S(2)}) async-start(), calls=%async_computation.5 | async-start | bytes 2621440 | tf_op jit(solution)/shard_map/reduce_scatter | solution.py:102
  89.1 10.7 %copy-start.4 = (bf16[2048,256]{1,0:T(8,128)(2,1)S(1)}, bf16[2048,256]{1,0:T(8,128)(2,1)}, u32[]{:S(2)}) copy-start(bf16[2048,256]{1,0:T(8,128)(2,1)} %bitcast_select_fusion.4) | copy-start | bytes 3145732
  106.8 2.7 %copy-start.7 = (s32[1,64]{1,0:T(1,128)S(1)}, s32[1,64]{1,0:T(1,128)}, u32[]{:S(2)}) copy-start(s32[1,64]{1,0:T(1,128)} %param.20) | copy-start | bytes 772
  106.9 37.0 %copy-start.3 = (bf16[512,512]{1,0:T(8,128)(2,1)S(1)}, bf16[512,512]{1,0:T(8,128)(2,1)}, u32[]{:S(2)}) copy-start(bf16[512,512]{1,0:T(8,128)(2,1)} %param.12) | copy-start | bytes 1572868
  111.1 24.7 %all-to-all-start.1 = ((bf16[64,8,256]{2,1,0:T(8,128)(2,1)}), bf16[64,8,256]{2,1,0:T(8,128)(2,1)S(1)}, u32[]{:S(2)}, u32[]{:S(2)}) async-start(bf16[64,8,256]{2,1,0:T(8,128)(2,1)} %broadcast_select_fusion), calls=%async_computation.2 | async-start | bytes 524288 | tf_op jit(solution)/shard_map/all_to_all | solution.py:71
Sparse Core Ops, SparseCore 0:
  9.8 37.2 all-gather.4
  57.6 27.5 all-gather.2
  109.6 34.1 reduce-scatter.1

commit v2 on v1

--- a/solution.py
+++ b/solution.py
@@ -1,6 +1,10 @@
+import functools
+
 import jax
 import jax.numpy as jnp
 from jax import lax
+from jax.experimental import pallas as pl
+from jax.experimental.pallas import tpu as pltpu
 from jax.sharding import PartitionSpec as P
 
 EPSILON = 1e-05
@@ -13,6 +17,83 @@
     centred = values - average
     spread = jnp.mean(centred * centred, axis=1, keepdims=True)
     return (centred * lax.rsqrt(spread + EPSILON) * norm_gain).astype(jnp.bfloat16)
+
+
+def _exchange_kernel(axis, other, n, per_peer, x_ref, y_ref, send_sem, recv_sem, local_sem):
+    me = lax.axis_index(axis)
+    fixed = lax.axis_index(other)
+
+    def dev(peer):
+        return {axis: peer, other: fixed}
+
+    barrier = pltpu.get_barrier_semaphore()
+
+    def greet(k, carry):
+        pl.semaphore_signal(
+            barrier, inc=1, device_id=dev(lax.rem(me + k, n)), device_id_type=pl.DeviceIdType.MESH
+        )
+        return carry
+
+    lax.fori_loop(1, n, greet, 0)
+    pl.semaphore_wait(barrier, n - 1)
+
+    def src_of(peer):
+        return x_ref.at[peer] if per_peer else x_ref
+
+    own = pltpu.make_async_copy(src_of(me), y_ref.at[me], local_sem)
+    own.start()
+
+    def outgoing(k):
+        peer = lax.rem(me + k, n)
+        return pltpu.make_async_remote_copy(
+            src_ref=src_of(peer),
+            dst_ref=y_ref.at[me],
+            send_sem=send_sem.at[k],
+            recv_sem=recv_sem.at[k],
+            device_id=dev(peer),
+            device_id_type=pl.DeviceIdType.MESH,
+        )
+
+    def incoming(k):
+        sender = lax.rem(me + n - k, n)
+        return pltpu.make_async_remote_copy(
+            src_ref=src_of(me),
+            dst_ref=y_ref.at[sender],
+            send_sem=send_sem.at[k],
+            recv_sem=recv_sem.at[k],
+            device_id=dev(sender),
+            device_id_type=pl.DeviceIdType.MESH,
+        )
+
+    def start(k, carry):
+        outgoing(k).start()
+        return carry
+
+    lax.fori_loop(1, n, start, 0)
+
+    def finish(k, carry):
+        outgoing(k).wait_send()
+        incoming(k).wait_recv()
+        return carry
+
+    lax.fori_loop(1, n, finish, 0)
+    own.wait()
+
+
+def exchange(x, axis, other, n, per_peer, cid):
+    out_shape = x.shape[1:] if per_peer else x.shape
+    return pl.pallas_call(
+        functools.partial(_exchange_kernel, axis, other, n, per_peer),
+        out_shape=jax.ShapeDtypeStruct((n,) + out_shape, x.dtype),
+        in_specs=[pl.BlockSpec(memory_space=pl.ANY)],
+        out_specs=pl.BlockSpec(memory_space=pl.ANY),
+        scratch_shapes=[
+            pltpu.SemaphoreType.DMA((n,)),
+            pltpu.SemaphoreType.DMA((n,)),
+            pltpu.SemaphoreType.DMA,
+        ],
+        compiler_params=pltpu.CompilerParams(collective_id=cid, has_side_effects=True),
+    )(x)
 
 
 def body(
@@ -33,16 +114,17 @@
     holders = old_table[0]
     held_len = cached_lens[0]
     span_len = span_lens[0]
-    tok_rows = tokens.shape[0]
+    tok_rows, tok_cols = tokens.shape
     share = old_cache.shape[1]
     width = old_cache.shape[2]
     block_rows = share * tp_count
     capacity = groups * block_rows
 
-    arrived = lax.all_to_all(old_cache, "seq", split_axis=0, concat_axis=0, tiled=True)
+    arrived = exchange(old_cache, "seq", "tp", groups, True, 0)
     cache_share = jnp.take(arrived, holders, axis=0)
 
-    full_rows = lax.all_gather(tokens, "tp", axis=1, tiled=True)
+    gathered = exchange(tokens, "tp", "seq", tp_count, False, 1)
+    full_rows = gathered.transpose(1, 0, 2).reshape(tok_rows, tp_count * tok_cols)
     normed = normalize(full_rows, norm_gain)
     query = jnp.dot(normed, w_query, preferred_element_type=jnp.float32).astype(jnp.bfloat16)
     keyval = jnp.dot(normed, w_keyval, preferred_element_type=jnp.float32).astype(jnp.bfloat16)
@@ -68,11 +150,10 @@
     block_ids = lax.broadcasted_iota(jnp.int32, (groups, groups), 1)
     matches = targets[None, :] == device_ids
     sources = jnp.sum(jnp.where(matches, block_ids, 0), axis=1)
-    new_cache = lax.all_to_all(
-        jnp.take(fresh_share, sources, axis=0), "seq", split_axis=0, concat_axis=0, tiled=True
-    )
-
-    cached = lax.all_gather(cache_share, "tp", axis=1, tiled=True).reshape(capacity, width)
+    new_cache = exchange(jnp.take(fresh_share, sources, axis=0), "seq", "tp", groups, True, 2)
+
+    pieces = exchange(cache_share, "tp", "seq", tp_count, False, 3)
+    cached = pieces.transpose(1, 0, 2, 3).reshape(capacity, width)
     positions = lax.broadcasted_iota(jnp.int32, (capacity, 1), 0)
     fresh = jnp.where(
         positions < held_len,
@@ -98,11 +179,12 @@
         jnp.bfloat16
     )
     context = context.reshape(tok_rows, local_heads * head_size)
-    partial_out = jnp.dot(context, w_out, preferred_element_type=jnp.float32)
-    summed = lax.psum_scatter(
-        partial_out.astype(jnp.bfloat16), "tp", scatter_dimension=1, tiled=True
-    ).astype(jnp.float32)
-    total = tokens.astype(jnp.float32) + summed
+    out_blocks = w_out.reshape(w_out.shape[0], tp_count, tok_cols)
+    partial_out = jnp.einsum(
+        "tk,kpn->ptn", context, out_blocks, preferred_element_type=jnp.float32
+    ).astype(jnp.bfloat16)
+    summed = exchange(partial_out, "tp", "seq", tp_count, True, 4).astype(jnp.float32)
+    total = tokens.astype(jnp.float32) + jnp.sum(summed, axis=0)
     mixed = jnp.where(row_pos < span_len, total, jnp.zeros_like(total)).astype(jnp.bfloat16)
     return (mixed, new_cache)
 

time: 154 us -> 168 us (1.091)
  Pallas kernels: 0 us -> 107 us
  waiting for transfers between devices: 65.4 us -> 0 us
  starting transfers between devices: 24.8 us -> 0 us
  between operations: 15.3 us -> 2.3 us
  local copies, waits for them, and re-layouts: 5.21 us -> 13.2 us
  other arithmetic: 17 us -> 21 us
    pallas_call x0 -> x5, Pallas kernels: none -> 107 us  [exchange(): pl.pallas_call(functools.partial(_exchange_kernel, axis, other, n, per_pe...]
    all_gather x2 -> x0, waiting for transfers between devices: 33.1 us -> none  [the longest x1 21.4 us: body(): lax.all_gather(cache_share, 'tp', axis=1, tiled=True)]
    all_to_all x2 -> x0, starting transfers between devices: 24.5 us -> none  [the longest x1 13 us: body(): lax.all_to_all(old_cache, 'seq', split_axis=0, concat_axis=0, tiled=True)]
    all_to_all x2 -> x0, waiting for transfers between devices: 23.5 us -> none  [the longest x1 13.1 us: body(): lax.all_to_all(jnp.take(fresh_share, sources, axis=0), 'seq', split_axis=...]
    reduce_scatter x1 -> x0, waiting for transfers between devices: 8.03 us -> none  [body(): lax.psum_scatter(partial_out.astype(jnp.bfloat16), 'tp', scatter_dimensio...]
    convert_element_type x0 -> x1, local copies, waits for them, and re-layouts: none -> 5.24 us  [normalize(): values = rows.astype(jnp.float32)]
    convert_element_type x0 -> x1, other arithmetic: none -> 2.52 us  [normalize(): values = rows.astype(jnp.float32)]
    dot_general x1, matrix products: 4.31 us -> 2.09 us  [body(): jnp.dot(normed, w_query, preferred_element_type=jnp.float32)]
  transfers between devices with their start and end apart: 5 -> 0, of which waited for: 5 -> 0; matrix products, arithmetic and copies ran while one was open for 7% -> 0% of each run, Pallas kernels for 0% -> 0%
where the time goes in v2:
time: 168 us; the launch traced here: 167 us
  Pallas kernels  107 us (64%)
  matrix products  24.1 us (14%)
  other arithmetic  21 us (12%)
  local copies, waits for them, and re-layouts  13.2 us (8%)
  between operations  2.3 us (1%)
    pallas_call x5, Pallas kernels, exchange(): pl.pallas_call(functools.partial(_exchange_kernel, axis, other, n, per_pe...  107 us
    sub x1, matrix products, body(): weights = jnp.exp(scores - top)  10.7 us
    dot_general x1, matrix products, body(): jnp.einsum('htk,kd->thd', probs, values, preferred_element_type=jnp.float32)  7.19 us
    convert_element_type x1, local copies, waits for them, and re-layouts, normalize(): values = rows.astype(jnp.float32)  5.24 us

profile of v2, /device:TPU:1, one launch (start us, length us, event | category | flops | bytes accessed | tf_op | source)
XLA Modules:
  0.0 167.5 jit_solution(16382235483932462134)
XLA Ops:
  0.6 0.0 copy-start
  2.1 0.8 select_reduce_fusion
  2.9 0.7 compare_and_fusion.1
  3.6 0.7 compare_select_fusion.1
  4.3 0.1 fusion.21
  4.4 20.9 %shard_map.113 = bf16[64,8,256]{2,1,0:T(8,128)(2,1)} custom-call(bf16[64,8,256]{2,1,0:T(8,128)(2,1)} %x_ref.2), custom_call_target="tpu_custom_call" | custom-call | tf_op jit(solution)/shard_map/pallas_call | solution.py:85
  25.2 1.5 gather_fusion
  26.8 1.8 %iota_compare_fusion = pred[512,2048]{0,1:T(8,128)(4,1)} fusion(s32[512]{0:T(512)S(1)} %iota_add_fusion.1), kind=kLoop, calls=%fused_computation.21 | loop fusion | flops 1048576 | bytes 1050624 | tf_op jit(solution)/shard_map/le | solution.py:173
  28.6 27.2 %shard_map.115 = bf16[4,512,512]{2,1,0:T(8,128)(2,1)} custom-call(bf16[512,512]{1,0:T(8,128)(2,1)} %x_ref.3), custom_call_target="tpu_custom_call" | custom-call | tf_op jit(solution)/shard_map/pallas_call | solution.py:85
  55.8 0.0 copy-start.1
  55.8 2.1 %convert_reduce_fusion = f32[512]{0:T(512)S(1)} fusion(bf16[4,512,512]{2,1,0:T(8,128)(2,1)} %shard_map.115), kind=kLoop, calls=%fused_computation.12 | loop fusion | flops 2096640 | bytes 2099200 | tf_op jit(solution)/shard_map/reduce_sum | solution.py:16
  57.9 2.3 %fusion.7 = f32[512]{0:T(512)S(1)} fusion(bf16[4,512,512]{2,1,0:T(8,128)(2,1)} %shard_map.115, f32[512]{0:T(512)S(1)} %broadcast_multiply_fusion), kind=kLoop, calls=%fused_computation.15 | loop fusion | flops 4193792 | bytes 2101248 | tf_op jit(solution)/shard_map/reduce_sum | solution.py:18
  60.2 0.0 copy-done.1
  60.2 2.5 %convert_bitcast_fusion = f32[512,4,512]{2,0,1:T(8,128)} fusion(bf16[4,512,512]{2,1,0:T(8,128)(2,1)S(1)} %copy-done.1), kind=kLoop, calls=%fused_computation.13 | loop fusion | flops 1048576 | bytes 6291456 | tf_op jit(solution)/shard_map/convert_element_type | solution.py:15
  62.7 0.0 copy-start.6
  62.7 5.2 %copy.25 = f32[512,4,512]{0,2,1:T(8,128)} copy(f32[512,4,512]{2,0,1:T(8,128)} %convert_bitcast_fusion) | data formatting | bytes 8388608 | tf_op jit(solution)/shard_map/convert_element_type | solution.py:15
  67.9 0.0 copy-done.6
  67.9 0.0 copy-start.3
  67.9 2.8 %fusion.10 = bf16[512,2048]{0,1:T(8,128)(2,1)S(1)} fusion(f32[512,4,512]{0,2,1:T(8,128)} %copy.25, f32[2048]{0:T(1024)S(1)} %copy-done.6, f32[512]{0:T(512)S(1)} %add_rsqrt_fusion, f32[512]{0:T(512)S(1)} %broadcast_multiply_fusion), kind=kLoop, calls=%fused_computation.19 | loop fusion | flops 4194304 | bytes 6303744 | tf_op jit(solution)/shard_map/convert_element_type | solution.py:19
  70.8 0.0 copy-done.3
  70.8 1.5 convolution_convert_fusion.1
  72.2 0.0 copy-done
  72.2 2.1 %convolution_convert_fusion = bf16[512,512]{0,1:T(8,128)(2,1)} fusion(bf16[512,2048]{0,1:T(8,128)(2,1)S(1)} %fusion.10, bf16[2048,512]{1,0:T(8,128)(2,1)S(1)} %copy-done), kind=kOutput, calls=%fused_computation.27 | convolution fusion | flops 1074003968 | bytes 4718592 | tf_op jit(solution)/shard_map/dot_general | solution.py:129
  74.3 0.1 broadcast.109
  74.4 2.7 %dynamic_update_slice.3 = bf16[2048,256]{1,0:T(8,128)(2,1)S(1)} dynamic-update-slice(bf16[2048,256]{1,0:T(8,128)(2,1)S(1)} %broadcast.109, bf16[512,256]{1,0:T(8,128)(2,1)} %convolution_convert_fusion.1, s32[]{:T(128)S(6)} %select_n.39, s32[]{:T(128)} %constant.9.clone.1) | dynamic-update-slice | bytes 524292 | tf_op jit(solution)/shard_map/dynamic_update_slice | solution.py:132
  77.1 1.1 select_select_fusion
  78.2 1.5 gather_fusion.1
  79.7 0.8 broadcast_select_fusion.x_ref
  80.5 17.0 %shard_map.117 = bf16[64,8,256]{2,1,0:T(8,128)(2,1)} custom-call(bf16[64,8,256]{2,1,0:T(8,128)(2,1)} %broadcast_select_fusion.x_ref), custom_call_target="tpu_custom_call" | custom-call | tf_op jit(solution)/shard_map/pallas_call | solution.py:85
  97.5 15.2 %shard_map.114 = bf16[4,64,8,256]{3,2,1,0:T(8,128)(2,1)} custom-call(bf16[64,8,256]{2,1,0:T(8,128)(2,1)} %get-tuple-element.4.x_ref), custom_call_target="tpu_custom_call" | custom-call | tf_op jit(solution)/shard_map/pallas_call | solution.py:85
  112.7 1.4 copy.24
  114.1 2.4 %bitcast_select_fusion.4 = bf16[2048,256]{1,0:T(8,128)(2,1)} fusion(bf16[64,4,8,256]{3,2,1,0:T(8,128)(2,1)S(1)} %copy.24, bf16[2048,256]{1,0:T(8,128)(2,1)S(1)} %dynamic_update_slice.3, pred[2048]{0:T(1024)(128)(4,1)S(1)} %get-tuple-element.9, pred[2048]{0:T(1024)(128)(4,1)S(1)} %get-tuple-element.10), kind=kLoop, calls=%fused_computation.30 | loop fusion | flops 1048576 | bytes 3149824 | tf_op jit(solution)/shard_map/jit(_where)/select_n | solution.py:158
  116.5 0.0 copy-start.4
  116.5 10.7 %fusion.24 = (f32[4,512]{1,0:T(4,128)S(1)}, f32[4,512,2048]{1,2,0:T(8,128)}) fusion(pred[512,2048]{0,1:T(8,128)(4,1)} %iota_compare_fusion, bf16[512,4,128]{0,2,1:T(8,128)(2,1)} %bitcast.81, bf16[2048,256]{1,0:T(8,128)(2,1)} %bitcast_select_fusion.4), kind=kOutput, calls=%fused_computation.58 | convolution fusion | flops 1090521088 | bytes 18882560 | tf_op jit(solution)/shard_map/sub | solution.py:176
  127.2 0.0 copy-done.4
  127.2 0.0 copy-start.7
  127.2 7.2 %fusion.18 = bf16[128,4,512]{2,0,1:T(8,128)(2,1)S(1)} fusion(f32[4,512,2048]{1,2,0:T(8,128)} %get-tuple-element.8, f32[4,512]{1,0:T(4,128)S(1)} %get-tuple-element.7, bf16[2048,256]{1,0:T(8,128)(2,1)S(1)} %copy-done.4), kind=kOutput, calls=%fused_computation.28 | convolution fusion | flops 1082392576 | bytes 17833984 | tf_op jit(solution)/shard_map/htk,kd->thd/dot_general | solution.py:178
  134.4 0.0 copy-done.7
  134.4 2.6 %convert_bitcast_fusion.1.x_ref = bf16[4,512,512]{2,1,0:T(8,128)(2,1)} fusion(bf16[512,512,1]{0,1,2:T(8,128)(2,1)S(1)} %bitcast.82, bf16[64,4,8,512]{3,2,1,0:T(8,128)(2,1)S(1)} %bitcast.79), kind=kOutput, calls=%fused_computation.25 | convolution fusion | flops 1074790400 | bytes 4718592 | tf_op jit(solution)/shard_map/tk,kpn->ptn/dot_general | solution.py:183
  137.1 0.0 copy-start.2
  137.1 0.0 copy-start.5
  137.1 26.7 %shard_map.116 = bf16[4,512,512]{2,1,0:T(8,128)(2,1)} custom-call(bf16[4,512,512]{2,1,0:T(8,128)(2,1)} %convert_bitcast_fusion.1.x_ref), custom_call_target="tpu_custom_call" | custom-call | tf_op jit(solution)/shard_map/pallas_call | solution.py:85
  163.8 2.0 %convert_reduce_fusion.1 = f32[512,512]{1,0:T(8,128)S(1)} fusion(bf16[4,512,512]{2,1,0:T(8,128)(2,1)} %shard_map.116), kind=kLoop, calls=%fused_computation.20 | loop fusion | flops 1835008 | bytes 3145728 | tf_op jit(solution)/shard_map/reduce_sum | solution.py:187
  165.8 0.0 copy-done.2
  165.8 1.0 select_convert_fusion
  166.8 0.0 copy-done.5
  166.8 0.7 copy.48
  (10 shorter events, 0.1 us)
Async XLA Ops:
  0.6 71.6 %copy-start = (bf16[2048,512]{1,0:T(8,128)(2,1)S(1)}, bf16[2048,512]{1,0:T(8,128)(2,1)}, u32[]{:S(2)}) copy-start(bf16[2048,512]{1,0:T(8,128)(2,1)} %param.14) | copy-start | bytes 6291460
  55.8 4.4 %copy-start.1 = (bf16[4,512,512]{2,1,0:T(8,128)(2,1)S(1)}, bf16[4,512,512]{2,1,0:T(8,128)(2,1)}, u32[]{:S(2)}) copy-start(bf16[4,512,512]{2,1,0:T(8,128)(2,1)} %shard_map.115) | copy-start | bytes 6291460
  62.7 5.2 %copy-start.6 = (f32[2048]{0:T(1024)S(1)}, f32[2048]{0:T(1024)}, u32[]{:S(2)}) copy-start(f32[2048]{0:T(1024)} %param.13) | copy-start | bytes 24580
  67.9 2.8 %copy-start.3 = (bf16[2048,256]{1,0:T(8,128)(2,1)S(1)}, bf16[2048,256]{1,0:T(8,128)(2,1)}, u32[]{:S(2)}) copy-start(bf16[2048,256]{1,0:T(8,128)(2,1)} %param.15) | copy-start | bytes 3145732
  116.5 10.7 %copy-start.4 = (bf16[2048,256]{1,0:T(8,128)(2,1)S(1)}, bf16[2048,256]{1,0:T(8,128)(2,1)}, u32[]{:S(2)}) copy-start(bf16[2048,256]{1,0:T(8,128)(2,1)} %bitcast_select_fusion.4) | copy-start | bytes 3145732
  127.2 7.2 %copy-start.7 = (bf16[512,2048]{1,0:T(8,128)(2,1)S(1)}, bf16[512,2048]{1,0:T(8,128)(2,1)}, u32[]{:S(2)}) copy-start(bf16[512,2048]{1,0:T(8,128)(2,1)} %param.16) | copy-start | bytes 6291460
  137.1 28.7 %copy-start.2 = (bf16[512,512]{1,0:T(8,128)(2,1)S(1)}, bf16[512,512]{1,0:T(8,128)(2,1)}, u32[]{:S(2)}) copy-start(bf16[512,512]{1,0:T(8,128)(2,1)} %x_ref.3) | copy-start | bytes 1572868
  137.1 29.7 %copy-start.5 = (bf16[64,8,256]{2,1,0:T(8,128)(2,1)S(1)}, bf16[64,8,256]{2,1,0:T(8,128)(2,1)}, u32[]{:S(2)}) copy-start(bf16[64,8,256]{2,1,0:T(8,128)(2,1)} %shard_map.117) | copy-start | bytes 786436

commit v3 on v1

v3 whole, which is shorter than its diff:
```python
import functools

import jax
import jax.numpy as jnp
from jax import lax
from jax.experimental import pallas as pl
from jax.experimental.pallas import tpu as pltpu
from jax.sharding import PartitionSpec as P

EPSILON = 1e-05
MASKED = -1e30


def normalize(rows, norm_gain):
    values = rows.astype(jnp.float32)
    average = jnp.mean(values, axis=1, keepdims=True)
    centred = values - average
    spread = jnp.mean(centred * centred, axis=1, keepdims=True)
    return (centred * lax.rsqrt(spread + EPSILON) * norm_gain).astype(jnp.bfloat16)


MESH = pl.DeviceIdType.MESH


def _remote(src, dst, send, recv, dev):
    return pltpu.make_async_remote_copy(
        src_ref=src, dst_ref=dst, send_sem=send, recv_sem=recv, device_id=dev, device_id_type=MESH
    )


def _greet(nseq, s, t, left, right):
    barrier = pltpu.get_barrier_semaphore()

    def one(k, carry):
        pl.semaphore_signal(
            barrier, inc=1, device_id={"seq": lax.rem(s + k, nseq), "tp": t}, device_id_type=MESH
        )
        return carry

    lax.fori_loop(1, nseq, one, 0)
    for p in (left, right):
        pl.semaphore_signal(barrier, inc=1, device_id={"seq": s, "tp": p}, device_id_type=MESH)
    pl.semaphore_wait(barrier, nseq + 1)


def _seq_copies(nseq, s, t, src_ref, dst_ref, send, recv):
    def outgoing(k):
        peer = lax.rem(s + k, nseq)
        return _remote(src_ref.at[peer], dst_ref.at[s], send.at[k], recv.at[k],
                       {"seq": peer, "tp": t})

    def incoming(k):
        sender = lax.rem(s + nseq - k, nseq)
        return _remote(src_ref.at[s], dst_ref.at[sender], send.at[k], recv.at[k],
                       {"seq": sender, "tp": t})

    return outgoing, incoming


def _loop(n, fn):
    def step(k, carry):
        fn(k)
        return carry

    lax.fori_loop(1, n, step, 0)


def _in_kernel(nseq, ntp, tok_ref, cache_ref, tok_out, cache_out, tsend, trecv, csend, crecv,
               ssend, srecv, lsem):
    s = lax.axis_index("seq")
    t = lax.axis_index("tp")
    right = lax.rem(t + 1, ntp)
    left = lax.rem(t + ntp - 1, ntp)
    across = lax.rem(t + 2, ntp)
    rdev = {"seq": s, "tp": right}
    ldev = {"seq": s, "tp": left}
    rows, cols = tok_ref.shape
    half = rows // 2
    blocks = nseq // 2
    _greet(nseq, s, t, left, right)

    own_tok = pltpu.make_async_copy(tok_ref, tok_out.at[:, pl.ds(t * cols, cols)], lsem.at[0])
    own_tok.start()
    tok_r = _remote(tok_ref, tok_out.at[:, pl.ds(t * cols, cols)], tsend.at[0], trecv.at[0], rdev)
    tok_l = _remote(tok_ref, tok_out.at[:, pl.ds(t * cols, cols)], tsend.at[1], trecv.at[1], ldev)
    tok_r.start()
    tok_l.start()

    own_cache = pltpu.make_async_copy(cache_ref.at[s], cache_out.at[s, t], lsem.at[1])
    own_cache.start()
    seq_out, seq_in = _seq_copies(nseq, s, t, cache_ref, cache_out.at[:, t], ssend, srecv)
    _loop(nseq, lambda k: seq_out(k).start())

    _remote(tok_ref, tok_out.at[:, pl.ds(left * cols, cols)], tsend.at[0], trecv.at[0], ldev).wait_recv()
    fwd_r = _remote(tok_out.at[pl.ds(0, half), pl.ds(left * cols, cols)], tok_out.at[pl.ds(0, half), pl.ds(left * cols, cols)],
                    tsend.at[2], trecv.at[2], rdev)
    fwd_r.start()
    _remote(tok_ref, tok_out.at[:, pl.ds(right * cols, cols)], tsend.at[1], trecv.at[1], rdev).wait_recv()
    fwd_l = _remote(tok_out.at[pl.ds(half, half), pl.ds(right * cols, cols)], tok_out.at[pl.ds(half, half), pl.ds(right * cols, cols)],
                    tsend.at[3], trecv.at[3], ldev)
    fwd_l.start()

    _loop(nseq, lambda k: seq_in(k).wait_recv())
    own_cache.wait()
    mine = cache_out.at[:, t]
    cache_r = _remote(mine, mine, csend.at[0], crecv.at[0], rdev)
    cache_l = _remote(mine, mine, csend.at[1], crecv.at[1], ldev)
    cache_r.start()
    cache_l.start()
    _remote(mine, cache_out.at[:, left], csend.at[0], crecv.at[0], ldev).wait_recv()
    cfwd_r = _remote(cache_out.at[pl.ds(0, blocks), left], cache_out.at[pl.ds(0, blocks), left],
                     csend.at[2], crecv.at[2], rdev)
    cfwd_r.start()
    _remote(mine, cache_out.at[:, right], csend.at[1], crecv.at[1], rdev).wait_recv()
    cfwd_l = _remote(cache_out.at[pl.ds(blocks, blocks), right],
                     cache_out.at[pl.ds(blocks, blocks), right], csend.at[3], crecv.at[3], ldev)
    cfwd_l.start()

    _remote(tok_ref.at[pl.ds(0, half)], tok_out.at[pl.ds(0, half), pl.ds(across * cols, cols)], tsend.at[2], trecv.at[2], ldev).wait_recv()
    _remote(tok_ref.at[pl.ds(half, half)], tok_out.at[pl.ds(half, half), pl.ds(across * cols, cols)], tsend.at[3], trecv.at[3], rdev).wait_recv()
    _remote(cache_out.at[pl.ds(0, blocks), t], cache_out.at[pl.ds(0, blocks), across], csend.at[2], crecv.at[2], ldev).wait_recv()
    _remote(cache_out.at[pl.ds(blocks, blocks), t], cache_out.at[pl.ds(blocks, blocks), across], csend.at[3], crecv.at[3],
            rdev).wait_recv()
    for c in (tok_r, tok_l, fwd_r, fwd_l, cache_r, cache_l, cfwd_r, cfwd_l):
        c.wait_send()
    _loop(nseq, lambda k: seq_out(k).wait_send())
    own_tok.wait()


def gather_inputs(tokens, old_cache, nseq, ntp):
    rows, cols = tokens.shape
    _, share, width = old_cache.shape
    return pl.pallas_call(
        functools.partial(_in_kernel, nseq, ntp),
        out_shape=(
            jax.ShapeDtypeStruct((rows, ntp * cols), tokens.dtype),
            jax.ShapeDtypeStruct((nseq, ntp, share, width), old_cache.dtype),
        ),
        in_specs=[pl.BlockSpec(memory_space=pl.ANY)] * 2,
        out_specs=(pl.BlockSpec(memory_space=pl.ANY), pl.BlockSpec(memory_space=pl.ANY)),
        scratch_shapes=[
            pltpu.SemaphoreType.DMA((4,)),
            pltpu.SemaphoreType.DMA((4,)),
            pltpu.SemaphoreType.DMA((4,)),
            pltpu.SemaphoreType.DMA((4,)),
            pltpu.SemaphoreType.DMA((nseq,)),
            pltpu.SemaphoreType.DMA((nseq,)),
            pltpu.SemaphoreType.DMA((2,)),
        ],
        compiler_params=pltpu.CompilerParams(collective_id=0, has_side_effects=True),
    )(tokens, old_cache)


def _out_kernel(nseq, ntp, part_ref, share_ref, rs_out, new_out, stage, rsend, rrecv, ssend,
                srecv, lsem):
    s = lax.axis_index("seq")
    t = lax.axis_index("tp")
    right = lax.rem(t + 1, ntp)
    left = lax.rem(t + ntp - 1, ntp)
    across = lax.rem(t + 2, ntp)
    rdev = {"seq": s, "tp": right}
    ldev = {"seq": s, "tp": left}
    half = part_ref.shape[1] // 2
    _greet(nseq, s, t, left, right)

    own_part = pltpu.make_async_copy(part_ref.at[t], rs_out.at[t], lsem.at[0])
    own_part.start()
    own_new = pltpu.make_async_copy(share_ref.at[s], new_out.at[s], lsem.at[1])
    own_new.start()
    to_r = _remote(part_ref.at[right], rs_out.at[t], rsend.at[0], rrecv.at[0], rdev)
    to_l = _remote(part_ref.at[left], rs_out.at[t], rsend.at[1], rrecv.at[1], ldev)
    via_r = _remote(part_ref.at[across, pl.ds(0, half)], stage.at[0], rsend.at[2], rrecv.at[2], rdev)
    via_l = _remote(part_ref.at[across, pl.ds(half, half)], stage.at[1], rsend.at[3], rrecv.at[3],
                    ldev)
    for c in (to_r, to_l, via_r, via_l):
        c.start()
    seq_out, seq_in = _seq_copies(nseq, s, t, share_ref, new_out, ssend, srecv)
    _loop(nseq, lambda k: seq_out(k).start())

    _remote(part_ref.at[across, pl.ds(0, half)], stage.at[0], rsend.at[2], rrecv.at[2],
            ldev).wait_recv()
    fwd_r = _remote(stage.at[0], rs_out.at[left, pl.ds(0, half)], rsend.at[4], rrecv.at[4], rdev)
    fwd_r.start()
    _remote(part_ref.at[across, pl.ds(half, half)], stage.at[1], rsend.at[3], rrecv.at[3],
            rdev).wait_recv()
    fwd_l = _remote(stage.at[1], rs_out.at[right, pl.ds(half, half)], rsend.at[5], rrecv.at[5],
                    ldev)
    fwd_l.start()

    _remote(part_ref.at[t], rs_out.at[left], rsend.at[0], rrecv.at[0], ldev).wait_recv()
    _remote(part_ref.at[t], rs_out.at[right], rsend.at[1], rrecv.at[1], rdev).wait_recv()
    _remote(stage.at[0], rs_out.at[across, pl.ds(0, half)], rsend.at[4], rrecv.at[4],
            ldev).wait_recv()
    _remote(stage.at[1], rs_out.at[across, pl.ds(half, half)], rsend.at[5], rrecv.at[5],
            rdev).wait_recv()
    _loop(nseq, lambda k: seq_in(k).wait_recv())
    for c in (to_r, to_l, via_r, via_l, fwd_r, fwd_l):
        c.wait_send()
    _loop(nseq, lambda k: seq_out(k).wait_send())
    own_part.wait()
    own_new.wait()


def scatter_outputs(partial, share, nseq, ntp):
    _, rows, cols = partial.shape
    return pl.pallas_call(
        functools.partial(_out_kernel, nseq, ntp),
        out_shape=(
            jax.ShapeDtypeStruct(partial.shape, partial.dtype),
            jax.ShapeDtypeStruct(share.shape, share.dtype),
        ),
        in_specs=[pl.BlockSpec(memory_space=pl.ANY)] * 2,
        out_specs=(pl.BlockSpec(memory_space=pl.ANY), pl.BlockSpec(memory_space=pl.ANY)),
        scratch_shapes=[
            pltpu.VMEM((2, rows // 2, cols), partial.dtype),
            pltpu.SemaphoreType.DMA((6,)),
            pltpu.SemaphoreType.DMA((6,)),
            pltpu.SemaphoreType.DMA((nseq,)),
            pltpu.SemaphoreType.DMA((nseq,)),
            pltpu.SemaphoreType.DMA((2,)),
        ],
        compiler_params=pltpu.CompilerParams(collective_id=1, has_side_effects=True),
    )(partial, share)


def body(
    tokens,
    norm_gain,
    w_query,
    w_keyval,
    w_out,
    span_lens,
    cached_lens,
    old_table,
    new_table,
    old_cache,
):
    groups = lax.axis_size("seq")
    tp_count = lax.axis_size("tp")
    tp_index = lax.axis_index("tp")
    holders = old_table[0]
    held_len = cached_lens[0]
    span_len = span_lens[0]
    tok_rows, tok_cols = tokens.shape
    share = old_cache.shape[1]
    width = old_cache.shape[2]
    block_rows = share * tp_count
    capacity = groups * block_rows

    tok_all, cache_all = gather_inputs(tokens, old_cache, groups, tp_count)
    full_rows = tok_all
    normed = normalize(full_rows, norm_gain)
    query = jnp.dot(normed, w_query, preferred_element_type=jnp.float32).astype(jnp.bfloat16)
    keyval = jnp.dot(normed, w_keyval, preferred_element_type=jnp.float32).astype(jnp.bfloat16)

    cached = jnp.take(cache_all, holders, axis=0).reshape(capacity, width)
    shifted = lax.dynamic_update_slice(
        jnp.zeros((capacity, width), jnp.bfloat16), keyval, (held_len, jnp.int32(0))
    )
    positions = lax.broadcasted_iota(jnp.int32, (capacity, 1), 0)
    fresh = jnp.where(
        positions < held_len,
        cached,
        jnp.where(positions < held_len + span_len, shifted, jnp.zeros_like(shifted)),
    )
    fresh_share = lax.dynamic_slice_in_dim(
        fresh.reshape(groups, block_rows, width), tp_index * share, share, 1
    )
    targets = new_table[0]
    device_ids = lax.broadcasted_iota(jnp.int32, (groups, groups), 0)
    block_ids = lax.broadcasted_iota(jnp.int32, (groups, groups), 1)
    matches = targets[None, :] == device_ids
    sources = jnp.sum(jnp.where(matches, block_ids, 0), axis=1)
    sorted_share = jnp.take(fresh_share, sources, axis=0)
    head_size = width // 2
    keys = fresh[:, :head_size]
    values = fresh[:, head_size:]
    local_heads = query.shape[1] // head_size
    query3 = query.reshape(tok_rows, local_heads, head_size)
    scores = jnp.einsum(
        "thd,kd->htk", query3, keys, preferred_element_type=jnp.float32
    ) * head_size ** (-0.5)
    row_pos = lax.broadcasted_iota(jnp.int32, (tok_rows, 1), 0)
    key_pos = lax.broadcasted_iota(jnp.int32, (1, capacity), 1)
    allowed = key_pos <= held_len + row_pos
    scores = jnp.where(allowed[None], scores, MASKED)
    top = jnp.max(scores, axis=2, keepdims=True)
    weights = jnp.exp(scores - top)
    probs = (weights / jnp.sum(weights, axis=2, keepdims=True)).astype(jnp.bfloat16)
    context = jnp.einsum("htk,kd->thd", probs, values, preferred_element_type=jnp.float32).astype(
        jnp.bfloat16
    )
    context = context.reshape(tok_rows, local_heads * head_size)
    out_blocks = w_out.reshape(w_out.shape[0], tp_count, tok_cols)
    partial_out = jnp.einsum(
        "tk,kpn->ptn", context, out_blocks, preferred_element_type=jnp.float32
    ).astype(jnp.bfloat16)
    summed, new_cache = scatter_outputs(partial_out, sorted_share, groups, tp_count)
    summed = summed.astype(jnp.float32)
    total = tokens.astype(jnp.float32) + jnp.sum(summed, axis=0)
    mixed = jnp.where(row_pos < span_len, total, jnp.zeros_like(total)).astype(jnp.bfloat16)
    return (mixed, new_cache)


def solution(mesh):
    in_specs = (
        P("seq", "tp"),
        P(),
        P(None, "tp"),
        P(),
        P("tp", None),
        P("seq"),
        P("seq"),
        P("seq", None),
        P("seq", None),
        P("seq", "tp", None),
    )
    out_specs = (P("seq", "tp"), P("seq", "tp", None))
    return jax.shard_map(body, mesh=mesh, in_specs=in_specs, out_specs=out_specs, check_vma=False)
```

time: 154 us -> 128 us (0.83)
  Pallas kernels: 0 us -> 77.4 us
  waiting for transfers between devices: 65.4 us -> 0 us
  starting transfers between devices: 24.8 us -> 0 us
  between operations: 15.3 us -> 2.36 us
  local copies, waits for them, and re-layouts: 5.21 us -> 7.97 us
  other arithmetic: 17 us -> 14.7 us
    pallas_call x0 -> x2, Pallas kernels: none -> 77.4 us  [the longest x1 44.3 us: gather_inputs(): pl.pallas_call(functools.partial(_in_kernel, nseq, ntp), out_shape=(jax.S...]
    all_gather x2 -> x0, waiting for transfers between devices: 33.1 us -> none  [the longest x1 21.4 us: body(): lax.all_gather(cache_share, 'tp', axis=1, tiled=True)]
    all_to_all x2 -> x0, starting transfers between devices: 24.5 us -> none  [the longest x1 13 us: body(): lax.all_to_all(old_cache, 'seq', split_axis=0, concat_axis=0, tiled=True)]
    all_to_all x2 -> x0, waiting for transfers between devices: 23.5 us -> none  [the longest x1 13.1 us: body(): lax.all_to_all(jnp.take(fresh_share, sources, axis=0), 'seq', split_axis=...]
    reduce_scatter x1 -> x0, waiting for transfers between devices: 8.03 us -> none  [body(): lax.psum_scatter(partial_out.astype(jnp.bfloat16), 'tp', scatter_dimensio...]
    select_n x4, other arithmetic: 3.43 us -> 0.88 us  [the longest x2 0.85 us: body(): sorted_share = jnp.take(fresh_share, sources, axis=0)]
    reduce_sum x0 -> x1, other arithmetic: none -> 2.01 us  [body(): total = tokens.astype(jnp.float32) + jnp.sum(summed, axis=0)]
    select_n x0 -> x1, local copies, waits for them, and re-layouts: none -> 1.89 us  [body(): jnp.where(positions < held_len + span_len, shifted, jnp.zeros_like(shifted))]
  transfers between devices with their start and end apart: 5 -> 0, of which waited for: 5 -> 0; matrix products, arithmetic and copies ran while one was open for 7% -> 0% of each run, Pallas kernels for 0% -> 0%
where the time goes in v3:
time: 128 us; the launch traced here: 127 us
  Pallas kernels  77.4 us (60%)
  matrix products  24.8 us (19%)
  other arithmetic  14.7 us (11%)
  local copies, waits for them, and re-layouts  7.97 us (6%)
  between operations  2.36 us (2%)
    pallas_call x1, Pallas kernels, gather_inputs(): pl.pallas_call(functools.partial(_in_kernel, nseq, ntp), out_shape=(jax.S...  44.3 us
    pallas_call x1, Pallas kernels, scatter_outputs(): pl.pallas_call(functools.partial(_out_kernel, nseq, ntp), out_shape=(jax....  33.1 us
    sub x1, matrix products, body(): weights = jnp.exp(scores - top)  10.5 us
    dot_general x1, matrix products, body(): jnp.einsum('htk,kd->thd', probs, values, preferred_element_type=jnp.float32)  7.19 us
    select_n x1, other arithmetic, body(): jnp.where(positions < held_len, cached, jnp.where(positions < held_len +...  3.81 us
    dot_general x1, matrix products, body(): jnp.dot(normed, w_query, preferred_element_type=jnp.float32)  3.76 us
    dot_general x1, matrix products, body(): jnp.einsum('tk,kpn->ptn', context, out_blocks, preferred_element_type=jnp...  2.63 us

profile of v3, /device:TPU:1, one launch (start us, length us, event | category | flops | bytes accessed | tf_op | source)
XLA Modules:
  0.0 127.2 jit_solution(16458049227622640395)
XLA Ops:
  0.6 0.0 copy-start
  0.6 0.0 copy-start.7
  2.1 44.3 %shard_map.113 = (bf16[512,2048]{1,0:T(8,128)(2,1)}, bf16[64,4,8,256]{3,2,1,0:T(8,128)(2,1)}) custom-call(bf16[512,512]{1,0:T(8,128)(2,1)} %tok_ref.1, bf16[64,8,256]{2,1,0:T(8,128)(2,1)} %cache_ref.1), custom_call_target="tpu_custom_call" | custom-call | tf_op jit(solution)/shard_map/pallas_call | solution.py:133
  46.5 0.0 copy-start.1
  46.5 0.0 copy-start.9
  46.5 2.1 %convert_reduce_fusion = f32[512]{0:T(512)S(1)} fusion(bf16[512,2048]{1,0:T(8,128)(2,1)} %get-tuple-element.7), kind=kLoop, calls=%fused_computation.12 | loop fusion | flops 2096640 | bytes 2099200 | tf_op jit(solution)/shard_map/reduce_sum | solution.py:16
  48.6 2.3 %fusion.8 = f32[512]{0:T(512)S(1)} fusion(bf16[512,2048]{1,0:T(8,128)(2,1)} %get-tuple-element.7, f32[512]{0:T(512)S(1)} %broadcast_multiply_fusion), kind=kLoop, calls=%fused_computation.15 | loop fusion | flops 4193792 | bytes 2101248 | tf_op jit(solution)/shard_map/reduce_sum | solution.py:18
  50.9 0.0 copy-done.7
  50.9 0.0 copy-done.1
  50.9 0.7 fusion.10
  51.6 0.0 copy-done.9
  51.6 0.0 copy-start.3
  51.6 0.0 copy-start.10
  51.6 0.7 fusion.19
  52.4 0.6 copy-done.3
  53.0 0.1 broadcast.115
  53.0 1.9 %select_n.81 = bf16[2048,256]{1,0:T(8,128)(2,1)S(1)} dynamic-update-slice(bf16[2048,256]{1,0:T(8,128)(2,1)S(1)} %broadcast.115, bf16[512,256]{1,0:T(8,128)(2,1)S(1)} %fusion.19, s32[]{:T(128)S(6)} %select_n.76, s32[]{:T(128)} %constant.16.clone.1) | dynamic-update-slice | bytes 524292 | tf_op jit(solution)/shard_map/jit(_where)/select_n | solution.py:264
  54.9 0.0 copy-start.2
  55.0 0.0 copy-done.10
  55.0 0.9 copy-done.2
  55.9 1.8 %gather_fusion = bf16[64,4,8,256]{3,2,1,0:T(8,128)(2,1)S(1)} fusion(bf16[64,4,8,256]{3,2,1,0:T(8,128)(2,1)} %get-tuple-element.6, s32[1024]{0:T(1024)S(1)} %pad_clamp_fusion.1), kind=kCustom, calls=%fused_computation | custom fusion | bytes 2097408 | tf_op jit(solution)/shard_map/jit(_take)/gather | solution.py:256
  57.8 0.1 broadcast_in_dim.72
  57.9 0.1 broadcast_in_dim.73
  58.0 3.8 %fusion.20 = bf16[2048,256]{1,0:T(8,128)(2,1)} fusion(bf16[2048,256]{1,0:T(8,128)(2,1)} %copy-done.2, bf16[64,4,8,256]{3,2,1,0:T(8,128)(2,1)S(1)} %gather_fusion, pred[2048]{0:T(1024)(128)(4,1)S(1)} %broadcast_in_dim.73, pred[2048]{0:T(1024)(128)(4,1)S(1)} %iota_compare_fusion.2), kind=kLoop, calls=%fused_computation.30 | loop fusion | flops 1048576 | bytes 3149824 | tf_op jit(solution)/shard_map/jit(_where)/select_n | solution.py:261
  61.8 0.0 copy-done
  61.8 0.0 copy-start.5
  61.8 3.8 %convolution_convert_fusion = bf16[512,512]{0,1:T(8,128)(2,1)} fusion(bf16[512,2048]{1,0:T(8,128)(2,1)} %copy-done.3, bf16[2048,512]{1,0:T(8,128)(2,1)S(1)} %copy-done), kind=kOutput, calls=%fused_computation.25 | convolution fusion | flops 1074003968 | bytes 4718592 | tf_op jit(solution)/shard_map/dot_general | solution.py:253
  65.6 1.9 %iota_compare_fusion = pred[512,2048]{0,1:T(8,128)(4,1)} fusion(s32[512]{0:T(512)S(1)} %iota_add_fusion), kind=kLoop, calls=%fused_computation.19 | loop fusion | flops 1048576 | bytes 1050624 | tf_op jit(solution)/shard_map/le | solution.py:285
  67.5 0.0 copy-done.5
  67.5 10.5 %fusion.26 = (f32[4,512]{1,0:T(4,128)S(1)}, f32[4,512,2048]{1,2,0:T(8,128)}) fusion(pred[512,2048]{0,1:T(8,128)(4,1)} %iota_compare_fusion, bf16[512,4,128]{0,2,1:T(8,128)(2,1)} %bitcast.76, bf16[2048,256]{1,0:T(8,128)(2,1)S(1)} %copy-done.5), kind=kOutput, calls=%fused_computation.57 | convolution fusion | flops 1090521088 | bytes 18882560 | tf_op jit(solution)/shard_map/sub | solution.py:288
  78.0 0.0 copy-start.8
  78.0 7.2 %fusion.18 = bf16[128,4,512]{2,0,1:T(8,128)(2,1)S(1)} fusion(f32[4,512,2048]{1,2,0:T(8,128)} %get-tuple-element.11, f32[4,512]{1,0:T(4,128)S(1)} %get-tuple-element.10, bf16[2048,256]{1,0:T(8,128)(2,1)S(1)} %copy-done.5), kind=kOutput, calls=%fused_computation.26 | convolution fusion | flops 1082392576 | bytes 17833984 | tf_op jit(solution)/shard_map/htk,kd->thd/dot_general | solution.py:290
  85.2 0.0 copy-start.11
  85.2 0.0 copy-done.8
  85.2 2.6 %convert_bitcast_fusion.part_ref = bf16[4,512,512]{2,1,0:T(8,128)(2,1)} fusion(bf16[512,512,1]{0,1,2:T(8,128)(2,1)S(1)} %bitcast.77, bf16[64,4,8,512]{3,2,1,0:T(8,128)(2,1)S(1)} %bitcast.74), kind=kOutput, calls=%fused_computation.23 | convolution fusion | flops 1074790400 | bytes 4718592 | tf_op jit(solution)/shard_map/tk,kpn->ptn/dot_general | solution.py:295
  87.8 0.0 copy-start.4
  87.8 1.0 constant_dynamic-slice_fusion
  88.9 0.0 copy-done.11
  88.9 0.1 select_reduce_fusion
  89.0 0.6 gather_fusion.1
  89.6 0.8 broadcast_select_fusion.share_ref
  90.5 33.1 %shard_map.114 = (bf16[4,512,512]{2,1,0:T(8,128)(2,1)}, bf16[64,8,256]{2,1,0:T(8,128)(2,1)}) custom-call(bf16[4,512,512]{2,1,0:T(8,128)(2,1)} %convert_bitcast_fusion.part_ref, bf16[64,8,256]{2,1,0:T(8,128)(2,1)} %broadcast_select_fusion.share_ref), custom_call_target="tpu_custom_call" | custom-call | tf_op jit(solution)/shard_map/pallas_call | solution.py:206
  123.5 0.0 copy-start.6
  123.6 2.0 %convert_reduce_fusion.1 = f32[512,512]{1,0:T(8,128)S(1)} fusion(bf16[4,512,512]{2,1,0:T(8,128)(2,1)} %get-tuple-element.8), kind=kLoop, calls=%fused_computation.18 | loop fusion | flops 1835008 | bytes 3145728 | tf_op jit(solution)/shard_map/reduce_sum | solution.py:300
  125.6 0.0 copy-done.4
  125.6 1.0 select_convert_fusion
  126.5 0.0 copy-done.6
  126.5 0.7 copy.44
  (12 shorter events, 0.1 us)
Async XLA Ops:
  0.6 61.2 %copy-start = (bf16[2048,512]{1,0:T(8,128)(2,1)S(1)}, bf16[2048,512]{1,0:T(8,128)(2,1)}, u32[]{:S(2)}) copy-start(bf16[2048,512]{1,0:T(8,128)(2,1)} %param.12) | copy-start | bytes 6291460
  0.6 50.2 %copy-start.7 = (f32[2048]{0:T(1024)S(1)}, f32[2048]{0:T(1024)}, u32[]{:S(2)}) copy-start(f32[2048]{0:T(1024)} %param.11) | copy-start | bytes 24580
  46.5 4.4 %copy-start.1 = (bf16[512,2048]{1,0:T(8,128)(2,1)S(1)}, bf16[512,2048]{1,0:T(8,128)(2,1)}, u32[]{:S(2)}) copy-start(bf16[512,2048]{1,0:T(8,128)(2,1)} %get-tuple-element.7) | copy-start | bytes 6291460
  46.5 5.1 %copy-start.9 = (bf16[2048,256]{1,0:T(8,128)(2,1)S(1)}, bf16[2048,256]{1,0:T(8,128)(2,1)}, u32[]{:S(2)}) copy-start(bf16[2048,256]{1,0:T(8,128)(2,1)} %param.13) | copy-start | bytes 3145732
  51.6 1.4 %copy-start.3 = (bf16[512,2048]{1,0:T(8,128)(2,1)}, bf16[512,2048]{1,0:T(8,128)(2,1)S(1)}, u32[]{:S(2)}) copy-start(bf16[512,2048]{1,0:T(8,128)(2,1)S(1)} %fusion.10) | copy-start | bytes 6291460
  51.6 3.3 %copy-start.10 = (s32[1,64]{1,0:T(1,128)S(1)}, s32[1,64]{1,0:T(1,128)}, u32[]{:S(2)}) copy-start(s32[1,64]{1,0:T(1,128)} %param.17) | copy-start | bytes 772
  54.9 1.0 copy-start.2
  61.8 5.6 %copy-start.5 = (bf16[2048,256]{1,0:T(8,128)(2,1)S(1)}, bf16[2048,256]{1,0:T(8,128)(2,1)}, u32[]{:S(2)}) copy-start(bf16[2048,256]{1,0:T(8,128)(2,1)} %fusion.20) | copy-start | bytes 3145732
  78.0 7.2 %copy-start.8 = (bf16[512,2048]{1,0:T(8,128)(2,1)S(1)}, bf16[512,2048]{1,0:T(8,128)(2,1)}, u32[]{:S(2)}) copy-start(bf16[512,2048]{1,0:T(8,128)(2,1)} %param.14) | copy-start | bytes 6291460
  85.2 3.7 %copy-start.11 = (s32[1,64]{1,0:T(1,128)S(1)}, s32[1,64]{1,0:T(1,128)}, u32[]{:S(2)}) copy-start(s32[1,64]{1,0:T(1,128)} %param.18) | copy-start | bytes 772
  87.8 37.7 %copy-start.4 = (bf16[512,512]{1,0:T(8,128)(2,1)S(1)}, bf16[512,512]{1,0:T(8,128)(2,1)}, u32[]{:S(2)}) copy-start(bf16[512,512]{1,0:T(8,128)(2,1)} %tok_ref.1) | copy-start | bytes 1572868
  123.5 3.0 %copy-start.6 = (bf16[64,8,256]{2,1,0:T(8,128)(2,1)S(1)}, bf16[64,8,256]{2,1,0:T(8,128)(2,1)}, u32[]{:S(2)}) copy-start(bf16[64,8,256]{2,1,0:T(8,128)(2,1)} %get-tuple-element.15) | copy-start | bytes 786436

commit v4 on v3

v4 whole, which is shorter than its diff:
```python
import functools

import jax
import jax.numpy as jnp
from jax import lax
from jax.experimental import pallas as pl
from jax.experimental.pallas import tpu as pltpu
from jax.sharding import PartitionSpec as P

EPSILON = 1e-05
MASKED = -1e30


def normalize(rows, norm_gain):
    values = rows.astype(jnp.float32)
    average = jnp.mean(values, axis=1, keepdims=True)
    centred = values - average
    spread = jnp.mean(centred * centred, axis=1, keepdims=True)
    return (centred * lax.rsqrt(spread + EPSILON) * norm_gain).astype(jnp.bfloat16)


MESH = pl.DeviceIdType.MESH


def _remote(src, dst, send, recv, dev):
    return pltpu.make_async_remote_copy(
        src_ref=src, dst_ref=dst, send_sem=send, recv_sem=recv, device_id=dev, device_id_type=MESH
    )


def _greet(na, nb, s, t, left, right):
    barrier = pltpu.get_barrier_semaphore()
    a = s // nb
    b = s % nb

    def one_b(k, carry):
        pl.semaphore_signal(barrier, inc=1, device_id={"seq": a * nb + lax.rem(b + k, nb), "tp": t},
                            device_id_type=MESH)
        return carry

    def one_a(k, carry):
        pl.semaphore_signal(barrier, inc=1, device_id={"seq": lax.rem(a + k, na) * nb + b, "tp": t},
                            device_id_type=MESH)
        return carry

    lax.fori_loop(1, nb, one_b, 0)
    lax.fori_loop(1, na, one_a, 0)
    for p in (left, right):
        pl.semaphore_signal(barrier, inc=1, device_id={"seq": s, "tp": p}, device_id_type=MESH)
    pl.semaphore_wait(barrier, na + nb)


class SeqAllToAll:
    def __init__(self, na, nb, s, t, src, stage, dst, sems):
        self.na, self.nb, self.t, self.src, self.stage, self.dst = na, nb, t, src, stage, dst
        self.a = s // nb
        self.b = s % nb
        self.s1send, self.s1recv, self.s2send, self.s2recv, self.local = sems

    def _dev(self, a, b):
        return {"seq": a * self.nb + b, "tp": self.t}

    def _out1(self, k):
        peer = lax.rem(self.b + k, self.nb)
        return _remote(self.src.at[:, peer], self.stage.at[self.b], self.s1send.at[k],
                       self.s1recv.at[k], self._dev(self.a, peer))

    def _in1(self, k):
        sender = lax.rem(self.b + self.nb - k, self.nb)
        return _remote(self.src.at[:, self.b], self.stage.at[sender], self.s1send.at[k],
                       self.s1recv.at[k], self._dev(self.a, sender))

    def _out2(self, k):
        peer = lax.rem(self.a + k, self.na)
        return _remote(self.stage.at[:, peer], self.dst(self.a), self.s2send.at[k],
                       self.s2recv.at[k], self._dev(peer, self.b))

    def _in2(self, k):
        sender = lax.rem(self.a + self.na - k, self.na)
        return _remote(self.stage.at[:, self.a], self.dst(sender), self.s2send.at[k],
                       self.s2recv.at[k], self._dev(sender, self.b))

    def first(self):
        self.own1 = pltpu.make_async_copy(self.src.at[:, self.b], self.stage.at[self.b],
                                          self.local.at[0])
        self.own1.start()
        _loop(self.nb, lambda k: self._out1(k).start())

    def second(self):
        _loop(self.nb, lambda k: self._in1(k).wait_recv())
        self.own1.wait()
        self.own2 = pltpu.make_async_copy(self.stage.at[:, self.a], self.dst(self.a),
                                          self.local.at[1])
        self.own2.start()
        _loop(self.na, lambda k: self._out2(k).start())

    def arrived(self):
        _loop(self.na, lambda k: self._in2(k).wait_recv())
        self.own2.wait()

    def finish(self):
        _loop(self.nb, lambda k: self._out1(k).wait_send())
        _loop(self.na, lambda k: self._out2(k).wait_send())


def _seq_scratch(na, nb, share, width, dtype):
    return [
        pltpu.VMEM((nb, na, share, width), dtype),
        pltpu.SemaphoreType.DMA((nb,)),
        pltpu.SemaphoreType.DMA((nb,)),
        pltpu.SemaphoreType.DMA((na,)),
        pltpu.SemaphoreType.DMA((na,)),
        pltpu.SemaphoreType.DMA((2,)),
    ]


def _loop(n, fn):
    def step(k, carry):
        fn(k)
        return carry

    lax.fori_loop(1, n, step, 0)


def _in_kernel(na, nb, ntp, tok_ref, cache_ref, tok_out, cache_out, tsend, trecv, csend, crecv,
               lsem, stage, s1send, s1recv, s2send, s2recv, slocal):
    s = lax.axis_index("seq")
    t = lax.axis_index("tp")
    right = lax.rem(t + 1, ntp)
    left = lax.rem(t + ntp - 1, ntp)
    across = lax.rem(t + 2, ntp)
    rdev = {"seq": s, "tp": right}
    ldev = {"seq": s, "tp": left}
    rows, cols = tok_ref.shape
    half = rows // 2
    blocks = na * nb // 2
    _greet(na, nb, s, t, left, right)

    def tok_cols(p):
        return pl.ds(p * cols, cols)

    a2a = SeqAllToAll(na, nb, s, t, cache_ref, stage, lambda a_src: cache_out.at[a_src, :, t],
                      (s1send, s1recv, s2send, s2recv, slocal))
    a2a.first()

    own_tok = pltpu.make_async_copy(tok_ref, tok_out.at[:, tok_cols(t)], lsem.at[0])
    own_tok.start()
    tok_r = _remote(tok_ref, tok_out.at[:, tok_cols(t)], tsend.at[0], trecv.at[0], rdev)
    tok_l = _remote(tok_ref, tok_out.at[:, tok_cols(t)], tsend.at[1], trecv.at[1], ldev)
    tok_r.start()
    tok_l.start()

    a2a.second()

    _remote(tok_ref, tok_out.at[:, tok_cols(left)], tsend.at[0], trecv.at[0], ldev).wait_recv()
    fwd_r = _remote(tok_out.at[pl.ds(0, half), tok_cols(left)],
                    tok_out.at[pl.ds(0, half), tok_cols(left)], tsend.at[2], trecv.at[2], rdev)
    fwd_r.start()
    _remote(tok_ref, tok_out.at[:, tok_cols(right)], tsend.at[1], trecv.at[1], rdev).wait_recv()
    fwd_l = _remote(tok_out.at[pl.ds(half, half), tok_cols(right)],
                    tok_out.at[pl.ds(half, half), tok_cols(right)], tsend.at[3], trecv.at[3], ldev)
    fwd_l.start()

    a2a.arrived()
    flat = cache_out.reshape(na * nb, ntp, *cache_out.shape[3:])
    mine = flat.at[:, t]
    cache_r = _remote(mine, mine, csend.at[0], crecv.at[0], rdev)
    cache_l = _remote(mine, mine, csend.at[1], crecv.at[1], ldev)
    cache_r.start()
    cache_l.start()
    _remote(mine, flat.at[:, left], csend.at[0], crecv.at[0], ldev).wait_recv()
    cfwd_r = _remote(flat.at[pl.ds(0, blocks), left], flat.at[pl.ds(0, blocks), left],
                     csend.at[2], crecv.at[2], rdev)
    cfwd_r.start()
    _remote(mine, flat.at[:, right], csend.at[1], crecv.at[1], rdev).wait_recv()
    cfwd_l = _remote(flat.at[pl.ds(blocks, blocks), right], flat.at[pl.ds(blocks, blocks), right],
                     csend.at[3], crecv.at[3], ldev)
    cfwd_l.start()

    _remote(tok_ref.at[pl.ds(0, half)], tok_out.at[pl.ds(0, half), tok_cols(across)],
            tsend.at[2], trecv.at[2], ldev).wait_recv()
    _remote(tok_ref.at[pl.ds(half, half)], tok_out.at[pl.ds(half, half), tok_cols(across)],
            tsend.at[3], trecv.at[3], rdev).wait_recv()
    _remote(flat.at[pl.ds(0, blocks), t], flat.at[pl.ds(0, blocks), across],
            csend.at[2], crecv.at[2], ldev).wait_recv()
    _remote(flat.at[pl.ds(blocks, blocks), t], flat.at[pl.ds(blocks, blocks), across],
            csend.at[3], crecv.at[3], rdev).wait_recv()
    for c in (tok_r, tok_l, fwd_r, fwd_l, cache_r, cache_l, cfwd_r, cfwd_l):
        c.wait_send()
    a2a.finish()
    own_tok.wait()


def gather_inputs(tokens, old_cache, na, nb, ntp):
    rows, cols = tokens.shape
    _, share, width = old_cache.shape
    cache4 = old_cache.reshape(na, nb, share, width)
    return pl.pallas_call(
        functools.partial(_in_kernel, na, nb, ntp),
        out_shape=(
            jax.ShapeDtypeStruct((rows, ntp * cols), tokens.dtype),
            jax.ShapeDtypeStruct((na, nb, ntp, share, width), old_cache.dtype),
        ),
        in_specs=[pl.BlockSpec(memory_space=pl.ANY)] * 2,
        out_specs=(pl.BlockSpec(memory_space=pl.ANY), pl.BlockSpec(memory_space=pl.ANY)),
        scratch_shapes=[
            pltpu.SemaphoreType.DMA((4,)),
            pltpu.SemaphoreType.DMA((4,)),
            pltpu.SemaphoreType.DMA((4,)),
            pltpu.SemaphoreType.DMA((4,)),
            pltpu.SemaphoreType.DMA((2,)),
        ] + _seq_scratch(na, nb, share, width, old_cache.dtype),
        compiler_params=pltpu.CompilerParams(collective_id=0, has_side_effects=True),
    )(tokens, cache4)


def _out_kernel(na, nb, ntp, part_ref, share_ref, rs_out, new_out, stage_rs, rsend, rrecv, lsem,
                stage, s1send, s1recv, s2send, s2recv, slocal):
    s = lax.axis_index("seq")
    t = lax.axis_index("tp")
    right = lax.rem(t + 1, ntp)
    left = lax.rem(t + ntp - 1, ntp)
    across = lax.rem(t + 2, ntp)
    rdev = {"seq": s, "tp": right}
    ldev = {"seq": s, "tp": left}
    half = part_ref.shape[1] // 2
    _greet(na, nb, s, t, left, right)

    a2a = SeqAllToAll(na, nb, s, t, share_ref, stage, lambda a_src: new_out.at[a_src],
                      (s1send, s1recv, s2send, s2recv, slocal))
    a2a.first()

    own_part = pltpu.make_async_copy(part_ref.at[t], rs_out.at[t], lsem.at[0])
    own_part.start()
    to_r = _remote(part_ref.at[right], rs_out.at[t], rsend.at[0], rrecv.at[0], rdev)
    to_l = _remote(part_ref.at[left], rs_out.at[t], rsend.at[1], rrecv.at[1], ldev)
    via_r = _remote(part_ref.at[across, pl.ds(0, half)], stage_rs.at[0], rsend.at[2], rrecv.at[2],
                    rdev)
    via_l = _remote(part_ref.at[across, pl.ds(half, half)], stage_rs.at[1], rsend.at[3],
                    rrecv.at[3], ldev)
    for c in (to_r, to_l, via_r, via_l):
        c.start()

    a2a.second()

    _remote(part_ref.at[across, pl.ds(0, half)], stage_rs.at[0], rsend.at[2], rrecv.at[2],
            ldev).wait_recv()
    fwd_r = _remote(stage_rs.at[0], rs_out.at[left, pl.ds(0, half)], rsend.at[4], rrecv.at[4],
                    rdev)
    fwd_r.start()
    _remote(part_ref.at[across, pl.ds(half, half)], stage_rs.at[1], rsend.at[3], rrecv.at[3],
            rdev).wait_recv()
    fwd_l = _remote(stage_rs.at[1], rs_out.at[right, pl.ds(half, half)], rsend.at[5],
                    rrecv.at[5], ldev)
    fwd_l.start()

    a2a.arrived()
    _remote(part_ref.at[t], rs_out.at[left], rsend.at[0], rrecv.at[0], ldev).wait_recv()
    _remote(part_ref.at[t], rs_out.at[right], rsend.at[1], rrecv.at[1], rdev).wait_recv()
    _remote(stage_rs.at[0], rs_out.at[across, pl.ds(0, half)], rsend.at[4], rrecv.at[4],
            ldev).wait_recv()
    _remote(stage_rs.at[1], rs_out.at[across, pl.ds(half, half)], rsend.at[5], rrecv.at[5],
            rdev).wait_recv()
    for c in (to_r, to_l, via_r, via_l, fwd_r, fwd_l):
        c.wait_send()
    a2a.finish()
    own_part.wait()


def scatter_outputs(partial, share, na, nb, ntp):
    _, rows, cols = partial.shape
    _, block, width = share.shape
    share4 = share.reshape(na, nb, block, width)
    rs, new = pl.pallas_call(
        functools.partial(_out_kernel, na, nb, ntp),
        out_shape=(
            jax.ShapeDtypeStruct(partial.shape, partial.dtype),
            jax.ShapeDtypeStruct(share4.shape, share.dtype),
        ),
        in_specs=[pl.BlockSpec(memory_space=pl.ANY)] * 2,
        out_specs=(pl.BlockSpec(memory_space=pl.ANY), pl.BlockSpec(memory_space=pl.ANY)),
        scratch_shapes=[
            pltpu.VMEM((2, rows // 2, cols), partial.dtype),
            pltpu.SemaphoreType.DMA((6,)),
            pltpu.SemaphoreType.DMA((6,)),
            pltpu.SemaphoreType.DMA((1,)),
        ] + _seq_scratch(na, nb, block, width, share.dtype),
        compiler_params=pltpu.CompilerParams(collective_id=1, has_side_effects=True),
    )(partial, share4)
    return rs, new.reshape(share.shape)


def body(
    tokens,
    norm_gain,
    w_query,
    w_keyval,
    w_out,
    span_lens,
    cached_lens,
    old_table,
    new_table,
    old_cache,
):
    groups = lax.axis_size("seq")
    tp_count = lax.axis_size("tp")
    tp_index = lax.axis_index("tp")
    holders = old_table[0]
    held_len = cached_lens[0]
    span_len = span_lens[0]
    tok_rows, tok_cols = tokens.shape
    share = old_cache.shape[1]
    width = old_cache.shape[2]
    block_rows = share * tp_count
    capacity = groups * block_rows

    inner = min(groups, 8)
    outer = groups // inner
    tok_all, cache_all = gather_inputs(tokens, old_cache, outer, inner, tp_count)
    cache_all = cache_all.reshape(groups, tp_count, share, width)
    full_rows = tok_all
    normed = normalize(full_rows, norm_gain)
    query = jnp.dot(normed, w_query, preferred_element_type=jnp.float32).astype(jnp.bfloat16)
    keyval = jnp.dot(normed, w_keyval, preferred_element_type=jnp.float32).astype(jnp.bfloat16)

    cached = jnp.take(cache_all, holders, axis=0).reshape(capacity, width)
    shifted = lax.dynamic_update_slice(
        jnp.zeros((capacity, width), jnp.bfloat16), keyval, (held_len, jnp.int32(0))
    )
    positions = lax.broadcasted_iota(jnp.int32, (capacity, 1), 0)
    fresh = jnp.where(
        positions < held_len,
        cached,
        jnp.where(positions < held_len + span_len, shifted, jnp.zeros_like(shifted)),
    )
    fresh_share = lax.dynamic_slice_in_dim(
        fresh.reshape(groups, block_rows, width), tp_index * share, share, 1
    )
    targets = new_table[0]
    device_ids = lax.broadcasted_iota(jnp.int32, (groups, groups), 0)
    block_ids = lax.broadcasted_iota(jnp.int32, (groups, groups), 1)
    matches = targets[None, :] == device_ids
    sources = jnp.sum(jnp.where(matches, block_ids, 0), axis=1)
    sorted_share = jnp.take(fresh_share, sources, axis=0)
    head_size = width // 2
    keys = fresh[:, :head_size]
    values = fresh[:, head_size:]
    local_heads = query.shape[1] // head_size
    query3 = query.reshape(tok_rows, local_heads, head_size)
    scores = jnp.einsum(
        "thd,kd->htk", query3, keys, preferred_element_type=jnp.float32
    ) * head_size ** (-0.5)
    row_pos = lax.broadcasted_iota(jnp.int32, (tok_rows, 1), 0)
    key_pos = lax.broadcasted_iota(jnp.int32, (1, capacity), 1)
    allowed = key_pos <= held_len + row_pos
    scores = jnp.where(allowed[None], scores, MASKED)
    top = jnp.max(scores, axis=2, keepdims=True)
    weights = jnp.exp(scores - top)
    probs = (weights / jnp.sum(weights, axis=2, keepdims=True)).astype(jnp.bfloat16)
    context = jnp.einsum("htk,kd->thd", probs, values, preferred_element_type=jnp.float32).astype(
        jnp.bfloat16
    )
    context = context.reshape(tok_rows, local_heads * head_size)
    out_blocks = w_out.reshape(w_out.shape[0], tp_count, tok_cols)
    partial_out = jnp.einsum(
        "tk,kpn->ptn", context, out_blocks, preferred_element_type=jnp.float32
    ).astype(jnp.bfloat16)
    summed, new_cache = scatter_outputs(partial_out, sorted_share, outer, inner, tp_count)
    summed = summed.astype(jnp.float32)
    total = tokens.astype(jnp.float32) + jnp.sum(summed, axis=0)
    mixed = jnp.where(row_pos < span_len, total, jnp.zeros_like(total)).astype(jnp.bfloat16)
    return (mixed, new_cache)


def solution(mesh):
    in_specs = (
        P("seq", "tp"),
        P(),
        P(None, "tp"),
        P(),
        P("tp", None),
        P("seq"),
        P("seq"),
        P("seq", None),
        P("seq", None),
        P("seq", "tp", None),
    )
    out_specs = (P("seq", "tp"), P("seq", "tp", None))
    return jax.shard_map(body, mesh=mesh, in_specs=in_specs, out_specs=out_specs, check_vma=False)
```

time: 128 us -> 119 us (0.930)
  Pallas kernels: 77.4 us -> 68.8 us
    pallas_call x2, Pallas kernels: 77.4 us -> 68.8 us  [the longest x1 38.1 us: gather_inputs(): pl.pallas_call(functools.partial(_in_kernel, na, nb, ntp), out_shape=(jax...]
where the time goes in v4:
time: 119 us
  Pallas kernels  68.8 us (58%)
  matrix products  24.8 us (21%)
  other arithmetic  14.7 us (12%)
  local copies, waits for them, and re-layouts  8.05 us (7%)
  between operations  2.35 us (2%)
    pallas_call x1, Pallas kernels, gather_inputs(): pl.pallas_call(functools.partial(_in_kernel, na, nb, ntp), out_shape=(jax...  38.1 us
    pallas_call x1, Pallas kernels, scatter_outputs(): pl.pallas_call(functools.partial(_out_kernel, na, nb, ntp), out_shape=(ja...  30.7 us
    sub x1, matrix products, body(): weights = jnp.exp(scores - top)  10.5 us
    dot_general x1, matrix products, body(): jnp.einsum('htk,kd->thd', probs, values, preferred_element_type=jnp.float32)  7.19 us
    select_n x1, other arithmetic, body(): jnp.where(positions < held_len, cached, jnp.where(positions < held_len +...  3.81 us
    dot_general x1, matrix products, body(): jnp.dot(normed, w_query, preferred_element_type=jnp.float32)  3.77 us
    dot_general x1, matrix products, body(): jnp.einsum('tk,kpn->ptn', context, out_blocks, preferred_element_type=jnp...  2.63 us

profile of v4, /device:TPU:1, one launch (start us, length us, event | category | flops | bytes accessed | tf_op | source)
XLA Modules:
  0.0 118.8 jit_solution(6897399138436948307)
XLA Ops:
  0.6 0.0 copy-start
  0.6 0.0 copy-start.7
  2.1 38.1 %shard_map.113 = (bf16[512,2048]{1,0:T(8,128)(2,1)}, bf16[8,8,4,8,256]{4,3,2,1,0:T(8,128)(2,1)}) custom-call(bf16[512,512]{1,0:T(8,128)(2,1)} %tok_ref.1, bf16[8,8,8,256]{3,2,1,0:T(8,128)(2,1)} %bitcast.80), custom_call_target="tpu_custom_call" | custom-call | tf_op jit(solution)/shard_map/pallas_call | solution.py:198
  40.3 0.0 copy-start.1
  40.3 0.0 copy-start.9
  40.3 2.1 %convert_reduce_fusion = f32[512]{0:T(512)S(1)} fusion(bf16[512,2048]{1,0:T(8,128)(2,1)} %get-tuple-element.7), kind=kLoop, calls=%fused_computation.12 | loop fusion | flops 2096640 | bytes 2099200 | tf_op jit(solution)/shard_map/reduce_sum | solution.py:16
  42.4 2.3 %fusion.8 = f32[512]{0:T(512)S(1)} fusion(bf16[512,2048]{1,0:T(8,128)(2,1)} %get-tuple-element.7, f32[512]{0:T(512)S(1)} %broadcast_multiply_fusion), kind=kLoop, calls=%fused_computation.15 | loop fusion | flops 4193792 | bytes 2101248 | tf_op jit(solution)/shard_map/reduce_sum | solution.py:18
  44.7 0.0 copy-done.7
  44.7 0.0 copy-done.1
  44.7 0.7 fusion.10
  45.4 0.0 copy-done.9
  45.4 0.0 copy-start.3
  45.4 0.0 copy-start.10
  45.5 0.7 fusion.19
  46.2 0.6 copy-done.3
  46.8 0.1 broadcast.121
  46.9 1.9 %select_n.83 = bf16[2048,256]{1,0:T(8,128)(2,1)S(1)} dynamic-update-slice(bf16[2048,256]{1,0:T(8,128)(2,1)S(1)} %broadcast.121, bf16[512,256]{1,0:T(8,128)(2,1)S(1)} %fusion.19, s32[]{:T(128)S(6)} %select_n.78, s32[]{:T(128)} %constant.16.clone.1) | dynamic-update-slice | bytes 524292 | tf_op jit(solution)/shard_map/jit(_where)/select_n | solution.py:334
  48.8 0.0 copy-start.2
  48.8 0.0 copy-done.10
  48.8 0.9 copy-done.2
  49.7 1.8 %gather_fusion = bf16[64,4,8,256]{3,2,1,0:T(8,128)(2,1)S(1)} fusion(bf16[64,4,8,256]{3,2,1,0:T(8,128)(2,1)} %bitcast.78, s32[1024]{0:T(1024)S(1)} %pad_clamp_fusion.1), kind=kCustom, calls=%fused_computation | custom fusion | bytes 2097408 | tf_op jit(solution)/shard_map/jit(_take)/gather | solution.py:326
  51.6 0.1 broadcast_in_dim.72
  51.7 0.1 broadcast_in_dim.73
  51.9 3.8 %fusion.20 = bf16[2048,256]{1,0:T(8,128)(2,1)} fusion(bf16[2048,256]{1,0:T(8,128)(2,1)} %copy-done.2, bf16[64,4,8,256]{3,2,1,0:T(8,128)(2,1)S(1)} %gather_fusion, pred[2048]{0:T(1024)(128)(4,1)S(1)} %broadcast_in_dim.73, pred[2048]{0:T(1024)(128)(4,1)S(1)} %iota_compare_fusion.2), kind=kLoop, calls=%fused_computation.30 | loop fusion | flops 1048576 | bytes 3149824 | tf_op jit(solution)/shard_map/jit(_where)/select_n | solution.py:331
  55.7 0.0 copy-done
  55.7 0.0 copy-start.5
  55.7 3.8 %convolution_convert_fusion = bf16[512,512]{0,1:T(8,128)(2,1)} fusion(bf16[512,2048]{1,0:T(8,128)(2,1)} %copy-done.3, bf16[2048,512]{1,0:T(8,128)(2,1)S(1)} %copy-done), kind=kOutput, calls=%fused_computation.25 | convolution fusion | flops 1074003968 | bytes 4718592 | tf_op jit(solution)/shard_map/dot_general | solution.py:323
  59.5 1.9 %iota_compare_fusion = pred[512,2048]{0,1:T(8,128)(4,1)} fusion(s32[512]{0:T(512)S(1)} %iota_add_fusion), kind=kLoop, calls=%fused_computation.19 | loop fusion | flops 1048576 | bytes 1050624 | tf_op jit(solution)/shard_map/le | solution.py:355
  61.3 0.0 copy-done.5
  61.3 10.5 %fusion.26 = (f32[4,512]{1,0:T(4,128)S(1)}, f32[4,512,2048]{1,2,0:T(8,128)}) fusion(pred[512,2048]{0,1:T(8,128)(4,1)} %iota_compare_fusion, bf16[512,4,128]{0,2,1:T(8,128)(2,1)} %bitcast.84, bf16[2048,256]{1,0:T(8,128)(2,1)S(1)} %copy-done.5), kind=kOutput, calls=%fused_computation.57 | convolution fusion | flops 1090521088 | bytes 18882560 | tf_op jit(solution)/shard_map/sub | solution.py:358
  71.8 0.0 copy-start.8
  71.8 7.2 %fusion.18 = bf16[128,4,512]{2,0,1:T(8,128)(2,1)S(1)} fusion(f32[4,512,2048]{1,2,0:T(8,128)} %get-tuple-element.11, f32[4,512]{1,0:T(4,128)S(1)} %get-tuple-element.10, bf16[2048,256]{1,0:T(8,128)(2,1)S(1)} %copy-done.5), kind=kOutput, calls=%fused_computation.26 | convolution fusion | flops 1082392576 | bytes 17833984 | tf_op jit(solution)/shard_map/htk,kd->thd/dot_general | solution.py:360
  79.0 0.0 copy-start.11
  79.0 0.0 copy-done.8
  79.0 2.6 %convert_bitcast_fusion.part_ref = bf16[4,512,512]{2,1,0:T(8,128)(2,1)} fusion(bf16[512,512,1]{0,1,2:T(8,128)(2,1)S(1)} %bitcast.85, bf16[64,4,8,512]{3,2,1,0:T(8,128)(2,1)S(1)} %bitcast.82), kind=kOutput, calls=%fused_computation.23 | convolution fusion | flops 1074790400 | bytes 4718592 | tf_op jit(solution)/shard_map/tk,kpn->ptn/dot_general | solution.py:365
  81.7 0.0 copy-start.4
  81.7 1.0 constant_dynamic-slice_fusion
  82.7 0.0 copy-done.11
  82.7 0.1 select_reduce_fusion
  82.9 0.6 gather_fusion.1
  83.5 0.1 reduce_sum.53
  83.5 0.8 broadcast_select_fusion.share_ref
  84.4 30.7 %shard_map.114 = (bf16[4,512,512]{2,1,0:T(8,128)(2,1)}, bf16[8,8,8,256]{3,2,1,0:T(8,128)(2,1)}) custom-call(bf16[4,512,512]{2,1,0:T(8,128)(2,1)} %convert_bitcast_fusion.part_ref, bf16[8,8,8,256]{3,2,1,0:T(8,128)(2,1)} %broadcast_select_fusion.share_ref), custom_call_target="tpu_custom_call" | custom-call | tf_op jit(solution)/shard_map/pallas_call | solution.py:274
  115.1 0.0 copy-start.6
  115.1 2.0 %convert_reduce_fusion.1 = f32[512,512]{1,0:T(8,128)S(1)} fusion(bf16[4,512,512]{2,1,0:T(8,128)(2,1)} %get-tuple-element.8), kind=kLoop, calls=%fused_computation.18 | loop fusion | flops 1835008 | bytes 3145728 | tf_op jit(solution)/shard_map/reduce_sum | solution.py:370
  117.1 0.0 copy-done.4
  117.1 1.0 select_convert_fusion
  118.1 0.0 copy-done.6
  118.1 0.7 copy.44
  (12 shorter events, 0.1 us)
Async XLA Ops:
  0.6 55.0 %copy-start = (bf16[2048,512]{1,0:T(8,128)(2,1)S(1)}, bf16[2048,512]{1,0:T(8,128)(2,1)}, u32[]{:S(2)}) copy-start(bf16[2048,512]{1,0:T(8,128)(2,1)} %param.12) | copy-start | bytes 6291460
  0.6 44.1 %copy-start.7 = (f32[2048]{0:T(1024)S(1)}, f32[2048]{0:T(1024)}, u32[]{:S(2)}) copy-start(f32[2048]{0:T(1024)} %param.11) | copy-start | bytes 24580
  40.3 4.4 %copy-start.1 = (bf16[512,2048]{1,0:T(8,128)(2,1)S(1)}, bf16[512,2048]{1,0:T(8,128)(2,1)}, u32[]{:S(2)}) copy-start(bf16[512,2048]{1,0:T(8,128)(2,1)} %get-tuple-element.7) | copy-start | bytes 6291460
  40.3 5.1 %copy-start.9 = (bf16[2048,256]{1,0:T(8,128)(2,1)S(1)}, bf16[2048,256]{1,0:T(8,128)(2,1)}, u32[]{:S(2)}) copy-start(bf16[2048,256]{1,0:T(8,128)(2,1)} %param.13) | copy-start | bytes 3145732
  45.4 1.4 %copy-start.3 = (bf16[512,2048]{1,0:T(8,128)(2,1)}, bf16[512,2048]{1,0:T(8,128)(2,1)S(1)}, u32[]{:S(2)}) copy-start(bf16[512,2048]{1,0:T(8,128)(2,1)S(1)} %fusion.10) | copy-start | bytes 6291460
  45.4 3.3 %copy-start.10 = (s32[1,64]{1,0:T(1,128)S(1)}, s32[1,64]{1,0:T(1,128)}, u32[]{:S(2)}) copy-start(s32[1,64]{1,0:T(1,128)} %param.17) | copy-start | bytes 772
  48.8 1.0 copy-start.2
  55.7 5.6 %copy-start.5 = (bf16[2048,256]{1,0:T(8,128)(2,1)S(1)}, bf16[2048,256]{1,0:T(8,128)(2,1)}, u32[]{:S(2)}) copy-start(bf16[2048,256]{1,0:T(8,128)(2,1)} %fusion.20) | copy-start | bytes 3145732
  71.8 7.2 %copy-start.8 = (bf16[512,2048]{1,0:T(8,128)(2,1)S(1)}, bf16[512,2048]{1,0:T(8,128)(2,1)}, u32[]{:S(2)}) copy-start(bf16[512,2048]{1,0:T(8,128)(2,1)} %param.14) | copy-start | bytes 6291460
  79.0 3.7 %copy-start.11 = (s32[1,64]{1,0:T(1,128)S(1)}, s32[1,64]{1,0:T(1,128)}, u32[]{:S(2)}) copy-start(s32[1,64]{1,0:T(1,128)} %param.18) | copy-start | bytes 772
  81.7 35.4 %copy-start.4 = (bf16[512,512]{1,0:T(8,128)(2,1)S(1)}, bf16[512,512]{1,0:T(8,128)(2,1)}, u32[]{:S(2)}) copy-start(bf16[512,512]{1,0:T(8,128)(2,1)} %tok_ref.1) | copy-start | bytes 1572868
  115.1 3.0 %copy-start.6 = (bf16[8,8,8,256]{3,2,1,0:T(8,128)(2,1)S(1)}, bf16[8,8,8,256]{3,2,1,0:T(8,128)(2,1)}, u32[]{:S(2)}) copy-start(bf16[8,8,8,256]{3,2,1,0:T(8,128)(2,1)} %get-tuple-element.9) | copy-start | bytes 786436

commit v5 on v4

--- a/solution.py
+++ b/solution.py
@@ -288,6 +288,49 @@
         compiler_params=pltpu.CompilerParams(collective_id=1, has_side_effects=True),
     )(partial, share4)
     return rs, new.reshape(share.shape)
+
+
+def _attend_kernel(scale, lens_ref, q_ref, k_ref, v_ref, o_ref):
+    chunk = q_ref.shape[0]
+    capacity = k_ref.shape[0]
+    held = lens_ref[0]
+    first = pl.program_id(1) * chunk
+    scores = lax.dot_general(
+        q_ref[...], k_ref[...], (((1,), (1,)), ((), ())), preferred_element_type=jnp.float32
+    ) * scale
+    row_pos = first + lax.broadcasted_iota(jnp.int32, (chunk, capacity), 0)
+    key_pos = lax.broadcasted_iota(jnp.int32, (chunk, capacity), 1)
+    scores = jnp.where(key_pos <= held + row_pos, scores, MASKED)
+    top = jnp.max(scores, axis=1, keepdims=True)
+    weights = jnp.exp(scores - top)
+    probs = (weights / jnp.sum(weights, axis=1, keepdims=True)).astype(jnp.bfloat16)
+    o_ref[...] = jnp.dot(probs, v_ref[...], preferred_element_type=jnp.float32).astype(o_ref.dtype)
+
+
+def attend(query, fresh, held_len, head_size, chunk=128):
+    rows, qcols = query.shape
+    capacity = fresh.shape[0]
+    heads = qcols // head_size
+    lens = jnp.reshape(held_len, (1,)).astype(jnp.int32)
+    return pl.pallas_call(
+        functools.partial(_attend_kernel, head_size ** (-0.5)),
+        out_shape=jax.ShapeDtypeStruct((rows, qcols), jnp.bfloat16),
+        grid_spec=pltpu.PrefetchScalarGridSpec(
+            num_scalar_prefetch=1,
+            grid=(heads, rows // chunk),
+            in_specs=[
+                pl.BlockSpec((chunk, head_size), lambda h, r, lens: (r, h)),
+                pl.BlockSpec((capacity, head_size), lambda h, r, lens: (0, 0)),
+                pl.BlockSpec((capacity, head_size), lambda h, r, lens: (0, 1)),
+            ],
+            out_specs=pl.BlockSpec((chunk, head_size), lambda h, r, lens: (r, h)),
+        ),
+        cost_estimate=pl.CostEstimate(
+            flops=4 * rows * capacity * qcols,
+            transcendentals=rows * capacity * heads,
+            bytes_accessed=2 * (2 * rows * qcols + 2 * capacity * head_size),
+        ),
+    )(lens, query, fresh, fresh)
 
 
 def body(
@@ -343,24 +386,8 @@
     sources = jnp.sum(jnp.where(matches, block_ids, 0), axis=1)
     sorted_share = jnp.take(fresh_share, sources, axis=0)
     head_size = width // 2
-    keys = fresh[:, :head_size]
-    values = fresh[:, head_size:]
-    local_heads = query.shape[1] // head_size
-    query3 = query.reshape(tok_rows, local_heads, head_size)
-    scores = jnp.einsum(
-        "thd,kd->htk", query3, keys, preferred_element_type=jnp.float32
-    ) * head_size ** (-0.5)
+    context = attend(query, fresh, held_len, head_size)
     row_pos = lax.broadcasted_iota(jnp.int32, (tok_rows, 1), 0)
-    key_pos = lax.broadcasted_iota(jnp.int32, (1, capacity), 1)
-    allowed = key_pos <= held_len + row_pos
-    scores = jnp.where(allowed[None], scores, MASKED)
-    top = jnp.max(scores, axis=2, keepdims=True)
-    weights = jnp.exp(scores - top)
-    probs = (weights / jnp.sum(weights, axis=2, keepdims=True)).astype(jnp.bfloat16)
-    context = jnp.einsum("htk,kd->thd", probs, values, preferred_element_type=jnp.float32).astype(
-        jnp.bfloat16
-    )
-    context = context.reshape(tok_rows, local_heads * head_size)
     out_blocks = w_out.reshape(w_out.shape[0], tp_count, tok_cols)
     partial_out = jnp.einsum(
         "tk,kpn->ptn", context, out_blocks, preferred_element_type=jnp.float32

time: 119 us -> 116 us (0.975); the launches traced: 119 us -> 114 us
  matrix products: 24.8 us -> 8.76 us
  Pallas kernels: 68.8 us -> 83.8 us
  other arithmetic: 14.7 us -> 11.3 us
    pallas_call x0 -> x1, Pallas kernels: none -> 16.3 us  [attend(): pl.pallas_call(functools.partial(_attend_kernel, head_size ** (-0.5)), ou...]
    sub x1 -> x0, matrix products: 10.5 us -> none  [body(): weights = jnp.exp(scores - top)]
    dot_general x1 -> x0, matrix products: 7.19 us -> none  [body(): jnp.einsum('htk,kd->thd', probs, values, preferred_element_type=jnp.float32)]
    le x1 -> x0, other arithmetic: 1.86 us -> none  [body(): allowed = key_pos <= held_len + row_pos]
    dot_general x1, matrix products: 2.63 us -> 4.39 us  [body(): jnp.einsum('tk,kpn->ptn', context, out_blocks, preferred_element_type=jnp...]
    dot_general x1, matrix products: 3.77 us -> 2.07 us  [body(): jnp.dot(normed, w_query, preferred_element_type=jnp.float32)]
    reduce_sum x1, other arithmetic: 2.27 us -> 0.68 us  [normalize(): spread = jnp.mean(centred * centred, axis=1, keepdims=True)]
    dot_general x1, matrix products: 0.72 us -> 2.3 us  [body(): jnp.dot(normed, w_keyval, preferred_element_type=jnp.float32)]
where the time goes in v5:
time: 116 us; the launch traced here: 114 us
  Pallas kernels  83.8 us (72%)
  other arithmetic  11.3 us (10%)
  matrix products  8.76 us (8%)
  local copies, waits for them, and re-layouts  7.51 us (6%)
  between operations  2.34 us (2%)
    pallas_call x1, Pallas kernels, gather_inputs(): pl.pallas_call(functools.partial(_in_kernel, na, nb, ntp), out_shape=(jax...  38.1 us
    pallas_call x1, Pallas kernels, scatter_outputs(): pl.pallas_call(functools.partial(_out_kernel, na, nb, ntp), out_shape=(ja...  29.4 us
    pallas_call x1, Pallas kernels, attend(): pl.pallas_call(functools.partial(_attend_kernel, head_size ** (-0.5)), ou...  16.3 us
    dot_general x1, matrix products, body(): jnp.einsum('tk,kpn->ptn', context, out_blocks, preferred_element_type=jnp...  4.39 us
    select_n x1, other arithmetic, body(): jnp.where(positions < held_len, cached, jnp.where(positions < held_len +...  3.81 us

profile of v5, /device:TPU:1, one launch (start us, length us, event | category | flops | bytes accessed | tf_op | source)
XLA Modules:
  0.0 113.8 jit_solution(3846452658771668942)
XLA Ops:
  0.6 0.0 copy-start
  1.4 38.1 %shard_map.113 = (bf16[512,2048]{1,0:T(8,128)(2,1)}, bf16[8,8,4,8,256]{4,3,2,1,0:T(8,128)(2,1)}) custom-call(bf16[512,512]{1,0:T(8,128)(2,1)} %tok_ref.1, bf16[8,8,8,256]{3,2,1,0:T(8,128)(2,1)} %bitcast.47), custom_call_target="tpu_custom_call" | custom-call | tf_op jit(solution)/shard_map/pallas_call | solution.py:198
  39.6 0.0 copy-start.1
  39.6 0.0 copy-start.6
  39.6 2.1 %convert_reduce_fusion = f32[512]{0:T(512)S(1)} fusion(bf16[512,2048]{1,0:T(8,128)(2,1)} %get-tuple-element.6), kind=kLoop, calls=%fused_computation.3 | loop fusion | flops 2096640 | bytes 2099200 | tf_op jit(solution)/shard_map/reduce_sum | solution.py:16
  41.7 0.1 copy-done.1
  41.8 0.7 fusion.2
  42.5 0.0 copy-done.6
  42.5 0.7 fusion.4
  43.2 0.0 copy-done
  43.2 0.0 copy-start.3
  43.2 0.0 copy-start.7
  43.3 2.1 %convolution_convert_fusion.q_ref = bf16[512,512]{1,0:T(8,128)(2,1)} fusion(bf16[512,2048]{1,0:T(8,128)(2,1)S(1)} %fusion.4, bf16[2048,512]{1,0:T(8,128)(2,1)S(1)} %copy-done), kind=kOutput, calls=%fused_computation.14 | convolution fusion | flops 1074003968 | bytes 4718592 | tf_op jit(solution)/shard_map/dot_general | solution.py:366
  45.3 0.0 copy-done.3
  46.0 0.0 copy-done.7
  46.0 0.0 copy-start.8
  46.0 2.3 %fusion.10 = bf16[512,256]{1,0:T(8,128)(2,1)S(1)} fusion(bf16[512,2048]{1,0:T(8,128)(2,1)} %copy-done.3, bf16[2048,256]{1,0:T(8,128)(2,1)S(1)} %copy-done.7, pred[512]{0:T(512)(128)(4,1)S(1)} %compare_reduce_fusion), kind=kOutput, calls=%fused_computation.16 | convolution fusion | flops 537133056 | bytes 3408384 | tf_op jit(solution)/shard_map/dot_general | solution.py:367
  48.4 0.1 broadcast.103
  48.4 1.9 %select_n.79 = bf16[2048,256]{1,0:T(8,128)(2,1)S(1)} dynamic-update-slice(bf16[2048,256]{1,0:T(8,128)(2,1)S(1)} %broadcast.103, bf16[512,256]{1,0:T(8,128)(2,1)S(1)} %fusion.10, s32[]{:T(128)S(6)} %select_n.74, s32[]{:T(128)} %constant.25.clone.1) | dynamic-update-slice | bytes 524292 | tf_op jit(solution)/shard_map/jit(_where)/select_n | solution.py:377
  50.3 0.0 copy-start.2
  50.3 0.0 copy-done.8
  50.4 1.0 copy-done.2
  51.3 1.8 %gather_fusion = bf16[64,4,8,256]{3,2,1,0:T(8,128)(2,1)S(1)} fusion(bf16[64,4,8,256]{3,2,1,0:T(8,128)(2,1)} %bitcast.45, s32[1024]{0:T(1024)S(1)} %pad_clamp_fusion.1), kind=kCustom, calls=%fused_computation | custom fusion | bytes 2097408 | tf_op jit(solution)/shard_map/jit(_take)/gather | solution.py:369
  53.2 0.1 broadcast_in_dim.57
  53.3 0.1 broadcast_in_dim.58
  53.5 3.8 %fusion.11.k_ref.v_ref = bf16[2048,256]{1,0:T(8,128)(2,1)} fusion(bf16[2048,256]{1,0:T(8,128)(2,1)} %copy-done.2, bf16[64,4,8,256]{3,2,1,0:T(8,128)(2,1)S(1)} %gather_fusion, pred[2048]{0:T(1024)(128)(4,1)S(1)} %broadcast_in_dim.58, pred[2048]{0:T(1024)(128)(4,1)S(1)} %iota_compare_fusion.1), kind=kLoop, calls=%fused_computation.18 | loop fusion | flops 1048576 | bytes 3149824 | tf_op jit(solution)/shard_map/jit(_where)/select_n | solution.py:374
  57.3 16.3 %shard_map.114 = bf16[512,512]{1,0:T(8,128)(2,1)} custom-call(s32[1]{0:T(128)} %copy.25.lens_ref, bf16[512,512]{1,0:T(8,128)(2,1)} %convolution_convert_fusion.q_ref, bf16[2048,256]{1,0:T(8,128)(2,1)} %fusion.11.k_ref.v_ref, bf16[2048,256]{1,0:T(8,128)(2,1)} %fusion.11.k_ref.v_ref), custom_call_target="tpu_custom_call" | custom-call | flops 2147483648 | bytes 2097152 | tf_op jit(solution)/shard_map/pallas_call | solution.py:315
  73.6 0.0 copy-start.9
  73.6 4.4 %convert_bitcast_fusion.part_ref = bf16[4,512,512]{2,1,0:T(8,128)(2,1)} fusion(bf16[64,4,8,512]{3,2,1,0:T(8,128)(2,1)} %bitcast.49, bf16[512,512]{1,0:T(8,128)(2,1)} %shard_map.114), kind=kOutput, calls=%fused_computation.13 | convolution fusion | flops 1074790400 | bytes 4718592 | tf_op jit(solution)/shard_map/tk,kpn->ptn/dot_general | solution.py:392
  78.0 1.0 constant_dynamic-slice_fusion
  78.9 0.0 copy-done.9
  78.9 0.1 select_reduce_fusion
  79.1 0.6 gather_fusion.1
  79.7 0.1 reduce_sum.43
  79.8 0.8 broadcast_select_fusion.share_ref
  80.6 29.4 %shard_map.115 = (bf16[4,512,512]{2,1,0:T(8,128)(2,1)}, bf16[8,8,8,256]{3,2,1,0:T(8,128)(2,1)}) custom-call(bf16[4,512,512]{2,1,0:T(8,128)(2,1)} %convert_bitcast_fusion.part_ref, bf16[8,8,8,256]{3,2,1,0:T(8,128)(2,1)} %broadcast_select_fusion.share_ref), custom_call_target="tpu_custom_call" | custom-call | tf_op jit(solution)/shard_map/pallas_call | solution.py:274
  110.0 0.0 copy-start.4
  110.0 0.0 copy-start.5
  110.0 2.1 %convert_reduce_fusion.1 = f32[512,512]{1,0:T(8,128)S(1)} fusion(bf16[4,512,512]{2,1,0:T(8,128)(2,1)} %get-tuple-element.8), kind=kLoop, calls=%fused_computation.9 | loop fusion | flops 1835008 | bytes 3145728 | tf_op jit(solution)/shard_map/reduce_sum | solution.py:397
  112.1 0.0 copy-done.4
  112.1 0.9 select_convert_fusion
  113.1 0.0 copy-done.5
  113.1 0.7 copy.26
  (11 shorter events, 0.1 us)
Async XLA Ops:
  0.6 42.6 %copy-start = (bf16[2048,512]{1,0:T(8,128)(2,1)S(1)}, bf16[2048,512]{1,0:T(8,128)(2,1)}, u32[]{:S(2)}) copy-start(bf16[2048,512]{1,0:T(8,128)(2,1)} %param.12) | copy-start | bytes 6291460
  39.6 2.2 %copy-start.1 = (bf16[512,2048]{1,0:T(8,128)(2,1)S(1)}, bf16[512,2048]{1,0:T(8,128)(2,1)}, u32[]{:S(2)}) copy-start(bf16[512,2048]{1,0:T(8,128)(2,1)} %get-tuple-element.6) | copy-start | bytes 6291460
  39.6 2.9 %copy-start.6 = (f32[2048]{0:T(1024)S(1)}, f32[2048]{0:T(1024)}, u32[]{:S(2)}) copy-start(f32[2048]{0:T(1024)} %param.11) | copy-start | bytes 24580
  43.2 2.1 %copy-start.3 = (bf16[512,2048]{1,0:T(8,128)(2,1)}, bf16[512,2048]{1,0:T(8,128)(2,1)S(1)}, u32[]{:S(2)}) copy-start(bf16[512,2048]{1,0:T(8,128)(2,1)S(1)} %fusion.4) | copy-start | bytes 6291460
  43.2 2.8 %copy-start.7 = (bf16[2048,256]{1,0:T(8,128)(2,1)S(1)}, bf16[2048,256]{1,0:T(8,128)(2,1)}, u32[]{:S(2)}) copy-start(bf16[2048,256]{1,0:T(8,128)(2,1)} %param.13) | copy-start | bytes 3145732
  46.0 4.3 %copy-start.8 = (s32[1,64]{1,0:T(1,128)S(1)}, s32[1,64]{1,0:T(1,128)}, u32[]{:S(2)}) copy-start(s32[1,64]{1,0:T(1,128)} %param.17) | copy-start | bytes 772
  50.3 1.0 copy-start.2
  73.6 5.4 %copy-start.9 = (s32[1,64]{1,0:T(1,128)S(1)}, s32[1,64]{1,0:T(1,128)}, u32[]{:S(2)}) copy-start(s32[1,64]{1,0:T(1,128)} %param.18) | copy-start | bytes 772
  110.0 2.1 %copy-start.4 = (bf16[512,512]{1,0:T(8,128)(2,1)S(1)}, bf16[512,512]{1,0:T(8,128)(2,1)}, u32[]{:S(2)}) copy-start(bf16[512,512]{1,0:T(8,128)(2,1)} %tok_ref.1) | copy-start | bytes 1572868
  110.0 3.0 %copy-start.5 = (bf16[8,8,8,256]{3,2,1,0:T(8,128)(2,1)S(1)}, bf16[8,8,8,256]{3,2,1,0:T(8,128)(2,1)}, u32[]{:S(2)}) copy-start(bf16[8,8,8,256]{3,2,1,0:T(8,128)(2,1)} %get-tuple-element.9) | copy-start | bytes 786436

commit v6 on v5

--- a/solution.py
+++ b/solution.py
@@ -28,7 +28,7 @@
     )
 
 
-def _greet(na, nb, s, t, left, right):
+def _greet(na, nb, s, t, *tp_peers):
     barrier = pltpu.get_barrier_semaphore()
     a = s // nb
     b = s % nb
@@ -45,9 +45,9 @@
 
     lax.fori_loop(1, nb, one_b, 0)
     lax.fori_loop(1, na, one_a, 0)
-    for p in (left, right):
+    for p in tp_peers:
         pl.semaphore_signal(barrier, inc=1, device_id={"seq": s, "tp": p}, device_id_type=MESH)
-    pl.semaphore_wait(barrier, na + nb)
+    pl.semaphore_wait(barrier, na + nb - 2 + len(tp_peers))
 
 
 class SeqAllToAll:
@@ -333,6 +333,112 @@
     )(lens, query, fresh, fresh)
 
 
+def _tail_kernel(na, nb, ntp, scale, chunk, lens_ref, q_ref, kt_ref, v_ref, w_ref, share_ref,
+                 rs_out, new_out, ctx, part, psend, precv, plocal, stage, s1send, s1recv, s2send,
+                 s2recv, slocal):
+    s = lax.axis_index("seq")
+    t = lax.axis_index("tp")
+    rows, qcols = q_ref.shape
+    head_size, capacity = kt_ref.shape
+    heads = qcols // head_size
+    cols = w_ref.shape[1] // ntp
+    chunks = rows // chunk
+    _greet(na, nb, s, t, *[lax.rem(t + k, ntp) for k in range(1, ntp)])
+    a2a = SeqAllToAll(na, nb, s, t, share_ref, stage, lambda a_src: new_out.at[a_src],
+                      (s1send, s1recv, s2send, s2recv, slocal))
+    a2a.first()
+    held = lens_ref[0]
+
+    def slice_out(c, k):
+        peer = lax.rem(t + k, ntp)
+        return _remote(part.at[c, :, pl.ds(pl.multiple_of(peer * cols, cols), cols)],
+                       rs_out.at[t, pl.ds(pl.multiple_of(c * chunk, chunk), chunk)],
+                       psend.at[c, k], precv.at[c, k], {"seq": s, "tp": peer})
+
+    def slice_in(c, k):
+        sender = lax.rem(t + ntp - k, ntp)
+        return _remote(part.at[c, :, pl.ds(0, cols)],
+                       rs_out.at[sender, pl.ds(pl.multiple_of(c * chunk, chunk), chunk)],
+                       psend.at[c, k], precv.at[c, k], {"seq": s, "tp": sender})
+
+    def slice_own(c):
+        return pltpu.make_async_copy(
+            part.at[c, :, pl.ds(pl.multiple_of(t * cols, cols), cols)],
+            rs_out.at[t, pl.ds(pl.multiple_of(c * chunk, chunk), chunk)], plocal.at[c])
+
+    def do_chunk(c):
+        first = pl.multiple_of(c * chunk, chunk)
+        row_pos = first + lax.broadcasted_iota(jnp.int32, (chunk, capacity), 0)
+        key_pos = lax.broadcasted_iota(jnp.int32, (chunk, capacity), 1)
+        allowed = key_pos <= held + row_pos
+        for h in range(heads):
+            q = q_ref[pl.ds(first, chunk), pl.ds(h * head_size, head_size)]
+            scores = jnp.dot(q, kt_ref[...], preferred_element_type=jnp.float32) * scale
+            scores = jnp.where(allowed, scores, MASKED)
+            top = jnp.max(scores, axis=1, keepdims=True)
+            weights = jnp.exp(scores - top)
+            inv = 1.0 / jnp.sum(weights, axis=1, keepdims=True)
+            probs = (weights * inv).astype(jnp.bfloat16)
+            ctx[:, pl.ds(h * head_size, head_size)] = jnp.dot(
+                probs, v_ref[...], preferred_element_type=jnp.float32).astype(ctx.dtype)
+        part[c] = jnp.dot(ctx[...], w_ref[...], preferred_element_type=jnp.float32).astype(
+            part.dtype)
+        slice_own(c).start()
+        for k in range(1, ntp):
+            slice_out(c, k).start()
+
+    do_chunk(0)
+    a2a.second()
+
+    def rest(c, carry):
+        do_chunk(c)
+        return carry
+
+    lax.fori_loop(1, chunks, rest, 0)
+    a2a.arrived()
+
+    def drain(c, carry):
+        for k in range(1, ntp):
+            slice_in(c, k).wait_recv()
+            slice_out(c, k).wait_send()
+        slice_own(c).wait()
+        return carry
+
+    lax.fori_loop(0, chunks, drain, 0)
+    a2a.finish()
+
+
+def attend_and_scatter(query, fresh, held_len, w_out, share, na, nb, ntp, head_size, chunk=128):
+    rows, qcols = query.shape
+    capacity = fresh.shape[0]
+    cols = w_out.shape[1] // ntp
+    _, block, width = share.shape
+    share4 = share.reshape(na, nb, block, width)
+    keys_t = fresh[:, :head_size].T
+    values = fresh[:, head_size:]
+    lens = jnp.reshape(held_len, (1,)).astype(jnp.int32)
+    vmem = pl.BlockSpec(memory_space=pltpu.VMEM)
+    rs, new = pl.pallas_call(
+        functools.partial(_tail_kernel, na, nb, ntp, head_size ** (-0.5), chunk),
+        out_shape=(
+            jax.ShapeDtypeStruct((ntp, rows, cols), jnp.bfloat16),
+            jax.ShapeDtypeStruct(share4.shape, share.dtype),
+        ),
+        in_specs=[pl.BlockSpec(memory_space=pltpu.SMEM), vmem, vmem, vmem, vmem,
+                  pl.BlockSpec(memory_space=pl.ANY)],
+        out_specs=(pl.BlockSpec(memory_space=pl.ANY), pl.BlockSpec(memory_space=pl.ANY)),
+        scratch_shapes=[
+            pltpu.VMEM((chunk, qcols), jnp.bfloat16),
+            pltpu.VMEM((rows // chunk, chunk, w_out.shape[1]), jnp.bfloat16),
+            pltpu.SemaphoreType.DMA((rows // chunk, ntp)),
+            pltpu.SemaphoreType.DMA((rows // chunk, ntp)),
+            pltpu.SemaphoreType.DMA((rows // chunk,)),
+        ] + _seq_scratch(na, nb, block, width, share.dtype),
+        compiler_params=pltpu.CompilerParams(collective_id=1, has_side_effects=True),
+    )(lens, query, keys_t, values, w_out, share4)
+    return rs, new.reshape(share.shape)
+
+
 def body(
     tokens,
     norm_gain,
@@ -386,13 +492,10 @@
     sources = jnp.sum(jnp.where(matches, block_ids, 0), axis=1)
     sorted_share = jnp.take(fresh_share, sources, axis=0)
     head_size = width // 2
-    context = attend(query, fresh, held_len, head_size)
+    summed, new_cache = attend_and_scatter(
+        query, fresh, held_len, w_out, sorted_share, outer, inner, tp_count, head_size
+    )
     row_pos = lax.broadcasted_iota(jnp.int32, (tok_rows, 1), 0)
-    out_blocks = w_out.reshape(w_out.shape[0], tp_count, tok_cols)
-    partial_out = jnp.einsum(
-        "tk,kpn->ptn", context, out_blocks, preferred_element_type=jnp.float32
-    ).astype(jnp.bfloat16)
-    summed, new_cache = scatter_outputs(partial_out, sorted_share, outer, inner, tp_count)
     summed = summed.astype(jnp.float32)
     total = tokens.astype(jnp.float32) + jnp.sum(summed, axis=0)
     mixed = jnp.where(row_pos < span_len, total, jnp.zeros_like(total)).astype(jnp.bfloat16)

time: 116 us -> 104 us (0.90); the launches traced: 114 us -> 103 us
  Pallas kernels: 83.8 us -> 75.7 us
  matrix products: 8.76 us -> 4.37 us
  local copies, waits for them, and re-layouts: 7.51 us -> 10.1 us
    pallas_call x2 -> x1, Pallas kernels: 45.7 us -> 37.6 us  [attend_and_scatter(): pl.pallas_call(functools.partial(_tail_kernel, na, nb, ntp, head_size **...]
    dot_general x1 -> x0, matrix products: 4.39 us -> none  [body(): jnp.einsum('tk,kpn->ptn', context, out_blocks, preferred_element_type=jnp...]
    transpose x0 -> x1, local copies, waits for them, and re-layouts: none -> 2.06 us  [attend_and_scatter(): keys_t = fresh[:, :head_size].T]
    gather x1, local copies, waits for them, and re-layouts: 1.84 us -> 3.22 us  [body(): cached = jnp.take(cache_all, holders, axis=0).reshape(capacity, width)]
where the time goes in v6:
time: 104 us; the launch traced here: 103 us
  Pallas kernels  75.7 us (73%)
  other arithmetic  10.7 us (10%)
  local copies, waits for them, and re-layouts  10.1 us (10%)
  matrix products  4.37 us (4%)
  between operations  2.35 us (2%)
    pallas_call x1, Pallas kernels, gather_inputs(): pl.pallas_call(functools.partial(_in_kernel, na, nb, ntp), out_shape=(jax...  38.1 us
    pallas_call x1, Pallas kernels, attend_and_scatter(): pl.pallas_call(functools.partial(_tail_kernel, na, nb, ntp, head_size **...  37.6 us
    gather x1, local copies, waits for them, and re-layouts, body(): cached = jnp.take(cache_all, holders, axis=0).reshape(capacity, width)  3.22 us
    select_n x1, other arithmetic, body(): jnp.where(positions < held_len, cached, jnp.where(positions < held_len +...  3.15 us
    dot_general x1, matrix products, body(): jnp.dot(normed, w_keyval, preferred_element_type=jnp.float32)  2.3 us
    reduce_sum x1, other arithmetic, normalize(): average = jnp.mean(values, axis=1, keepdims=True)  2.09 us

profile of v6, /device:TPU:1, one launch (start us, length us, event | category | flops | bytes accessed | tf_op | source)
XLA Modules:
  0.0 103.2 jit_solution(6887927311894927275)
XLA Ops:
  0.6 0.0 copy-start
  1.4 38.1 %shard_map.113 = (bf16[512,2048]{1,0:T(8,128)(2,1)}, bf16[8,8,4,8,256]{4,3,2,1,0:T(8,128)(2,1)}) custom-call(bf16[512,512]{1,0:T(8,128)(2,1)} %tok_ref.1, bf16[8,8,8,256]{3,2,1,0:T(8,128)(2,1)} %bitcast.38), custom_call_target="tpu_custom_call" | custom-call | tf_op jit(solution)/shard_map/pallas_call | solution.py:198
  39.6 0.0 copy-start.1
  39.6 0.0 copy-start.6
  39.6 2.1 %convert_reduce_fusion = f32[512]{0:T(512)S(1)} fusion(bf16[512,2048]{1,0:T(8,128)(2,1)} %get-tuple-element.6), kind=kLoop, calls=%fused_computation.3 | loop fusion | flops 2096640 | bytes 2099200 | tf_op jit(solution)/shard_map/reduce_sum | solution.py:16
  41.7 0.1 copy-done.1
  41.8 0.7 fusion.2
  42.5 0.0 copy-done.6
  42.5 0.7 fusion.4
  43.2 0.0 copy-done
  43.2 0.0 copy-start.3
  43.2 0.0 copy-start.7
  43.3 2.1 %convolution_convert_fusion.q_ref = bf16[512,512]{1,0:T(8,128)(2,1)} fusion(bf16[512,2048]{1,0:T(8,128)(2,1)S(1)} %fusion.4, bf16[2048,512]{1,0:T(8,128)(2,1)S(1)} %copy-done), kind=kOutput, calls=%fused_computation.10 | convolution fusion | flops 1074003968 | bytes 4718592 | tf_op jit(solution)/shard_map/dot_general | solution.py:472
  45.3 0.0 copy-done.3
  46.0 0.0 copy-done.7
  46.0 0.0 copy-start.8
  46.0 2.3 %fusion.5 = bf16[512,256]{1,0:T(8,128)(2,1)S(1)} fusion(bf16[512,2048]{1,0:T(8,128)(2,1)} %copy-done.3, bf16[2048,256]{1,0:T(8,128)(2,1)S(1)} %copy-done.7, pred[512]{0:T(512)(128)(4,1)S(1)} %compare_reduce_fusion), kind=kOutput, calls=%fused_computation.12 | convolution fusion | flops 537133056 | bytes 3408384 | tf_op jit(solution)/shard_map/dot_general | solution.py:473
  48.4 0.1 broadcast.103
  48.4 1.9 %select_n.79 = bf16[2048,256]{1,0:T(8,128)(2,1)S(1)} dynamic-update-slice(bf16[2048,256]{1,0:T(8,128)(2,1)S(1)} %broadcast.103, bf16[512,256]{1,0:T(8,128)(2,1)S(1)} %fusion.5, s32[]{:T(128)S(6)} %select_n.74, s32[]{:T(128)} %constant.25.clone.1) | dynamic-update-slice | bytes 524292 | tf_op jit(solution)/shard_map/jit(_where)/select_n | solution.py:483
  50.3 0.0 copy-start.2
  50.3 0.0 copy-done.8
  50.4 3.2 %gather_fusion = bf16[64,4,8,256]{3,2,1,0:T(8,128)(2,1)} fusion(bf16[64,4,8,256]{3,2,1,0:T(8,128)(2,1)} %bitcast.36, s32[1024]{0:T(1024)S(1)} %pad_clamp_fusion.1), kind=kCustom, calls=%fused_computation | custom fusion | bytes 2097408 | tf_op jit(solution)/shard_map/jit(_take)/gather | solution.py:475
  53.6 0.1 broadcast_in_dim.57
  53.7 0.1 broadcast_in_dim.58
  53.9 0.0 copy-done.2
  53.9 3.2 %fusion.6 = bf16[2048,256]{1,0:T(8,128)(2,1)S(1)} fusion(bf16[2048,256]{1,0:T(8,128)(2,1)} %copy-done.2, bf16[64,4,8,256]{3,2,1,0:T(8,128)(2,1)} %gather_fusion, pred[2048]{0:T(1024)(128)(4,1)S(1)} %broadcast_in_dim.58, pred[2048]{0:T(1024)(128)(4,1)S(1)} %iota_compare_fusion.1), kind=kLoop, calls=%fused_computation.14 | loop fusion | flops 1048576 | bytes 3149824 | tf_op jit(solution)/shard_map/jit(_where)/select_n | solution.py:480
  57.0 0.0 copy-start.9
  57.1 1.0 %fusion.9 = (bf16[2048,128]{1,0:T(8,128)(2,1)}, bf16[128,2048]{0,1:T(8,128)(2,1)}) fusion(bf16[2048,256]{1,0:T(8,128)(2,1)S(1)} %fusion.6), kind=kLoop, calls=%fused_computation.36 | loop fusion | bytes 2097152 | tf_op jit(solution)/shard_map/slice | solution.py:418
  58.1 2.1 %copy.14.kt_ref = bf16[128,2048]{1,0:T(8,128)(2,1)} copy(bf16[128,2048]{0,1:T(8,128)(2,1)} %get-tuple-element.11) | data formatting | bytes 1048576 | tf_op jit(solution)/shard_map/transpose | solution.py:417
  60.2 0.0 copy-done.9
  60.2 0.1 select_reduce_fusion
  60.3 0.6 gather_fusion.1
  60.9 0.1 reduce_sum.43
  61.0 0.8 broadcast_select_fusion.share_ref
  61.9 37.6 %shard_map.114 = (bf16[4,512,512]{2,1,0:T(8,128)(2,1)}, bf16[8,8,8,256]{3,2,1,0:T(8,128)(2,1)}) custom-call(s32[1]{0:T(128)} %copy.18.lens_ref, bf16[512,512]{1,0:T(8,128)(2,1)} %convolution_convert_fusion.q_ref, bf16[128,2048]{1,0:T(8,128)(2,1)} %copy.14.kt_ref, bf16[2048,128]{1,0:T(8,128)(2,1)} %get-tuple-element.10.v_ref, bf16[512,2048]{1,0:T(8,128)(2,1)} %w_ref.1, ...), custom_call_target="tpu_custom_call" | custom-call | tf_op jit(solution)/shard_map/pallas_call | solution.py:421
  99.4 0.0 copy-start.4
  99.5 0.0 copy-start.5
  99.5 2.1 %convert_reduce_fusion.1 = f32[512,512]{1,0:T(8,128)S(1)} fusion(bf16[4,512,512]{2,1,0:T(8,128)(2,1)} %get-tuple-element.8), kind=kLoop, calls=%fused_computation.9 | loop fusion | flops 1835008 | bytes 3145728 | tf_op jit(solution)/shard_map/reduce_sum | solution.py:500
  101.5 0.0 copy-done.4
  101.6 0.9 select_convert_fusion
  102.5 0.0 copy-done.5
  102.5 0.7 copy.19
  (12 shorter events, 0.1 us)
Async XLA Ops:
  0.6 42.6 %copy-start = (bf16[2048,512]{1,0:T(8,128)(2,1)S(1)}, bf16[2048,512]{1,0:T(8,128)(2,1)}, u32[]{:S(2)}) copy-start(bf16[2048,512]{1,0:T(8,128)(2,1)} %param.12) | copy-start | bytes 6291460
  39.6 2.2 %copy-start.1 = (bf16[512,2048]{1,0:T(8,128)(2,1)S(1)}, bf16[512,2048]{1,0:T(8,128)(2,1)}, u32[]{:S(2)}) copy-start(bf16[512,2048]{1,0:T(8,128)(2,1)} %get-tuple-element.6) | copy-start | bytes 6291460
  39.6 2.9 %copy-start.6 = (f32[2048]{0:T(1024)S(1)}, f32[2048]{0:T(1024)}, u32[]{:S(2)}) copy-start(f32[2048]{0:T(1024)} %param.11) | copy-start | bytes 24580
  43.2 2.1 %copy-start.3 = (bf16[512,2048]{1,0:T(8,128)(2,1)}, bf16[512,2048]{1,0:T(8,128)(2,1)S(1)}, u32[]{:S(2)}) copy-start(bf16[512,2048]{1,0:T(8,128)(2,1)S(1)} %fusion.4) | copy-start | bytes 6291460
  43.2 2.8 %copy-start.7 = (bf16[2048,256]{1,0:T(8,128)(2,1)S(1)}, bf16[2048,256]{1,0:T(8,128)(2,1)}, u32[]{:S(2)}) copy-start(bf16[2048,256]{1,0:T(8,128)(2,1)} %param.13) | copy-start | bytes 3145732
  46.0 4.3 %copy-start.8 = (s32[1,64]{1,0:T(1,128)S(1)}, s32[1,64]{1,0:T(1,128)}, u32[]{:S(2)}) copy-start(s32[1,64]{1,0:T(1,128)} %param.17) | copy-start | bytes 772
  50.3 3.5 %copy-start.2 = (bf16[2048,256]{1,0:T(8,128)(2,1)}, bf16[2048,256]{1,0:T(8,128)(2,1)S(1)}, u32[]{:S(2)}) copy-start(bf16[2048,256]{1,0:T(8,128)(2,1)S(1)} %select_n.79) | copy-start | bytes 3145732
  57.0 3.1 %copy-start.9 = (s32[1,64]{1,0:T(1,128)S(1)}, s32[1,64]{1,0:T(1,128)}, u32[]{:S(2)}) copy-start(s32[1,64]{1,0:T(1,128)} %param.18) | copy-start | bytes 772
  99.4 2.1 %copy-start.4 = (bf16[512,512]{1,0:T(8,128)(2,1)S(1)}, bf16[512,512]{1,0:T(8,128)(2,1)}, u32[]{:S(2)}) copy-start(bf16[512,512]{1,0:T(8,128)(2,1)} %tok_ref.1) | copy-start | bytes 1572868
  99.5 3.0 %copy-start.5 = (bf16[8,8,8,256]{3,2,1,0:T(8,128)(2,1)S(1)}, bf16[8,8,8,256]{3,2,1,0:T(8,128)(2,1)}, u32[]{:S(2)}) copy-start(bf16[8,8,8,256]{3,2,1,0:T(8,128)(2,1)} %get-tuple-element.9) | copy-start | bytes 786436

commit v7 on v6

--- a/solution.py
+++ b/solution.py
@@ -333,21 +333,78 @@
     )(lens, query, fresh, fresh)
 
 
-def _tail_kernel(na, nb, ntp, scale, chunk, lens_ref, q_ref, kt_ref, v_ref, w_ref, share_ref,
+def _prep_kernel(ntp, lens_ref, holders_ref, sources_ref, cache_ref, kv_ref, fresh, kt, share_buf,
+                 fresh32):
+    t = lax.axis_index("tp")
+    capacity, width = fresh.shape
+    head_size = width // 2
+    block_rows = cache_ref.shape[1]
+    share = block_rows // ntp
+    held = lens_ref[0]
+    span = lens_ref[1]
+
+    def place(b, carry):
+        fresh32[pl.ds(pl.multiple_of(b * block_rows, block_rows), block_rows), :] = (
+            cache_ref[holders_ref[b]].astype(jnp.float32))
+        return carry
+
+    lax.fori_loop(0, capacity // block_rows, place, 0)
+    padded = jnp.concatenate(
+        [kv_ref[...].astype(jnp.float32),
+         jnp.zeros((capacity - kv_ref.shape[0], width), jnp.float32)], axis=0)
+    shifted = pltpu.roll(padded, held, 0)
+    positions = lax.broadcasted_iota(jnp.int32, (capacity, width), 0)
+    full = jnp.where(positions < held, fresh32[...],
+                     jnp.where(positions < held + span, shifted, 0.0))
+    fresh32[...] = full
+    fresh[...] = full.astype(fresh.dtype)
+    kt[...] = fresh[:, pl.ds(0, head_size)].T
+
+    def pick(d, carry):
+        start = pl.multiple_of(sources_ref[d] * block_rows + t * share, share)
+        share_buf[d] = fresh32[pl.ds(start, share), :].astype(share_buf.dtype)
+        return carry
+
+    lax.fori_loop(0, share_buf.shape[0], pick, 0)
+
+
+def prepare(cache, keyval, lens, holders, sources, ntp):
+    blocks, block_rows, width = cache.shape
+    capacity = blocks * block_rows
+    vmem = pl.BlockSpec(memory_space=pltpu.VMEM)
+    smem = pl.BlockSpec(memory_space=pltpu.SMEM)
+    return pl.pallas_call(
+        functools.partial(_prep_kernel, ntp),
+        out_shape=(
+            jax.ShapeDtypeStruct((capacity, width), cache.dtype),
+            jax.ShapeDtypeStruct((width // 2, capacity), cache.dtype),
+            jax.ShapeDtypeStruct((blocks, block_rows // ntp, width), cache.dtype),
+        ),
+        in_specs=[smem, smem, smem, vmem, vmem],
+        out_specs=(vmem, vmem, vmem),
+        scratch_shapes=[pltpu.VMEM((capacity, width), jnp.float32)],
+    )(lens, holders, sources, cache, keyval)
+
+
+def _tail_kernel(na, nb, ntp, scale, chunk, lens_ref, q_ref, fresh, kt, share_buf, w_ref,
                  rs_out, new_out, ctx, part, psend, precv, plocal, stage, s1send, s1recv, s2send,
                  s2recv, slocal):
     s = lax.axis_index("seq")
     t = lax.axis_index("tp")
     rows, qcols = q_ref.shape
-    head_size, capacity = kt_ref.shape
+    capacity, width = fresh.shape
+    head_size = width // 2
+    share = share_buf.shape[1]
     heads = qcols // head_size
     cols = w_ref.shape[1] // ntp
     chunks = rows // chunk
+    held = lens_ref[0]
+
     _greet(na, nb, s, t, *[lax.rem(t + k, ntp) for k in range(1, ntp)])
-    a2a = SeqAllToAll(na, nb, s, t, share_ref, stage, lambda a_src: new_out.at[a_src],
+    sorted4 = share_buf.reshape(na, nb, share, width)
+    a2a = SeqAllToAll(na, nb, s, t, sorted4, stage, lambda a_src: new_out.at[a_src],
                       (s1send, s1recv, s2send, s2recv, slocal))
     a2a.first()
-    held = lens_ref[0]
 
     def slice_out(c, k):
         peer = lax.rem(t + k, ntp)
@@ -373,14 +430,15 @@
         allowed = key_pos <= held + row_pos
         for h in range(heads):
             q = q_ref[pl.ds(first, chunk), pl.ds(h * head_size, head_size)]
-            scores = jnp.dot(q, kt_ref[...], preferred_element_type=jnp.float32) * scale
+            scores = jnp.dot(q, kt[...], preferred_element_type=jnp.float32) * scale
             scores = jnp.where(allowed, scores, MASKED)
             top = jnp.max(scores, axis=1, keepdims=True)
             weights = jnp.exp(scores - top)
             inv = 1.0 / jnp.sum(weights, axis=1, keepdims=True)
             probs = (weights * inv).astype(jnp.bfloat16)
             ctx[:, pl.ds(h * head_size, head_size)] = jnp.dot(
-                probs, v_ref[...], preferred_element_type=jnp.float32).astype(ctx.dtype)
+                probs, fresh[:, pl.ds(head_size, head_size)],
+                preferred_element_type=jnp.float32).astype(ctx.dtype)
         part[c] = jnp.dot(ctx[...], w_ref[...], preferred_element_type=jnp.float32).astype(
             part.dtype)
         slice_own(c).start()
@@ -408,24 +466,22 @@
     a2a.finish()
 
 
-def attend_and_scatter(query, fresh, held_len, w_out, share, na, nb, ntp, head_size, chunk=128):
+def attend_and_scatter(query, cache, keyval, lens, holders, sources, w_out, na, nb, ntp,
+                       chunk=128):
     rows, qcols = query.shape
-    capacity = fresh.shape[0]
+    blocks, block_rows, width = cache.shape
+    share = block_rows // ntp
     cols = w_out.shape[1] // ntp
-    _, block, width = share.shape
-    share4 = share.reshape(na, nb, block, width)
-    keys_t = fresh[:, :head_size].T
-    values = fresh[:, head_size:]
-    lens = jnp.reshape(held_len, (1,)).astype(jnp.int32)
+    fresh, keys_t, sorted_share = prepare(cache, keyval, lens, holders, sources, ntp)
     vmem = pl.BlockSpec(memory_space=pltpu.VMEM)
+    smem = pl.BlockSpec(memory_space=pltpu.SMEM)
     rs, new = pl.pallas_call(
-        functools.partial(_tail_kernel, na, nb, ntp, head_size ** (-0.5), chunk),
+        functools.partial(_tail_kernel, na, nb, ntp, (width // 2) ** (-0.5), chunk),
         out_shape=(
             jax.ShapeDtypeStruct((ntp, rows, cols), jnp.bfloat16),
-            jax.ShapeDtypeStruct(share4.shape, share.dtype),
+            jax.ShapeDtypeStruct((na, nb, share, width), cache.dtype),
         ),
-        in_specs=[pl.BlockSpec(memory_space=pltpu.SMEM), vmem, vmem, vmem, vmem,
-                  pl.BlockSpec(memory_space=pl.ANY)],
+        in_specs=[smem, vmem, vmem, vmem, vmem, vmem],
         out_specs=(pl.BlockSpec(memory_space=pl.ANY), pl.BlockSpec(memory_space=pl.ANY)),
         scratch_shapes=[
             pltpu.VMEM((chunk, qcols), jnp.bfloat16),
@@ -433,10 +489,10 @@
             pltpu.SemaphoreType.DMA((rows // chunk, ntp)),
             pltpu.SemaphoreType.DMA((rows // chunk, ntp)),
             pltpu.SemaphoreType.DMA((rows // chunk,)),
-        ] + _seq_scratch(na, nb, block, width, share.dtype),
+        ] + _seq_scratch(na, nb, share, width, cache.dtype),
         compiler_params=pltpu.CompilerParams(collective_id=1, has_side_effects=True),
-    )(lens, query, keys_t, values, w_out, share4)
-    return rs, new.reshape(share.shape)
+    )(lens, query, fresh, keys_t, sorted_share, w_out)
+    return rs, new.reshape(blocks, share, width)
 
 
 def body(
@@ -472,28 +528,15 @@
     query = jnp.dot(normed, w_query, preferred_element_type=jnp.float32).astype(jnp.bfloat16)
     keyval = jnp.dot(normed, w_keyval, preferred_element_type=jnp.float32).astype(jnp.bfloat16)
 
-    cached = jnp.take(cache_all, holders, axis=0).reshape(capacity, width)
-    shifted = lax.dynamic_update_slice(
-        jnp.zeros((capacity, width), jnp.bfloat16), keyval, (held_len, jnp.int32(0))
-    )
-    positions = lax.broadcasted_iota(jnp.int32, (capacity, 1), 0)
-    fresh = jnp.where(
-        positions < held_len,
-        cached,
-        jnp.where(positions < held_len + span_len, shifted, jnp.zeros_like(shifted)),
-    )
-    fresh_share = lax.dynamic_slice_in_dim(
-        fresh.reshape(groups, block_rows, width), tp_index * share, share, 1
-    )
     targets = new_table[0]
     device_ids = lax.broadcasted_iota(jnp.int32, (groups, groups), 0)
     block_ids = lax.broadcasted_iota(jnp.int32, (groups, groups), 1)
     matches = targets[None, :] == device_ids
     sources = jnp.sum(jnp.where(matches, block_ids, 0), axis=1)
-    sorted_share = jnp.take(fresh_share, sources, axis=0)
-    head_size = width // 2
+    lens = jnp.stack([held_len, span_len]).astype(jnp.int32)
     summed, new_cache = attend_and_scatter(
-        query, fresh, held_len, w_out, sorted_share, outer, inner, tp_count, head_size
+        query, cache_all.reshape(groups, block_rows, width), keyval, lens, holders, sources,
+        w_out, outer, inner, tp_count
     )
     row_pos = lax.broadcasted_iota(jnp.int32, (tok_rows, 1), 0)
     summed = summed.astype(jnp.float32)

time: 104 us -> 97.6 us (0.938)
  local copies, waits for them, and re-layouts: 10.1 us -> 2.19 us
  Pallas kernels: 75.7 us -> 80.4 us
  other arithmetic: 10.7 us -> 7.77 us
    pallas_call x1 -> x2, Pallas kernels: 37.6 us -> 42.2 us  [the longest x1 37.7 us: attend_and_scatter(): pl.pallas_call(functools.partial(_tail_kernel, na, nb, ntp, (width // 2)...]
    select_n x5 -> x0, other arithmetic: 4.04 us -> none  [the longest x1 3.15 us: body(): jnp.where(positions < held_len, cached, jnp.where(positions < held_len +...]
    gather x2 -> x0, local copies, waits for them, and re-layouts: 3.82 us -> none  [the longest x1 3.22 us: body(): cached = jnp.take(cache_all, holders, axis=0).reshape(capacity, width)]
    transpose x1 -> x0, local copies, waits for them, and re-layouts: 2.06 us -> none  [attend_and_scatter(): keys_t = fresh[:, :head_size].T]
    select_n x1 -> x0, local copies, waits for them, and re-layouts: 1.89 us -> none  [body(): jnp.where(positions < held_len + span_len, shifted, jnp.zeros_like(shifted))]
    dot_general x1, matrix products: 2.07 us -> 3.63 us  [body(): jnp.dot(normed, w_query, preferred_element_type=jnp.float32)]
    unnamed x21 -> x17, local copies, waits for them, and re-layouts: 0.86 us -> 2.19 us
where the time goes in v7:
time: 97.6 us; the launch traced here: 97.4 us
  Pallas kernels  80.4 us (82%)
  other arithmetic  7.77 us (8%)
  matrix products  5.04 us (5%)
  local copies, waits for them, and re-layouts  2.19 us (2%)
  between operations  2.04 us (2%)
    pallas_call x1, Pallas kernels, gather_inputs(): pl.pallas_call(functools.partial(_in_kernel, na, nb, ntp), out_shape=(jax...  38.1 us
    pallas_call x1, Pallas kernels, attend_and_scatter(): pl.pallas_call(functools.partial(_tail_kernel, na, nb, ntp, (width // 2)...  37.7 us
    pallas_call x1, Pallas kernels, prepare(): pl.pallas_call(functools.partial(_prep_kernel, ntp), out_shape=(jax.Shape...  4.53 us
    dot_general x1, matrix products, body(): jnp.dot(normed, w_query, preferred_element_type=jnp.float32)  3.63 us
    unnamed x17, local copies, waits for them, and re-layouts  2.19 us
    reduce_sum x1, other arithmetic, normalize(): average = jnp.mean(values, axis=1, keepdims=True)  2.09 us
    reduce_sum x1, other arithmetic, body(): total = tokens.astype(jnp.float32) + jnp.sum(summed, axis=0)  2.07 us

profile of v7, /device:TPU:1, one launch (start us, length us, event | category | flops | bytes accessed | tf_op | source)
XLA Modules:
  0.0 97.4 jit_solution(14428773170214636616)
XLA Ops:
  0.6 0.0 copy-start
  0.6 38.1 %shard_map.113 = (bf16[512,2048]{1,0:T(8,128)(2,1)}, bf16[8,8,4,8,256]{4,3,2,1,0:T(8,128)(2,1)}) custom-call(bf16[512,512]{1,0:T(8,128)(2,1)} %tok_ref.1, bf16[8,8,8,256]{3,2,1,0:T(8,128)(2,1)} %bitcast.12), custom_call_target="tpu_custom_call" | custom-call | tf_op jit(solution)/shard_map/pallas_call | solution.py:198
  38.8 0.0 copy-start.1
  38.8 0.0 copy-start.5
  38.8 2.1 %convert_reduce_fusion = f32[512]{0:T(512)S(1)} fusion(bf16[512,2048]{1,0:T(8,128)(2,1)} %get-tuple-element.9), kind=kLoop, calls=%fused_computation.1 | loop fusion | flops 2096640 | bytes 2099200 | tf_op jit(solution)/shard_map/reduce_sum | solution.py:16
  40.9 0.1 copy-done.1
  41.0 0.7 fusion.2
  41.7 0.0 copy-done.5
  41.7 0.0 copy-start.6
  41.7 0.7 fusion.4
  42.4 0.0 copy-start.2
  42.4 1.3 %copy-done.2 = bf16[512,2048]{1,0:T(8,128)(2,1)} copy-done((bf16[512,2048]{1,0:T(8,128)(2,1)}, bf16[512,2048]{1,0:T(8,128)(2,1)S(1)}, u32[]{:S(2)}) %copy-start.2) | copy-done | bytes 2097176
  43.8 0.0 copy-done.6
  43.8 0.0 copy-start.7
  43.8 1.4 %convolution_convert_fusion.1.kv_ref = bf16[512,256]{1,0:T(8,128)(2,1)} fusion(bf16[512,2048]{1,0:T(8,128)(2,1)S(1)} %fusion.4, bf16[2048,256]{1,0:T(8,128)(2,1)S(1)} %copy-done.6), kind=kOutput, calls=%fused_computation.9 | convolution fusion | flops 537001984 | bytes 3407872 | tf_op jit(solution)/shard_map/dot_general | solution.py:529
  46.5 0.6 pad_add_fusion.lens_ref
  47.2 0.0 copy-done.7
  47.2 0.6 select_reduce_fusion.sources_ref
  47.8 4.5 %shard_map.114 = (bf16[2048,256]{1,0:T(8,128)(2,1)}, bf16[128,2048]{1,0:T(8,128)(2,1)}, bf16[64,8,256]{2,1,0:T(8,128)(2,1)}) custom-call(s32[2]{0:T(128)} %pad_add_fusion.lens_ref, s32[64]{0:T(128)} %bitcast.14, s32[64]{0:T(128)} %select_reduce_fusion.sources_ref, bf16[64,32,256]{2,1,0:T(8,128)(2,1)} %bitcast.11, ...), custom_call_target="tpu_custom_call" | custom-call | tf_op jit(solution)/shard_map/pallas_call | solution.py:376
  52.3 0.0 copy-done
  52.3 3.6 %convolution_convert_fusion.q_ref = bf16[512,512]{1,0:T(8,128)(2,1)} fusion(bf16[512,2048]{1,0:T(8,128)(2,1)} %copy-done.2, bf16[2048,512]{1,0:T(8,128)(2,1)S(1)} %copy-done), kind=kOutput, calls=%fused_computation.8 | convolution fusion | flops 1074003968 | bytes 4718592 | tf_op jit(solution)/shard_map/dot_general | solution.py:528
  55.9 37.7 %shard_map.115 = (bf16[4,512,512]{2,1,0:T(8,128)(2,1)}, bf16[8,8,8,256]{3,2,1,0:T(8,128)(2,1)}) custom-call(s32[2]{0:T(128)} %pad_add_fusion.lens_ref, bf16[512,512]{1,0:T(8,128)(2,1)} %convolution_convert_fusion.q_ref, bf16[2048,256]{1,0:T(8,128)(2,1)} %get-tuple-element.11.fresh, bf16[128,2048]{1,0:T(8,128)(2,1)} %get-tuple-element.12.kt, ...), custom_call_target="tpu_custom_call" | custom-call | tf_op jit(solution)/shard_map/pallas_call | solution.py:478
  93.7 0.0 copy-start.3
  93.7 0.0 copy-start.4
  93.7 2.1 %convert_reduce_fusion.1 = f32[512,512]{1,0:T(8,128)S(1)} fusion(bf16[4,512,512]{2,1,0:T(8,128)(2,1)} %get-tuple-element.14), kind=kLoop, calls=%fused_computation.7 | loop fusion | flops 1835008 | bytes 3145728 | tf_op jit(solution)/shard_map/reduce_sum | solution.py:543
  95.8 0.0 copy-done.3
  95.8 0.9 select_convert_fusion
  96.7 0.0 copy-done.4
  96.7 0.7 copy.15
  (3 shorter events, 0.0 us)
Async XLA Ops:
  0.6 51.7 %copy-start = (bf16[2048,512]{1,0:T(8,128)(2,1)S(1)}, bf16[2048,512]{1,0:T(8,128)(2,1)}, u32[]{:S(2)}) copy-start(bf16[2048,512]{1,0:T(8,128)(2,1)} %param.12) | copy-start | bytes 6291460
  38.8 2.2 %copy-start.1 = (bf16[512,2048]{1,0:T(8,128)(2,1)S(1)}, bf16[512,2048]{1,0:T(8,128)(2,1)}, u32[]{:S(2)}) copy-start(bf16[512,2048]{1,0:T(8,128)(2,1)} %get-tuple-element.9) | copy-start | bytes 6291460
  38.8 2.9 %copy-start.5 = (f32[2048]{0:T(1024)S(1)}, f32[2048]{0:T(1024)}, u32[]{:S(2)}) copy-start(f32[2048]{0:T(1024)} %param.11) | copy-start | bytes 24580
  41.7 2.1 %copy-start.6 = (bf16[2048,256]{1,0:T(8,128)(2,1)S(1)}, bf16[2048,256]{1,0:T(8,128)(2,1)}, u32[]{:S(2)}) copy-start(bf16[2048,256]{1,0:T(8,128)(2,1)} %param.13) | copy-start | bytes 3145732
  42.4 1.4 %copy-start.2 = (bf16[512,2048]{1,0:T(8,128)(2,1)}, bf16[512,2048]{1,0:T(8,128)(2,1)S(1)}, u32[]{:S(2)}) copy-start(bf16[512,2048]{1,0:T(8,128)(2,1)S(1)} %fusion.4) | copy-start | bytes 6291460
  43.8 3.4 %copy-start.7 = (s32[1,64]{1,0:T(1,128)S(1)}, s32[1,64]{1,0:T(1,128)}, u32[]{:S(2)}) copy-start(s32[1,64]{1,0:T(1,128)} %param.18) | copy-start | bytes 772
  93.7 2.1 %copy-start.3 = (bf16[512,512]{1,0:T(8,128)(2,1)S(1)}, bf16[512,512]{1,0:T(8,128)(2,1)}, u32[]{:S(2)}) copy-start(bf16[512,512]{1,0:T(8,128)(2,1)} %tok_ref.1) | copy-start | bytes 1572868
  93.7 3.0 %copy-start.4 = (bf16[8,8,8,256]{3,2,1,0:T(8,128)(2,1)S(1)}, bf16[8,8,8,256]{3,2,1,0:T(8,128)(2,1)}, u32[]{:S(2)}) copy-start(bf16[8,8,8,256]{3,2,1,0:T(8,128)(2,1)} %get-tuple-element.15) | copy-start | bytes 786436

commit v8 on v7

--- a/solution.py
+++ b/solution.py
@@ -386,9 +386,9 @@
     )(lens, holders, sources, cache, keyval)
 
 
-def _tail_kernel(na, nb, ntp, scale, chunk, lens_ref, q_ref, fresh, kt, share_buf, w_ref,
-                 rs_out, new_out, ctx, part, psend, precv, plocal, stage, s1send, s1recv, s2send,
-                 s2recv, slocal):
+def _tail_kernel(na, nb, ntp, scale, chunk, lens_ref, q_ref, fresh, kt, share_buf, w_ref, tok_ref,
+                 mixed_out, new_out, rs_out, ctx, part, psend, precv, plocal, stage, s1send, s1recv,
+                 s2send, s2recv, slocal):
     s = lax.axis_index("seq")
     t = lax.axis_index("tp")
     rows, qcols = q_ref.shape
@@ -463,10 +463,23 @@
         return carry
 
     lax.fori_loop(0, chunks, drain, 0)
+    span = lens_ref[1]
+
+    def combine(c, carry):
+        first = pl.multiple_of(c * chunk, chunk)
+        total = tok_ref[pl.ds(first, chunk), :].astype(jnp.float32)
+        for p in range(ntp):
+            total = total + rs_out[p, pl.ds(first, chunk), :].astype(jnp.float32)
+        row_pos = first + lax.broadcasted_iota(jnp.int32, total.shape, 0)
+        mixed_out[pl.ds(first, chunk), :] = jnp.where(row_pos < span, total, 0.0).astype(
+            mixed_out.dtype)
+        return carry
+
+    lax.fori_loop(0, chunks, combine, 0)
     a2a.finish()
 
 
-def attend_and_scatter(query, cache, keyval, lens, holders, sources, w_out, na, nb, ntp,
+def attend_and_scatter(query, cache, keyval, lens, holders, sources, w_out, tokens, na, nb, ntp,
                        chunk=128):
     rows, qcols = query.shape
     blocks, block_rows, width = cache.shape
@@ -475,15 +488,16 @@
     fresh, keys_t, sorted_share = prepare(cache, keyval, lens, holders, sources, ntp)
     vmem = pl.BlockSpec(memory_space=pltpu.VMEM)
     smem = pl.BlockSpec(memory_space=pltpu.SMEM)
-    rs, new = pl.pallas_call(
+    mixed, new = pl.pallas_call(
         functools.partial(_tail_kernel, na, nb, ntp, (width // 2) ** (-0.5), chunk),
         out_shape=(
-            jax.ShapeDtypeStruct((ntp, rows, cols), jnp.bfloat16),
+            jax.ShapeDtypeStruct(tokens.shape, tokens.dtype),
             jax.ShapeDtypeStruct((na, nb, share, width), cache.dtype),
         ),
-        in_specs=[smem, vmem, vmem, vmem, vmem, vmem],
-        out_specs=(pl.BlockSpec(memory_space=pl.ANY), pl.BlockSpec(memory_space=pl.ANY)),
+        in_specs=[smem, vmem, vmem, vmem, vmem, vmem, vmem],
+        out_specs=(vmem, pl.BlockSpec(memory_space=pl.ANY)),
         scratch_shapes=[
+            pltpu.VMEM((ntp, rows, cols), jnp.bfloat16),
             pltpu.VMEM((chunk, qcols), jnp.bfloat16),
             pltpu.VMEM((rows // chunk, chunk, w_out.shape[1]), jnp.bfloat16),
             pltpu.SemaphoreType.DMA((rows // chunk, ntp)),
@@ -491,8 +505,8 @@
             pltpu.SemaphoreType.DMA((rows // chunk,)),
         ] + _seq_scratch(na, nb, share, width, cache.dtype),
         compiler_params=pltpu.CompilerParams(collective_id=1, has_side_effects=True),
-    )(lens, query, fresh, keys_t, sorted_share, w_out)
-    return rs, new.reshape(blocks, share, width)
+    )(lens, query, fresh, keys_t, sorted_share, w_out, tokens)
+    return mixed, new.reshape(blocks, share, width)
 
 
 def body(
@@ -534,14 +548,10 @@
     matches = targets[None, :] == device_ids
     sources = jnp.sum(jnp.where(matches, block_ids, 0), axis=1)
     lens = jnp.stack([held_len, span_len]).astype(jnp.int32)
-    summed, new_cache = attend_and_scatter(
+    mixed, new_cache = attend_and_scatter(
         query, cache_all.reshape(groups, block_rows, width), keyval, lens, holders, sources,
-        w_out, outer, inner, tp_count
+        w_out, tokens, outer, inner, tp_count
     )
-    row_pos = lax.broadcasted_iota(jnp.int32, (tok_rows, 1), 0)
-    summed = summed.astype(jnp.float32)
-    total = tokens.astype(jnp.float32) + jnp.sum(summed, axis=0)
-    mixed = jnp.where(row_pos < span_len, total, jnp.zeros_like(total)).astype(jnp.bfloat16)
     return (mixed, new_cache)
 
 

time: 97.6 us -> 98.6 us (1.010)
  other arithmetic: 7.77 us -> 4.75 us
  local copies, waits for them, and re-layouts: 2.19 us -> 5.01 us
  Pallas kernels: 80.4 us -> 81.6 us
    unnamed x17 -> x14, local copies, waits for them, and re-layouts: 2.19 us -> 5.01 us
    reduce_sum x1 -> x0, other arithmetic: 2.07 us -> none  [body(): total = tokens.astype(jnp.float32) + jnp.sum(summed, axis=0)]
    pallas_call x1, Pallas kernels: 37.7 us -> 38.9 us  [attend_and_scatter(): pl.pallas_call(functools.partial(_tail_kernel, na, nb, ntp, (width // 2)...]
where the time goes in v8:
time: 98.6 us; the launch traced here: 98.4 us
  Pallas kernels  81.6 us (83%)
  matrix products  5.05 us (5%)
  local copies, waits for them, and re-layouts  5.01 us (5%)
  other arithmetic  4.75 us (5%)
  between operations  2.01 us (2%)
    pallas_call x1, Pallas kernels, attend_and_scatter(): pl.pallas_call(functools.partial(_tail_kernel, na, nb, ntp, (width // 2)...  38.9 us
    pallas_call x1, Pallas kernels, gather_inputs(): pl.pallas_call(functools.partial(_in_kernel, na, nb, ntp), out_shape=(jax...  38.1 us
    unnamed x14, local copies, waits for them, and re-layouts  5.01 us
    pallas_call x1, Pallas kernels, prepare(): pl.pallas_call(functools.partial(_prep_kernel, ntp), out_shape=(jax.Shape...  4.52 us
    dot_general x1, matrix products, body(): jnp.dot(normed, w_query, preferred_element_type=jnp.float32)  3.64 us
    reduce_sum x1, other arithmetic, normalize(): average = jnp.mean(values, axis=1, keepdims=True)  2.09 us

profile of v8, /device:TPU:1, one launch (start us, length us, event | category | flops | bytes accessed | tf_op | source)
XLA Modules:
  0.0 98.4 jit_solution(9856586038505061998)
XLA Ops:
  0.6 0.0 copy-start
  0.6 38.1 %shard_map.113 = (bf16[512,2048]{1,0:T(8,128)(2,1)}, bf16[8,8,4,8,256]{4,3,2,1,0:T(8,128)(2,1)}) custom-call(bf16[512,512]{1,0:T(8,128)(2,1)} %tok_ref.3, bf16[8,8,8,256]{3,2,1,0:T(8,128)(2,1)} %bitcast.10), custom_call_target="tpu_custom_call" | custom-call | tf_op jit(solution)/shard_map/pallas_call | solution.py:198
  38.8 0.0 copy-start.1
  38.8 0.0 copy-start.3
  38.8 2.1 %convert_reduce_fusion = f32[512]{0:T(512)S(1)} fusion(bf16[512,2048]{1,0:T(8,128)(2,1)} %get-tuple-element.9), kind=kLoop, calls=%fused_computation.1 | loop fusion | flops 2096640 | bytes 2099200 | tf_op jit(solution)/shard_map/reduce_sum | solution.py:16
  40.9 0.1 copy-done.1
  41.0 0.7 fusion.2
  41.7 0.0 copy-done.3
  41.7 0.0 copy-start.4
  41.7 0.7 fusion.4
  42.4 0.0 copy-start.2
  42.4 1.3 %copy-done.2 = bf16[512,2048]{1,0:T(8,128)(2,1)} copy-done((bf16[512,2048]{1,0:T(8,128)(2,1)}, bf16[512,2048]{1,0:T(8,128)(2,1)S(1)}, u32[]{:S(2)}) %copy-start.2) | copy-done | bytes 2097176
  43.8 0.0 copy-done.4
  43.8 0.0 copy-start.5
  43.8 1.4 %convolution_convert_fusion.1.kv_ref = bf16[512,256]{1,0:T(8,128)(2,1)} fusion(bf16[512,2048]{1,0:T(8,128)(2,1)S(1)} %fusion.4, bf16[2048,256]{1,0:T(8,128)(2,1)S(1)} %copy-done.4), kind=kOutput, calls=%fused_computation.8 | convolution fusion | flops 537001984 | bytes 3407872 | tf_op jit(solution)/shard_map/dot_general | solution.py:543
  46.5 0.6 pad_add_fusion.lens_ref
  47.1 0.0 copy-done.5
  47.1 0.6 select_reduce_fusion.sources_ref
  47.8 4.5 %shard_map.114 = (bf16[2048,256]{1,0:T(8,128)(2,1)}, bf16[128,2048]{1,0:T(8,128)(2,1)}, bf16[64,8,256]{2,1,0:T(8,128)(2,1)}) custom-call(s32[2]{0:T(128)} %pad_add_fusion.lens_ref, s32[64]{0:T(128)} %bitcast.12, s32[64]{0:T(128)} %select_reduce_fusion.sources_ref, bf16[64,32,256]{2,1,0:T(8,128)(2,1)} %bitcast.9, ...), custom_call_target="tpu_custom_call" | custom-call | tf_op jit(solution)/shard_map/pallas_call | solution.py:376
  52.3 0.0 copy-done
  52.3 3.6 %convolution_convert_fusion.q_ref = bf16[512,512]{1,0:T(8,128)(2,1)} fusion(bf16[512,2048]{1,0:T(8,128)(2,1)} %copy-done.2, bf16[2048,512]{1,0:T(8,128)(2,1)S(1)} %copy-done), kind=kOutput, calls=%fused_computation.7 | convolution fusion | flops 1074003968 | bytes 4718592 | tf_op jit(solution)/shard_map/dot_general | solution.py:542
  55.9 38.9 %shard_map.115 = (bf16[512,512]{1,0:T(8,128)(2,1)}, bf16[8,8,8,256]{3,2,1,0:T(8,128)(2,1)}) custom-call(s32[2]{0:T(128)} %pad_add_fusion.lens_ref, bf16[512,512]{1,0:T(8,128)(2,1)} %convolution_convert_fusion.q_ref, bf16[2048,256]{1,0:T(8,128)(2,1)} %get-tuple-element.11.fresh, bf16[128,2048]{1,0:T(8,128)(2,1)} %get-tuple-element.12.kt, ...), custom_call_target="tpu_custom_call" | custom-call | tf_op jit(solution)/shard_map/pallas_call | solution.py:491
  94.8 1.9 %copy.16 = bf16[512,512]{1,0:T(8,128)(2,1)} copy(bf16[512,512]{1,0:T(8,128)(2,1)} %get-tuple-element.18) | data formatting | bytes 1048576
  96.7 1.7 %copy.17 = bf16[64,8,256]{2,1,0:T(8,128)(2,1)} copy(bf16[64,8,256]{2,1,0:T(8,128)(2,1)} %bitcast.11) | data formatting | bytes 524288
  (2 shorter events, 0.0 us)
Async XLA Ops:
  0.6 51.7 %copy-start = (bf16[2048,512]{1,0:T(8,128)(2,1)S(1)}, bf16[2048,512]{1,0:T(8,128)(2,1)}, u32[]{:S(2)}) copy-start(bf16[2048,512]{1,0:T(8,128)(2,1)} %param.12) | copy-start | bytes 6291460
  38.8 2.2 %copy-start.1 = (bf16[512,2048]{1,0:T(8,128)(2,1)S(1)}, bf16[512,2048]{1,0:T(8,128)(2,1)}, u32[]{:S(2)}) copy-start(bf16[512,2048]{1,0:T(8,128)(2,1)} %get-tuple-element.9) | copy-start | bytes 6291460
  38.8 2.9 %copy-start.3 = (f32[2048]{0:T(1024)S(1)}, f32[2048]{0:T(1024)}, u32[]{:S(2)}) copy-start(f32[2048]{0:T(1024)} %param.11) | copy-start | bytes 24580
  41.7 2.1 %copy-start.4 = (bf16[2048,256]{1,0:T(8,128)(2,1)S(1)}, bf16[2048,256]{1,0:T(8,128)(2,1)}, u32[]{:S(2)}) copy-start(bf16[2048,256]{1,0:T(8,128)(2,1)} %param.13) | copy-start | bytes 3145732
  42.4 1.3 %copy-start.2 = (bf16[512,2048]{1,0:T(8,128)(2,1)}, bf16[512,2048]{1,0:T(8,128)(2,1)S(1)}, u32[]{:S(2)}) copy-start(bf16[512,2048]{1,0:T(8,128)(2,1)S(1)} %fusion.4) | copy-start | bytes 6291460
  43.8 3.4 %copy-start.5 = (s32[1,64]{1,0:T(1,128)S(1)}, s32[1,64]{1,0:T(1,128)}, u32[]{:S(2)}) copy-start(s32[1,64]{1,0:T(1,128)} %param.18) | copy-start | bytes 772

commit v9 on v7

--- a/solution.py
+++ b/solution.py
@@ -122,8 +122,9 @@
     lax.fori_loop(1, n, step, 0)
 
 
-def _in_kernel(na, nb, ntp, tok_ref, cache_ref, tok_out, cache_out, tsend, trecv, csend, crecv,
-               lsem, stage, s1send, s1recv, s2send, s2recv, slocal):
+def _in_kernel(na, nb, ntp, tok_ref, cache_ref, gain_ref, wq_ref, wkv_ref, q_out, kv_out,
+               cache_out, tok_all, tsend, trecv, csend, crecv, lsem, stage, s1send, s1recv,
+               s2send, s2recv, slocal):
     s = lax.axis_index("seq")
     t = lax.axis_index("tp")
     right = lax.rem(t + 1, ntp)
@@ -133,85 +134,106 @@
     ldev = {"seq": s, "tp": left}
     rows, cols = tok_ref.shape
     half = rows // 2
-    blocks = na * nb // 2
-    _greet(na, nb, s, t, left, right)
+    _greet(na, nb, s, t, left, right, across)
 
     def tok_cols(p):
-        return pl.ds(p * cols, cols)
+        return pl.ds(pl.multiple_of(p * cols, cols), cols)
 
     a2a = SeqAllToAll(na, nb, s, t, cache_ref, stage, lambda a_src: cache_out.at[a_src, :, t],
                       (s1send, s1recv, s2send, s2recv, slocal))
     a2a.first()
 
-    own_tok = pltpu.make_async_copy(tok_ref, tok_out.at[:, tok_cols(t)], lsem.at[0])
+    own_tok = pltpu.make_async_copy(tok_ref, tok_all.at[:, tok_cols(t)], lsem.at[0])
     own_tok.start()
-    tok_r = _remote(tok_ref, tok_out.at[:, tok_cols(t)], tsend.at[0], trecv.at[0], rdev)
-    tok_l = _remote(tok_ref, tok_out.at[:, tok_cols(t)], tsend.at[1], trecv.at[1], ldev)
+    tok_r = _remote(tok_ref, tok_all.at[:, tok_cols(t)], tsend.at[0], trecv.at[0], rdev)
+    tok_l = _remote(tok_ref, tok_all.at[:, tok_cols(t)], tsend.at[1], trecv.at[1], ldev)
     tok_r.start()
     tok_l.start()
 
     a2a.second()
 
-    _remote(tok_ref, tok_out.at[:, tok_cols(left)], tsend.at[0], trecv.at[0], ldev).wait_recv()
-    fwd_r = _remote(tok_out.at[pl.ds(0, half), tok_cols(left)],
-                    tok_out.at[pl.ds(0, half), tok_cols(left)], tsend.at[2], trecv.at[2], rdev)
+    _remote(tok_ref, tok_all.at[:, tok_cols(left)], tsend.at[0], trecv.at[0], ldev).wait_recv()
+    fwd_r = _remote(tok_all.at[pl.ds(0, half), tok_cols(left)],
+                    tok_all.at[pl.ds(0, half), tok_cols(left)], tsend.at[2], trecv.at[2], rdev)
     fwd_r.start()
-    _remote(tok_ref, tok_out.at[:, tok_cols(right)], tsend.at[1], trecv.at[1], rdev).wait_recv()
-    fwd_l = _remote(tok_out.at[pl.ds(half, half), tok_cols(right)],
-                    tok_out.at[pl.ds(half, half), tok_cols(right)], tsend.at[3], trecv.at[3], ldev)
+    _remote(tok_ref, tok_all.at[:, tok_cols(right)], tsend.at[1], trecv.at[1], rdev).wait_recv()
+    fwd_l = _remote(tok_all.at[pl.ds(half, half), tok_cols(right)],
+                    tok_all.at[pl.ds(half, half), tok_cols(right)], tsend.at[3], trecv.at[3], ldev)
     fwd_l.start()
 
     a2a.arrived()
     flat = cache_out.reshape(na * nb, ntp, *cache_out.shape[3:])
     mine = flat.at[:, t]
-    cache_r = _remote(mine, mine, csend.at[0], crecv.at[0], rdev)
-    cache_l = _remote(mine, mine, csend.at[1], crecv.at[1], ldev)
-    cache_r.start()
-    cache_l.start()
-    _remote(mine, flat.at[:, left], csend.at[0], crecv.at[0], ldev).wait_recv()
-    cfwd_r = _remote(flat.at[pl.ds(0, blocks), left], flat.at[pl.ds(0, blocks), left],
-                     csend.at[2], crecv.at[2], rdev)
-    cfwd_r.start()
-    _remote(mine, flat.at[:, right], csend.at[1], crecv.at[1], rdev).wait_recv()
-    cfwd_l = _remote(flat.at[pl.ds(blocks, blocks), right], flat.at[pl.ds(blocks, blocks), right],
-                     csend.at[3], crecv.at[3], ldev)
-    cfwd_l.start()
-
-    _remote(tok_ref.at[pl.ds(0, half)], tok_out.at[pl.ds(0, half), tok_cols(across)],
+
+    def cache_to(k):
+        peer = lax.rem(t + k, ntp)
+        return _remote(mine, mine, csend.at[k], crecv.at[k], {"seq": s, "tp": peer})
+
+    def cache_from(k):
+        sender = lax.rem(t + ntp - k, ntp)
+        return _remote(mine, flat.at[:, sender], csend.at[k], crecv.at[k],
+                       {"seq": s, "tp": sender})
+
+    for k in range(1, ntp):
+        cache_to(k).start()
+
+    _remote(tok_ref.at[pl.ds(0, half)], tok_all.at[pl.ds(0, half), tok_cols(across)],
             tsend.at[2], trecv.at[2], ldev).wait_recv()
-    _remote(tok_ref.at[pl.ds(half, half)], tok_out.at[pl.ds(half, half), tok_cols(across)],
+    _remote(tok_ref.at[pl.ds(half, half)], tok_all.at[pl.ds(half, half), tok_cols(across)],
             tsend.at[3], trecv.at[3], rdev).wait_recv()
-    _remote(flat.at[pl.ds(0, blocks), t], flat.at[pl.ds(0, blocks), across],
-            csend.at[2], crecv.at[2], ldev).wait_recv()
-    _remote(flat.at[pl.ds(blocks, blocks), t], flat.at[pl.ds(blocks, blocks), across],
-            csend.at[3], crecv.at[3], rdev).wait_recv()
-    for c in (tok_r, tok_l, fwd_r, fwd_l, cache_r, cache_l, cfwd_r, cfwd_l):
+    own_tok.wait()
+
+    chunk = 128
+
+    def project(c, carry):
+        first = pl.multiple_of(c * chunk, chunk)
+        values = tok_all[pl.ds(first, chunk), :].astype(jnp.float32)
+        average = jnp.mean(values, axis=1, keepdims=True)
+        centred = values - average
+        spread = jnp.mean(centred * centred, axis=1, keepdims=True)
+        normed = (centred * lax.rsqrt(spread + EPSILON) * gain_ref[...]).astype(jnp.bfloat16)
+        q_out[pl.ds(first, chunk), :] = jnp.dot(
+            normed, wq_ref[...], preferred_element_type=jnp.float32).astype(q_out.dtype)
+        kv_out[pl.ds(first, chunk), :] = jnp.dot(
+            normed, wkv_ref[...], preferred_element_type=jnp.float32).astype(kv_out.dtype)
+        return carry
+
+    lax.fori_loop(0, rows // chunk, project, 0)
+
+    for k in range(1, ntp):
+        cache_from(k).wait_recv()
+    for c in (tok_r, tok_l, fwd_r, fwd_l):
         c.wait_send()
+    for k in range(1, ntp):
+        cache_to(k).wait_send()
     a2a.finish()
-    own_tok.wait()
-
-
-def gather_inputs(tokens, old_cache, na, nb, ntp):
+
+
+def gather_inputs(tokens, old_cache, norm_gain, w_query, w_keyval, na, nb, ntp):
     rows, cols = tokens.shape
     _, share, width = old_cache.shape
     cache4 = old_cache.reshape(na, nb, share, width)
+    vmem = pl.BlockSpec(memory_space=pltpu.VMEM)
+    anywhere = pl.BlockSpec(memory_space=pl.ANY)
     return pl.pallas_call(
         functools.partial(_in_kernel, na, nb, ntp),
         out_shape=(
-            jax.ShapeDtypeStruct((rows, ntp * cols), tokens.dtype),
+            jax.ShapeDtypeStruct((rows, w_query.shape[1]), jnp.bfloat16),
+            jax.ShapeDtypeStruct((rows, w_keyval.shape[1]), jnp.bfloat16),
             jax.ShapeDtypeStruct((na, nb, ntp, share, width), old_cache.dtype),
         ),
-        in_specs=[pl.BlockSpec(memory_space=pl.ANY)] * 2,
-        out_specs=(pl.BlockSpec(memory_space=pl.ANY), pl.BlockSpec(memory_space=pl.ANY)),
+        in_specs=[anywhere, anywhere, vmem, vmem, vmem],
+        out_specs=(vmem, vmem, anywhere),
         scratch_shapes=[
+            pltpu.VMEM((rows, ntp * cols), tokens.dtype),
             pltpu.SemaphoreType.DMA((4,)),
             pltpu.SemaphoreType.DMA((4,)),
-            pltpu.SemaphoreType.DMA((4,)),
-            pltpu.SemaphoreType.DMA((4,)),
+            pltpu.SemaphoreType.DMA((ntp,)),
+            pltpu.SemaphoreType.DMA((ntp,)),
             pltpu.SemaphoreType.DMA((2,)),
         ] + _seq_scratch(na, nb, share, width, old_cache.dtype),
         compiler_params=pltpu.CompilerParams(collective_id=0, has_side_effects=True),
-    )(tokens, cache4)
+    )(tokens, cache4, norm_gain.reshape(1, -1).astype(jnp.float32), w_query, w_keyval)
 
 
 def _out_kernel(na, nb, ntp, part_ref, share_ref, rs_out, new_out, stage_rs, rsend, rrecv, lsem,
@@ -521,12 +543,10 @@
 
     inner = min(groups, 8)
     outer = groups // inner
-    tok_all, cache_all = gather_inputs(tokens, old_cache, outer, inner, tp_count)
+    query, keyval, cache_all = gather_inputs(
+        tokens, old_cache, norm_gain, w_query, w_keyval, outer, inner, tp_count
+    )
     cache_all = cache_all.reshape(groups, tp_count, share, width)
-    full_rows = tok_all
-    normed = normalize(full_rows, norm_gain)
-    query = jnp.dot(normed, w_query, preferred_element_type=jnp.float32).astype(jnp.bfloat16)
-    keyval = jnp.dot(normed, w_keyval, preferred_element_type=jnp.float32).astype(jnp.bfloat16)
 
     targets = new_table[0]
     device_ids = lax.broadcasted_iota(jnp.int32, (groups, groups), 0)

time: 97.6 us -> 91.5 us (0.938)
  matrix products: 5.04 us -> 0 us
  Pallas kernels: 80.4 us -> 83.8 us
  other arithmetic: 7.77 us -> 4.91 us
  local copies, waits for them, and re-layouts: 2.19 us -> 0.71 us
    dot_general x2 -> x0, matrix products: 5.04 us -> none  [the longest x1 3.63 us: body(): jnp.dot(normed, w_query, preferred_element_type=jnp.float32)]
    pallas_call x1, Pallas kernels: 38.1 us -> 42.4 us  [gather_inputs(): pl.pallas_call(functools.partial(_in_kernel, na, nb, ntp), out_shape=(jax...]
    reduce_sum x2 -> x0, other arithmetic: 2.77 us -> none  [the longest x1 2.09 us: normalize(): average = jnp.mean(values, axis=1, keepdims=True)]
    unnamed x17 -> x5, local copies, waits for them, and re-layouts: 2.19 us -> 0.71 us
where the time goes in v9:
time: 91.5 us; the launch traced here: 91.3 us
  Pallas kernels  83.8 us (92%)
  other arithmetic  4.91 us (5%)
  between operations  1.97 us (2%)
    pallas_call x1, Pallas kernels, gather_inputs(): pl.pallas_call(functools.partial(_in_kernel, na, nb, ntp), out_shape=(jax...  42.4 us
    pallas_call x1, Pallas kernels, attend_and_scatter(): pl.pallas_call(functools.partial(_tail_kernel, na, nb, ntp, (width // 2)...  36.9 us
    pallas_call x1, Pallas kernels, prepare(): pl.pallas_call(functools.partial(_prep_kernel, ntp), out_shape=(jax.Shape...  4.5 us
    reduce_sum x1, other arithmetic, body(): total = tokens.astype(jnp.float32) + jnp.sum(summed, axis=0)  2.07 us

profile of v9, /device:TPU:1, one launch (start us, length us, event | category | flops | bytes accessed | tf_op | source)
XLA Modules:
  0.0 91.3 jit_solution(10146704604858363280)
XLA Ops:
  1.9 0.6 pad_add_fusion.lens_ref
  2.5 1.3 %select_reduce_fusion.sources_ref = s32[64]{0:T(128)} fusion(s32[64]{0:T(128)} %bitcast.13), kind=kLoop, calls=%fused_computation.2 | loop fusion | flops 12224 | bytes 512 | tf_op jit(solution)/shard_map/reduce_sum | solution.py:555
  3.8 42.4 %shard_map.113 = (bf16[512,512]{1,0:T(8,128)(2,1)}, bf16[512,256]{1,0:T(8,128)(2,1)}, bf16[8,8,4,8,256]{4,3,2,1,0:T(8,128)(2,1)}) custom-call(bf16[512,512]{1,0:T(8,128)(2,1)} %tok_ref.1, bf16[8,8,8,256]{3,2,1,0:T(8,128)(2,1)} %bitcast.10, f32[1,2048]{1,0:T(1,128)} %bitcast.11, bf16[2048,512]{1,0:T(8,128)(2,1)} %wq_ref.1, bf16[2048,256]{1,0:T(8,128)(2,1)} %wkv_ref.1), custom_call_target="tpu_custom_call" | custom-call | tf_op jit(solution)/shard_map/pallas_call | solution.py:218
  46.2 4.5 %shard_map.114 = (bf16[2048,256]{1,0:T(8,128)(2,1)}, bf16[128,2048]{1,0:T(8,128)(2,1)}, bf16[64,8,256]{2,1,0:T(8,128)(2,1)}) custom-call(s32[2]{0:T(128)} %pad_add_fusion.lens_ref, s32[64]{0:T(128)} %bitcast.12, s32[64]{0:T(128)} %select_reduce_fusion.sources_ref, bf16[64,32,256]{2,1,0:T(8,128)(2,1)} %bitcast.8, bf16[512,256]{1,0:T(8,128)(2,1)} %get-tuple-element.12.kv_ref), custom_call_target="tpu_custom_call" | custom-call | tf_op jit(solution)/shard_map/pallas_call | solution.py:398
  50.7 36.9 %shard_map.115 = (bf16[4,512,512]{2,1,0:T(8,128)(2,1)}, bf16[8,8,8,256]{3,2,1,0:T(8,128)(2,1)}) custom-call(s32[2]{0:T(128)} %pad_add_fusion.lens_ref, bf16[512,512]{1,0:T(8,128)(2,1)} %get-tuple-element.10.q_ref, bf16[2048,256]{1,0:T(8,128)(2,1)} %get-tuple-element.13.fresh, bf16[128,2048]{1,0:T(8,128)(2,1)} %get-tuple-element.14.kt, ...), custom_call_target="tpu_custom_call" | custom-call | tf_op jit(solution)/shard_map/pallas_call | solution.py:500
  87.6 0.0 copy-start
  87.6 0.0 copy-start.1
  87.6 2.1 %convert_reduce_fusion = f32[512,512]{1,0:T(8,128)S(1)} fusion(bf16[4,512,512]{2,1,0:T(8,128)(2,1)} %get-tuple-element.16), kind=kLoop, calls=%fused_computation | loop fusion | flops 1835008 | bytes 3145728 | tf_op jit(solution)/shard_map/reduce_sum | solution.py:563
  89.7 0.0 copy-done
  89.7 0.9 %select_convert_fusion = bf16[512,512]{1,0:T(8,128)(2,1)} fusion(f32[512,512]{1,0:T(8,128)S(1)} %convert_reduce_fusion, bf16[512,512]{1,0:T(8,128)(2,1)S(1)} %copy-done, pred[512]{0:T(512)(128)(4,1)S(1)} %iota_compare_fusion.1), kind=kLoop, calls=%fused_computation.1 | loop fusion | flops 1048576 | bytes 2097664 | tf_op jit(solution)/shard_map/convert_element_type | solution.py:564
  90.6 0.0 copy-done.1
  90.6 0.7 copy.15
  (1 shorter events, 0.0 us)
Async XLA Ops:
  87.6 2.1 %copy-start = (bf16[512,512]{1,0:T(8,128)(2,1)S(1)}, bf16[512,512]{1,0:T(8,128)(2,1)}, u32[]{:S(2)}) copy-start(bf16[512,512]{1,0:T(8,128)(2,1)} %tok_ref.1) | copy-start | bytes 1572868
  87.6 3.0 %copy-start.1 = (bf16[8,8,8,256]{3,2,1,0:T(8,128)(2,1)S(1)}, bf16[8,8,8,256]{3,2,1,0:T(8,128)(2,1)}, u32[]{:S(2)}) copy-start(bf16[8,8,8,256]{3,2,1,0:T(8,128)(2,1)} %get-tuple-element.17) | copy-start | bytes 786436

commit v10 on v9

--- a/solution.py
+++ b/solution.py
@@ -161,27 +161,27 @@
                     tok_all.at[pl.ds(half, half), tok_cols(right)], tsend.at[3], trecv.at[3], ldev)
     fwd_l.start()
 
-    a2a.arrived()
-    flat = cache_out.reshape(na * nb, ntp, *cache_out.shape[3:])
-    mine = flat.at[:, t]
-
-    def cache_to(k):
-        peer = lax.rem(t + k, ntp)
-        return _remote(mine, mine, csend.at[k], crecv.at[k], {"seq": s, "tp": peer})
-
-    def cache_from(k):
-        sender = lax.rem(t + ntp - k, ntp)
-        return _remote(mine, flat.at[:, sender], csend.at[k], crecv.at[k],
-                       {"seq": s, "tp": sender})
-
-    for k in range(1, ntp):
-        cache_to(k).start()
-
     _remote(tok_ref.at[pl.ds(0, half)], tok_all.at[pl.ds(0, half), tok_cols(across)],
             tsend.at[2], trecv.at[2], ldev).wait_recv()
     _remote(tok_ref.at[pl.ds(half, half)], tok_all.at[pl.ds(half, half), tok_cols(across)],
             tsend.at[3], trecv.at[3], rdev).wait_recv()
     own_tok.wait()
+
+    a2a.arrived()
+    flat = cache_out.reshape(na * nb, ntp, *cache_out.shape[3:])
+    mine = flat.at[:, t]
+
+    def cache_to(k):
+        peer = lax.rem(t + k, ntp)
+        return _remote(mine, mine, csend.at[k], crecv.at[k], {"seq": s, "tp": peer})
+
+    def cache_from(k):
+        sender = lax.rem(t + ntp - k, ntp)
+        return _remote(mine, flat.at[:, sender], csend.at[k], crecv.at[k],
+                       {"seq": s, "tp": sender})
+
+    for k in range(1, ntp):
+        cache_to(k).start()
 
     chunk = 128
 

time: 91.5 us -> 92.8 us (1.014)
  Pallas kernels: 83.8 us -> 85 us
where the time goes in v10:
time: 92.8 us; the launch traced here: 92.6 us
  Pallas kernels  85 us (92%)
  other arithmetic  4.91 us (5%)
  between operations  1.97 us (2%)
    pallas_call x1, Pallas kernels, gather_inputs(): pl.pallas_call(functools.partial(_in_kernel, na, nb, ntp), out_shape=(jax...  42.8 us
    pallas_call x1, Pallas kernels, attend_and_scatter(): pl.pallas_call(functools.partial(_tail_kernel, na, nb, ntp, (width // 2)...  37.8 us
    pallas_call x1, Pallas kernels, prepare(): pl.pallas_call(functools.partial(_prep_kernel, ntp), out_shape=(jax.Shape...  4.5 us
    reduce_sum x1, other arithmetic, body(): total = tokens.astype(jnp.float32) + jnp.sum(summed, axis=0)  2.07 us

profile of v10, /device:TPU:1, one launch (start us, length us, event | category | flops | bytes accessed | tf_op | source)
XLA Modules:
  0.0 92.6 jit_solution(2217745709738261203)
XLA Ops:
  1.9 0.6 pad_add_fusion.lens_ref
  2.5 1.3 %select_reduce_fusion.sources_ref = s32[64]{0:T(128)} fusion(s32[64]{0:T(128)} %bitcast.13), kind=kLoop, calls=%fused_computation.2 | loop fusion | flops 12224 | bytes 512 | tf_op jit(solution)/shard_map/reduce_sum | solution.py:555
  3.8 42.8 %shard_map.113 = (bf16[512,512]{1,0:T(8,128)(2,1)}, bf16[512,256]{1,0:T(8,128)(2,1)}, bf16[8,8,4,8,256]{4,3,2,1,0:T(8,128)(2,1)}) custom-call(bf16[512,512]{1,0:T(8,128)(2,1)} %tok_ref.1, bf16[8,8,8,256]{3,2,1,0:T(8,128)(2,1)} %bitcast.10, f32[1,2048]{1,0:T(1,128)} %bitcast.11, bf16[2048,512]{1,0:T(8,128)(2,1)} %wq_ref.1, bf16[2048,256]{1,0:T(8,128)(2,1)} %wkv_ref.1), custom_call_target="tpu_custom_call" | custom-call | tf_op jit(solution)/shard_map/pallas_call | solution.py:218
  46.6 4.5 %shard_map.114 = (bf16[2048,256]{1,0:T(8,128)(2,1)}, bf16[128,2048]{1,0:T(8,128)(2,1)}, bf16[64,8,256]{2,1,0:T(8,128)(2,1)}) custom-call(s32[2]{0:T(128)} %pad_add_fusion.lens_ref, s32[64]{0:T(128)} %bitcast.12, s32[64]{0:T(128)} %select_reduce_fusion.sources_ref, bf16[64,32,256]{2,1,0:T(8,128)(2,1)} %bitcast.8, bf16[512,256]{1,0:T(8,128)(2,1)} %get-tuple-element.12.kv_ref), custom_call_target="tpu_custom_call" | custom-call | tf_op jit(solution)/shard_map/pallas_call | solution.py:398
  51.1 37.8 %shard_map.115 = (bf16[4,512,512]{2,1,0:T(8,128)(2,1)}, bf16[8,8,8,256]{3,2,1,0:T(8,128)(2,1)}) custom-call(s32[2]{0:T(128)} %pad_add_fusion.lens_ref, bf16[512,512]{1,0:T(8,128)(2,1)} %get-tuple-element.10.q_ref, bf16[2048,256]{1,0:T(8,128)(2,1)} %get-tuple-element.13.fresh, bf16[128,2048]{1,0:T(8,128)(2,1)} %get-tuple-element.14.kt, ...), custom_call_target="tpu_custom_call" | custom-call | tf_op jit(solution)/shard_map/pallas_call | solution.py:500
  88.9 0.0 copy-start
  88.9 0.0 copy-start.1
  88.9 2.1 %convert_reduce_fusion = f32[512,512]{1,0:T(8,128)S(1)} fusion(bf16[4,512,512]{2,1,0:T(8,128)(2,1)} %get-tuple-element.16), kind=kLoop, calls=%fused_computation | loop fusion | flops 1835008 | bytes 3145728 | tf_op jit(solution)/shard_map/reduce_sum | solution.py:563
  91.0 0.0 copy-done
  91.0 0.9 %select_convert_fusion = bf16[512,512]{1,0:T(8,128)(2,1)} fusion(f32[512,512]{1,0:T(8,128)S(1)} %convert_reduce_fusion, bf16[512,512]{1,0:T(8,128)(2,1)S(1)} %copy-done, pred[512]{0:T(512)(128)(4,1)S(1)} %iota_compare_fusion.1), kind=kLoop, calls=%fused_computation.1 | loop fusion | flops 1048576 | bytes 2097664 | tf_op jit(solution)/shard_map/convert_element_type | solution.py:564
  91.9 0.0 copy-done.1
  91.9 0.7 copy.15
  (1 shorter events, 0.0 us)
Async XLA Ops:
  88.9 2.1 %copy-start = (bf16[512,512]{1,0:T(8,128)(2,1)S(1)}, bf16[512,512]{1,0:T(8,128)(2,1)}, u32[]{:S(2)}) copy-start(bf16[512,512]{1,0:T(8,128)(2,1)} %tok_ref.1) | copy-start | bytes 1572868
  88.9 3.0 %copy-start.1 = (bf16[8,8,8,256]{3,2,1,0:T(8,128)(2,1)S(1)}, bf16[8,8,8,256]{3,2,1,0:T(8,128)(2,1)}, u32[]{:S(2)}) copy-start(bf16[8,8,8,256]{3,2,1,0:T(8,128)(2,1)} %get-tuple-element.17) | copy-start | bytes 786436

commit v11 on v9

--- a/solution.py
+++ b/solution.py
@@ -489,7 +489,7 @@
 
 
 def attend_and_scatter(query, cache, keyval, lens, holders, sources, w_out, na, nb, ntp,
-                       chunk=128):
+                       chunk=64):
     rows, qcols = query.shape
     blocks, block_rows, width = cache.shape
     share = block_rows // ntp
@@ -559,8 +559,9 @@
         w_out, outer, inner, tp_count
     )
     row_pos = lax.broadcasted_iota(jnp.int32, (tok_rows, 1), 0)
-    summed = summed.astype(jnp.float32)
-    total = tokens.astype(jnp.float32) + jnp.sum(summed, axis=0)
+    total = tokens.astype(jnp.float32)
+    for p in range(tp_count):
+        total = total + summed[p].astype(jnp.float32)
     mixed = jnp.where(row_pos < span_len, total, jnp.zeros_like(total)).astype(jnp.bfloat16)
     return (mixed, new_cache)
 

time: 91.5 us -> 93.1 us (1.017)
  Pallas kernels: 83.8 us -> 85.6 us
    reduce_sum x1 -> x0, other arithmetic: 2.07 us -> none  [body(): total = tokens.astype(jnp.float32) + jnp.sum(summed, axis=0)]
    pallas_call x1, Pallas kernels: 36.9 us -> 38.7 us  [attend_and_scatter(): pl.pallas_call(functools.partial(_tail_kernel, na, nb, ntp, (width // 2)...]
    convert_element_type x1, other arithmetic: 0.94 us -> 2.72 us  [body(): jnp.where(row_pos < span_len, total, jnp.zeros_like(total))]
where the time goes in v11:
time: 93.1 us; the launch traced here: 92.9 us
  Pallas kernels  85.6 us (92%)
  other arithmetic  4.63 us (5%)
  between operations  1.96 us (2%)
    pallas_call x1, Pallas kernels, gather_inputs(): pl.pallas_call(functools.partial(_in_kernel, na, nb, ntp), out_shape=(jax...  42.4 us
    pallas_call x1, Pallas kernels, attend_and_scatter(): pl.pallas_call(functools.partial(_tail_kernel, na, nb, ntp, (width // 2)...  38.7 us
    pallas_call x1, Pallas kernels, prepare(): pl.pallas_call(functools.partial(_prep_kernel, ntp), out_shape=(jax.Shape...  4.5 us
    convert_element_type x1, other arithmetic, body(): jnp.where(row_pos < span_len, total, jnp.zeros_like(total))  2.72 us

profile of v11, /device:TPU:1, one launch (start us, length us, event | category | flops | bytes accessed | tf_op | source)
XLA Modules:
  0.0 92.9 jit_solution(6788193366875481224)
XLA Ops:
  1.9 0.6 pad_add_fusion.lens_ref
  2.5 1.3 %select_reduce_fusion.sources_ref = s32[64]{0:T(128)} fusion(s32[64]{0:T(128)} %bitcast.25), kind=kLoop, calls=%fused_computation.6 | loop fusion | flops 12224 | bytes 512 | tf_op jit(solution)/shard_map/reduce_sum | solution.py:555
  3.8 42.4 %shard_map.113 = (bf16[512,512]{1,0:T(8,128)(2,1)}, bf16[512,256]{1,0:T(8,128)(2,1)}, bf16[8,8,4,8,256]{4,3,2,1,0:T(8,128)(2,1)}) custom-call(bf16[512,512]{1,0:T(8,128)(2,1)} %tok_ref.1, bf16[8,8,8,256]{3,2,1,0:T(8,128)(2,1)} %bitcast.22, f32[1,2048]{1,0:T(1,128)} %bitcast.23, bf16[2048,512]{1,0:T(8,128)(2,1)} %wq_ref.1, bf16[2048,256]{1,0:T(8,128)(2,1)} %wkv_ref.1), custom_call_target="tpu_custom_call" | custom-call | tf_op jit(solution)/shard_map/pallas_call | solution.py:218
  46.2 4.5 %shard_map.114 = (bf16[2048,256]{1,0:T(8,128)(2,1)}, bf16[128,2048]{1,0:T(8,128)(2,1)}, bf16[64,8,256]{2,1,0:T(8,128)(2,1)}) custom-call(s32[2]{0:T(128)} %pad_add_fusion.lens_ref, s32[64]{0:T(128)} %bitcast.24, s32[64]{0:T(128)} %select_reduce_fusion.sources_ref, bf16[64,32,256]{2,1,0:T(8,128)(2,1)} %bitcast.20, bf16[512,256]{1,0:T(8,128)(2,1)} %get-tuple-element.12.kv_ref), custom_call_target="tpu_custom_call" | custom-call | tf_op jit(solution)/shard_map/pallas_call | solution.py:398
  50.7 0.0 copy-start
  50.7 38.7 %shard_map.115 = (bf16[4,512,512]{2,1,0:T(8,128)(2,1)}, bf16[8,8,8,256]{3,2,1,0:T(8,128)(2,1)}) custom-call(s32[2]{0:T(128)} %pad_add_fusion.lens_ref, bf16[512,512]{1,0:T(8,128)(2,1)} %get-tuple-element.10.q_ref, bf16[2048,256]{1,0:T(8,128)(2,1)} %get-tuple-element.13.fresh, bf16[128,2048]{1,0:T(8,128)(2,1)} %get-tuple-element.14.kt, ...), custom_call_target="tpu_custom_call" | custom-call | tf_op jit(solution)/shard_map/pallas_call | solution.py:500
  89.5 0.0 copy-start.1
  89.5 0.0 copy-done
  89.5 2.7 %fusion.1 = bf16[512,512]{1,0:T(8,128)(2,1)} fusion(bf16[512,512]{1,0:T(8,128)(2,1)S(1)} %copy-done, bf16[4,512,512]{2,1,0:T(8,128)(2,1)} %get-tuple-element.16, pred[512]{0:T(512)(128)(4,1)S(1)} %iota_compare_fusion.1), kind=kLoop, calls=%fused_computation.2 | loop fusion | flops 2883584 | bytes 3146240 | tf_op jit(solution)/shard_map/convert_element_type | solution.py:565
  92.2 0.0 copy-done.1
  92.2 0.7 copy.15
  (1 shorter events, 0.0 us)
Async XLA Ops:
  50.7 38.8 %copy-start = (bf16[512,512]{1,0:T(8,128)(2,1)S(1)}, bf16[512,512]{1,0:T(8,128)(2,1)}, u32[]{:S(2)}) copy-start(bf16[512,512]{1,0:T(8,128)(2,1)} %tok_ref.1) | copy-start | bytes 1572868
  89.5 2.7 %copy-start.1 = (bf16[8,8,8,256]{3,2,1,0:T(8,128)(2,1)S(1)}, bf16[8,8,8,256]{3,2,1,0:T(8,128)(2,1)}, u32[]{:S(2)}) copy-start(bf16[8,8,8,256]{3,2,1,0:T(8,128)(2,1)} %get-tuple-element.17) | copy-start | bytes 786436

commit v12 on v11

--- a/solution.py
+++ b/solution.py
@@ -355,15 +355,21 @@
     )(lens, query, fresh, fresh)
 
 
-def _prep_kernel(ntp, lens_ref, holders_ref, sources_ref, cache_ref, kv_ref, fresh, kt, share_buf,
-                 fresh32):
+def _prep_kernel(ntp, held_ref, span_ref, holders_ref, targets_ref, cache_ref, kv_ref, fresh, kt,
+                 share_buf, fresh32, sources_ref):
     t = lax.axis_index("tp")
     capacity, width = fresh.shape
     head_size = width // 2
     block_rows = cache_ref.shape[1]
     share = block_rows // ntp
-    held = lens_ref[0]
-    span = lens_ref[1]
+    held = held_ref[0]
+    span = span_ref[0]
+
+    def invert(b, carry):
+        sources_ref[targets_ref[b]] = b
+        return carry
+
+    lax.fori_loop(0, targets_ref.shape[0], invert, 0)
 
     def place(b, carry):
         fresh32[pl.ds(pl.multiple_of(b * block_rows, block_rows), block_rows), :] = (
@@ -390,7 +396,7 @@
     lax.fori_loop(0, share_buf.shape[0], pick, 0)
 
 
-def prepare(cache, keyval, lens, holders, sources, ntp):
+def prepare(cache, keyval, held, span, holders, targets, ntp):
     blocks, block_rows, width = cache.shape
     capacity = blocks * block_rows
     vmem = pl.BlockSpec(memory_space=pltpu.VMEM)
@@ -402,10 +408,11 @@
             jax.ShapeDtypeStruct((width // 2, capacity), cache.dtype),
             jax.ShapeDtypeStruct((blocks, block_rows // ntp, width), cache.dtype),
         ),
-        in_specs=[smem, smem, smem, vmem, vmem],
+        in_specs=[smem, smem, smem, smem, vmem, vmem],
         out_specs=(vmem, vmem, vmem),
-        scratch_shapes=[pltpu.VMEM((capacity, width), jnp.float32)],
-    )(lens, holders, sources, cache, keyval)
+        scratch_shapes=[pltpu.VMEM((capacity, width), jnp.float32),
+                        pltpu.SMEM((targets.shape[0],), jnp.int32)],
+    )(held, span, holders, targets, cache, keyval)
 
 
 def _tail_kernel(na, nb, ntp, scale, chunk, lens_ref, q_ref, fresh, kt, share_buf, w_ref,
@@ -488,13 +495,13 @@
     a2a.finish()
 
 
-def attend_and_scatter(query, cache, keyval, lens, holders, sources, w_out, na, nb, ntp,
-                       chunk=64):
+def attend_and_scatter(query, cache, keyval, held, span, holders, targets, w_out, na, nb, ntp,
+                       chunk=128):
     rows, qcols = query.shape
     blocks, block_rows, width = cache.shape
     share = block_rows // ntp
     cols = w_out.shape[1] // ntp
-    fresh, keys_t, sorted_share = prepare(cache, keyval, lens, holders, sources, ntp)
+    fresh, keys_t, sorted_share = prepare(cache, keyval, held, span, holders, targets, ntp)
     vmem = pl.BlockSpec(memory_space=pltpu.VMEM)
     smem = pl.BlockSpec(memory_space=pltpu.SMEM)
     rs, new = pl.pallas_call(
@@ -513,7 +520,7 @@
             pltpu.SemaphoreType.DMA((rows // chunk,)),
         ] + _seq_scratch(na, nb, share, width, cache.dtype),
         compiler_params=pltpu.CompilerParams(collective_id=1, has_side_effects=True),
-    )(lens, query, fresh, keys_t, sorted_share, w_out)
+    )(held, query, fresh, keys_t, sorted_share, w_out)
     return rs, new.reshape(blocks, share, width)
 
 
@@ -548,15 +555,9 @@
     )
     cache_all = cache_all.reshape(groups, tp_count, share, width)
 
-    targets = new_table[0]
-    device_ids = lax.broadcasted_iota(jnp.int32, (groups, groups), 0)
-    block_ids = lax.broadcasted_iota(jnp.int32, (groups, groups), 1)
-    matches = targets[None, :] == device_ids
-    sources = jnp.sum(jnp.where(matches, block_ids, 0), axis=1)
-    lens = jnp.stack([held_len, span_len]).astype(jnp.int32)
     summed, new_cache = attend_and_scatter(
-        query, cache_all.reshape(groups, block_rows, width), keyval, lens, holders, sources,
-        w_out, outer, inner, tp_count
+        query, cache_all.reshape(groups, block_rows, width), keyval, cached_lens, span_lens,
+        holders, new_table[0], w_out, outer, inner, tp_count
     )
     row_pos = lax.broadcasted_iota(jnp.int32, (tok_rows, 1), 0)
     total = tokens.astype(jnp.float32)

time: 93.1 us -> 89.9 us (0.966)
  other arithmetic: 4.63 us -> 2.72 us
  Pallas kernels: 85.6 us -> 84.4 us
    pallas_call x1, Pallas kernels: 38.7 us -> 36.8 us  [attend_and_scatter(): pl.pallas_call(functools.partial(_tail_kernel, na, nb, ntp, (width // 2)...]
    reduce_sum x1 -> x0, other arithmetic: 1.29 us -> none  [body(): sources = jnp.sum(jnp.where(matches, block_ids, 0), axis=1)]
where the time goes in v12:
time: 89.9 us; the launch traced here: 89.8 us
  Pallas kernels  84.4 us (94%)
  other arithmetic  2.72 us (3%)
  between operations  1.96 us (2%)
    pallas_call x1, Pallas kernels, gather_inputs(): pl.pallas_call(functools.partial(_in_kernel, na, nb, ntp), out_shape=(jax...  42.5 us
    pallas_call x1, Pallas kernels, attend_and_scatter(): pl.pallas_call(functools.partial(_tail_kernel, na, nb, ntp, (width // 2)...  36.8 us
    pallas_call x1, Pallas kernels, prepare(): pl.pallas_call(functools.partial(_prep_kernel, ntp), out_shape=(jax.Shape...  5.1 us
    convert_element_type x1, other arithmetic, body(): jnp.where(row_pos < span_len, total, jnp.zeros_like(total))  2.72 us

profile of v12, /device:TPU:1, one launch (start us, length us, event | category | flops | bytes accessed | tf_op | source)
XLA Modules:
  0.0 89.8 jit_solution(15267105651447067958)
XLA Ops:
  1.9 42.5 %shard_map.113 = (bf16[512,512]{1,0:T(8,128)(2,1)}, bf16[512,256]{1,0:T(8,128)(2,1)}, bf16[8,8,4,8,256]{4,3,2,1,0:T(8,128)(2,1)}) custom-call(bf16[512,512]{1,0:T(8,128)(2,1)} %tok_ref.1, bf16[8,8,8,256]{3,2,1,0:T(8,128)(2,1)} %bitcast.22, f32[1,2048]{1,0:T(1,128)} %bitcast.23, bf16[2048,512]{1,0:T(8,128)(2,1)} %wq_ref.1, bf16[2048,256]{1,0:T(8,128)(2,1)} %wkv_ref.1), custom_call_target="tpu_custom_call" | custom-call | tf_op jit(solution)/shard_map/pallas_call | solution.py:218
  44.5 5.1 %shard_map.114 = (bf16[2048,256]{1,0:T(8,128)(2,1)}, bf16[128,2048]{1,0:T(8,128)(2,1)}, bf16[64,8,256]{2,1,0:T(8,128)(2,1)}) custom-call(s32[1]{0:T(128)S(6)} %copy.14.held_ref.lens_ref, s32[1]{0:T(128)} %copy.13.span_ref, s32[64]{0:T(128)} %bitcast.24, s32[64]{0:T(128)} %bitcast.25, bf16[64,32,256]{2,1,0:T(8,128)(2,1)} %bitcast.20, ...), custom_call_target="tpu_custom_call" | custom-call | tf_op jit(solution)/shard_map/pallas_call | solution.py:404
  49.6 0.0 copy-start
  49.6 36.8 %shard_map.115 = (bf16[4,512,512]{2,1,0:T(8,128)(2,1)}, bf16[8,8,8,256]{3,2,1,0:T(8,128)(2,1)}) custom-call(s32[1]{0:T(128)S(6)} %copy.14.held_ref.lens_ref, bf16[512,512]{1,0:T(8,128)(2,1)} %get-tuple-element.10.q_ref, bf16[2048,256]{1,0:T(8,128)(2,1)} %get-tuple-element.13.fresh, bf16[128,2048]{1,0:T(8,128)(2,1)} %get-tuple-element.14.kt, ...), custom_call_target="tpu_custom_call" | custom-call | tf_op jit(solution)/shard_map/pallas_call | solution.py:507
  86.3 0.0 copy-start.1
  86.3 0.0 copy-done
  86.3 2.7 %fusion.1 = bf16[512,512]{1,0:T(8,128)(2,1)} fusion(bf16[512,512]{1,0:T(8,128)(2,1)S(1)} %copy-done, bf16[4,512,512]{2,1,0:T(8,128)(2,1)} %get-tuple-element.16, pred[512]{0:T(512)(128)(4,1)S(1)} %iota_compare_fusion), kind=kLoop, calls=%fused_computation.2 | loop fusion | flops 2883584 | bytes 3146240 | tf_op jit(solution)/shard_map/convert_element_type | solution.py:566
  89.1 0.0 copy-done.1
  89.1 0.7 copy.15
  (1 shorter events, 0.0 us)
Async XLA Ops:
  49.6 36.8 %copy-start = (bf16[512,512]{1,0:T(8,128)(2,1)S(1)}, bf16[512,512]{1,0:T(8,128)(2,1)}, u32[]{:S(2)}) copy-start(bf16[512,512]{1,0:T(8,128)(2,1)} %tok_ref.1) | copy-start | bytes 1572868
  86.3 2.7 %copy-start.1 = (bf16[8,8,8,256]{3,2,1,0:T(8,128)(2,1)S(1)}, bf16[8,8,8,256]{3,2,1,0:T(8,128)(2,1)}, u32[]{:S(2)}) copy-start(bf16[8,8,8,256]{3,2,1,0:T(8,128)(2,1)} %get-tuple-element.17) | copy-start | bytes 786436

commit v13 on v12

--- a/solution.py
+++ b/solution.py
@@ -511,7 +511,7 @@
             jax.ShapeDtypeStruct((na, nb, share, width), cache.dtype),
         ),
         in_specs=[smem, vmem, vmem, vmem, vmem, vmem],
-        out_specs=(pl.BlockSpec(memory_space=pl.ANY), pl.BlockSpec(memory_space=pl.ANY)),
+        out_specs=(vmem, pl.BlockSpec(memory_space=pl.ANY)),
         scratch_shapes=[
             pltpu.VMEM((chunk, qcols), jnp.bfloat16),
             pltpu.VMEM((rows // chunk, chunk, w_out.shape[1]), jnp.bfloat16),

time: 89.9 us -> 91.2 us (1.014)
  Pallas kernels: 84.4 us -> 85.6 us
    pallas_call x1, Pallas kernels: 36.8 us -> 38 us  [attend_and_scatter(): pl.pallas_call(functools.partial(_tail_kernel, na, nb, ntp, (width // 2)...]
where the time goes in v13:
time: 91.2 us; the launch traced here: 91 us
  Pallas kernels  85.6 us (94%)
  other arithmetic  2.72 us (3%)
  between operations  1.96 us (2%)
    pallas_call x1, Pallas kernels, gather_inputs(): pl.pallas_call(functools.partial(_in_kernel, na, nb, ntp), out_shape=(jax...  42.5 us
    pallas_call x1, Pallas kernels, attend_and_scatter(): pl.pallas_call(functools.partial(_tail_kernel, na, nb, ntp, (width // 2)...  38 us
    pallas_call x1, Pallas kernels, prepare(): pl.pallas_call(functools.partial(_prep_kernel, ntp), out_shape=(jax.Shape...  5.1 us
    convert_element_type x1, other arithmetic, body(): jnp.where(row_pos < span_len, total, jnp.zeros_like(total))  2.72 us

profile of v13, /device:TPU:1, one launch (start us, length us, event | category | flops | bytes accessed | tf_op | source)
XLA Modules:
  0.0 91.0 jit_solution(15539536866673546475)
XLA Ops:
  1.9 42.5 %shard_map.113 = (bf16[512,512]{1,0:T(8,128)(2,1)}, bf16[512,256]{1,0:T(8,128)(2,1)}, bf16[8,8,4,8,256]{4,3,2,1,0:T(8,128)(2,1)}) custom-call(bf16[512,512]{1,0:T(8,128)(2,1)} %tok_ref.1, bf16[8,8,8,256]{3,2,1,0:T(8,128)(2,1)} %bitcast.22, f32[1,2048]{1,0:T(1,128)} %bitcast.23, bf16[2048,512]{1,0:T(8,128)(2,1)} %wq_ref.1, bf16[2048,256]{1,0:T(8,128)(2,1)} %wkv_ref.1), custom_call_target="tpu_custom_call" | custom-call | tf_op jit(solution)/shard_map/pallas_call | solution.py:218
  44.5 5.1 %shard_map.114 = (bf16[2048,256]{1,0:T(8,128)(2,1)}, bf16[128,2048]{1,0:T(8,128)(2,1)}, bf16[64,8,256]{2,1,0:T(8,128)(2,1)}) custom-call(s32[1]{0:T(128)S(6)} %copy.14.held_ref.lens_ref, s32[1]{0:T(128)} %copy.13.span_ref, s32[64]{0:T(128)} %bitcast.24, s32[64]{0:T(128)} %bitcast.25, bf16[64,32,256]{2,1,0:T(8,128)(2,1)} %bitcast.20, ...), custom_call_target="tpu_custom_call" | custom-call | tf_op jit(solution)/shard_map/pallas_call | solution.py:404
  49.6 0.0 copy-start
  49.6 38.0 %shard_map.115 = (bf16[4,512,512]{2,1,0:T(8,128)(2,1)}, bf16[8,8,8,256]{3,2,1,0:T(8,128)(2,1)}) custom-call(s32[1]{0:T(128)S(6)} %copy.14.held_ref.lens_ref, bf16[512,512]{1,0:T(8,128)(2,1)} %get-tuple-element.10.q_ref, bf16[2048,256]{1,0:T(8,128)(2,1)} %get-tuple-element.13.fresh, bf16[128,2048]{1,0:T(8,128)(2,1)} %get-tuple-element.14.kt, ...), custom_call_target="tpu_custom_call" | custom-call | tf_op jit(solution)/shard_map/pallas_call | solution.py:507
  87.6 0.0 copy-start.1
  87.6 0.0 copy-done
  87.6 2.7 %fusion.1 = bf16[512,512]{1,0:T(8,128)(2,1)} fusion(bf16[512,512]{1,0:T(8,128)(2,1)S(1)} %copy-done, bf16[4,512,512]{2,1,0:T(8,128)(2,1)} %get-tuple-element.16, pred[512]{0:T(512)(128)(4,1)S(1)} %iota_compare_fusion), kind=kLoop, calls=%fused_computation.2 | loop fusion | flops 2883584 | bytes 3146240 | tf_op jit(solution)/shard_map/convert_element_type | solution.py:566
  90.3 0.0 copy-done.1
  90.3 0.7 copy.15
  (1 shorter events, 0.0 us)
Async XLA Ops:
  49.6 38.0 %copy-start = (bf16[512,512]{1,0:T(8,128)(2,1)S(1)}, bf16[512,512]{1,0:T(8,128)(2,1)}, u32[]{:S(2)}) copy-start(bf16[512,512]{1,0:T(8,128)(2,1)} %tok_ref.1) | copy-start | bytes 1572868
  87.6 2.7 %copy-start.1 = (bf16[8,8,8,256]{3,2,1,0:T(8,128)(2,1)S(1)}, bf16[8,8,8,256]{3,2,1,0:T(8,128)(2,1)}, u32[]{:S(2)}) copy-start(bf16[8,8,8,256]{3,2,1,0:T(8,128)(2,1)} %get-tuple-element.17) | copy-start | bytes 786436

commit v14 on v12

--- a/solution.py
+++ b/solution.py
@@ -151,6 +151,21 @@
     tok_l.start()
 
     a2a.second()
+    a2a.arrived()
+    flat = cache_out.reshape(na * nb, ntp, *cache_out.shape[3:])
+    mine = flat.at[:, t]
+
+    def cache_to(k):
+        peer = lax.rem(t + k, ntp)
+        return _remote(mine, mine, csend.at[k], crecv.at[k], {"seq": s, "tp": peer})
+
+    def cache_from(k):
+        sender = lax.rem(t + ntp - k, ntp)
+        return _remote(mine, flat.at[:, sender], csend.at[k], crecv.at[k],
+                       {"seq": s, "tp": sender})
+
+    for k in range(1, ntp):
+        cache_to(k).start()
 
     _remote(tok_ref, tok_all.at[:, tok_cols(left)], tsend.at[0], trecv.at[0], ldev).wait_recv()
     fwd_r = _remote(tok_all.at[pl.ds(0, half), tok_cols(left)],
@@ -160,22 +175,6 @@
     fwd_l = _remote(tok_all.at[pl.ds(half, half), tok_cols(right)],
                     tok_all.at[pl.ds(half, half), tok_cols(right)], tsend.at[3], trecv.at[3], ldev)
     fwd_l.start()
-
-    a2a.arrived()
-    flat = cache_out.reshape(na * nb, ntp, *cache_out.shape[3:])
-    mine = flat.at[:, t]
-
-    def cache_to(k):
-        peer = lax.rem(t + k, ntp)
-        return _remote(mine, mine, csend.at[k], crecv.at[k], {"seq": s, "tp": peer})
-
-    def cache_from(k):
-        sender = lax.rem(t + ntp - k, ntp)
-        return _remote(mine, flat.at[:, sender], csend.at[k], crecv.at[k],
-                       {"seq": s, "tp": sender})
-
-    for k in range(1, ntp):
-        cache_to(k).start()
 
     _remote(tok_ref.at[pl.ds(0, half)], tok_all.at[pl.ds(0, half), tok_cols(across)],
             tsend.at[2], trecv.at[2], ldev).wait_recv()

time: 89.9 us -> 94.1 us (1.047)
  Pallas kernels: 84.4 us -> 88.6 us
    pallas_call x1, Pallas kernels: 42.5 us -> 48.1 us  [gather_inputs(): pl.pallas_call(functools.partial(_in_kernel, na, nb, ntp), out_shape=(jax...]
    pallas_call x1, Pallas kernels: 36.8 us -> 35.4 us  [attend_and_scatter(): pl.pallas_call(functools.partial(_tail_kernel, na, nb, ntp, (width // 2)...]
where the time goes in v14:
time: 94.1 us; the launch traced here: 94 us
  Pallas kernels  88.6 us (94%)
  other arithmetic  2.72 us (3%)
  between operations  1.96 us (2%)
    pallas_call x1, Pallas kernels, gather_inputs(): pl.pallas_call(functools.partial(_in_kernel, na, nb, ntp), out_shape=(jax...  48.1 us
    pallas_call x1, Pallas kernels, attend_and_scatter(): pl.pallas_call(functools.partial(_tail_kernel, na, nb, ntp, (width // 2)...  35.4 us
    pallas_call x1, Pallas kernels, prepare(): pl.pallas_call(functools.partial(_prep_kernel, ntp), out_shape=(jax.Shape...  5.1 us
    convert_element_type x1, other arithmetic, body(): jnp.where(row_pos < span_len, total, jnp.zeros_like(total))  2.72 us

profile of v14, /device:TPU:1, one launch (start us, length us, event | category | flops | bytes accessed | tf_op | source)
XLA Modules:
  0.0 94.0 jit_solution(5811386502655134691)
XLA Ops:
  1.9 48.1 %shard_map.113 = (bf16[512,512]{1,0:T(8,128)(2,1)}, bf16[512,256]{1,0:T(8,128)(2,1)}, bf16[8,8,4,8,256]{4,3,2,1,0:T(8,128)(2,1)}) custom-call(bf16[512,512]{1,0:T(8,128)(2,1)} %tok_ref.1, bf16[8,8,8,256]{3,2,1,0:T(8,128)(2,1)} %bitcast.22, f32[1,2048]{1,0:T(1,128)} %bitcast.23, bf16[2048,512]{1,0:T(8,128)(2,1)} %wq_ref.1, bf16[2048,256]{1,0:T(8,128)(2,1)} %wkv_ref.1), custom_call_target="tpu_custom_call" | custom-call | tf_op jit(solution)/shard_map/pallas_call | solution.py:217
  50.0 5.1 %shard_map.114 = (bf16[2048,256]{1,0:T(8,128)(2,1)}, bf16[128,2048]{1,0:T(8,128)(2,1)}, bf16[64,8,256]{2,1,0:T(8,128)(2,1)}) custom-call(s32[1]{0:T(128)S(6)} %copy.14.held_ref.lens_ref, s32[1]{0:T(128)} %copy.13.span_ref, s32[64]{0:T(128)} %bitcast.24, s32[64]{0:T(128)} %bitcast.25, bf16[64,32,256]{2,1,0:T(8,128)(2,1)} %bitcast.20, ...), custom_call_target="tpu_custom_call" | custom-call | tf_op jit(solution)/shard_map/pallas_call | solution.py:403
  55.1 0.0 copy-start
  55.1 35.4 %shard_map.115 = (bf16[4,512,512]{2,1,0:T(8,128)(2,1)}, bf16[8,8,8,256]{3,2,1,0:T(8,128)(2,1)}) custom-call(s32[1]{0:T(128)S(6)} %copy.14.held_ref.lens_ref, bf16[512,512]{1,0:T(8,128)(2,1)} %get-tuple-element.10.q_ref, bf16[2048,256]{1,0:T(8,128)(2,1)} %get-tuple-element.13.fresh, bf16[128,2048]{1,0:T(8,128)(2,1)} %get-tuple-element.14.kt, ...), custom_call_target="tpu_custom_call" | custom-call | tf_op jit(solution)/shard_map/pallas_call | solution.py:506
  90.5 0.0 copy-start.1
  90.5 0.0 copy-done
  90.5 2.7 %fusion.1 = bf16[512,512]{1,0:T(8,128)(2,1)} fusion(bf16[512,512]{1,0:T(8,128)(2,1)S(1)} %copy-done, bf16[4,512,512]{2,1,0:T(8,128)(2,1)} %get-tuple-element.16, pred[512]{0:T(512)(128)(4,1)S(1)} %iota_compare_fusion), kind=kLoop, calls=%fused_computation.2 | loop fusion | flops 2883584 | bytes 3146240 | tf_op jit(solution)/shard_map/convert_element_type | solution.py:565
  93.3 0.0 copy-done.1
  93.3 0.7 copy.15
  (1 shorter events, 0.0 us)
Async XLA Ops:
  55.1 35.4 %copy-start = (bf16[512,512]{1,0:T(8,128)(2,1)S(1)}, bf16[512,512]{1,0:T(8,128)(2,1)}, u32[]{:S(2)}) copy-start(bf16[512,512]{1,0:T(8,128)(2,1)} %tok_ref.1) | copy-start | bytes 1572868
  90.5 2.7 %copy-start.1 = (bf16[8,8,8,256]{3,2,1,0:T(8,128)(2,1)S(1)}, bf16[8,8,8,256]{3,2,1,0:T(8,128)(2,1)}, u32[]{:S(2)}) copy-start(bf16[8,8,8,256]{3,2,1,0:T(8,128)(2,1)} %get-tuple-element.17) | copy-start | bytes 786436

commit v15 on v12

--- a/solution.py
+++ b/solution.py
@@ -183,7 +183,7 @@
             tsend.at[3], trecv.at[3], rdev).wait_recv()
     own_tok.wait()
 
-    chunk = 128
+    chunk = min(rows, 256)
 
     def project(c, carry):
         first = pl.multiple_of(c * chunk, chunk)

time: 89.9 us -> 89.9 us (level)
  no operation moved by 1% of the time
where the time goes in v15:
time: 89.9 us; the launch traced here: 89.8 us
  Pallas kernels  84.4 us (94%)
  other arithmetic  2.72 us (3%)
  between operations  1.96 us (2%)
    pallas_call x1, Pallas kernels, gather_inputs(): pl.pallas_call(functools.partial(_in_kernel, na, nb, ntp), out_shape=(jax...  42.5 us
    pallas_call x1, Pallas kernels, attend_and_scatter(): pl.pallas_call(functools.partial(_tail_kernel, na, nb, ntp, (width // 2)...  36.8 us
    pallas_call x1, Pallas kernels, prepare(): pl.pallas_call(functools.partial(_prep_kernel, ntp), out_shape=(jax.Shape...  5.1 us
    convert_element_type x1, other arithmetic, body(): jnp.where(row_pos < span_len, total, jnp.zeros_like(total))  2.72 us

profile of v15, /device:TPU:1, one launch (start us, length us, event | category | flops | bytes accessed | tf_op | source)
XLA Modules:
  0.0 89.8 jit_solution(4742523148874151567)
XLA Ops:
  1.9 42.5 %shard_map.113 = (bf16[512,512]{1,0:T(8,128)(2,1)}, bf16[512,256]{1,0:T(8,128)(2,1)}, bf16[8,8,4,8,256]{4,3,2,1,0:T(8,128)(2,1)}) custom-call(bf16[512,512]{1,0:T(8,128)(2,1)} %tok_ref.1, bf16[8,8,8,256]{3,2,1,0:T(8,128)(2,1)} %bitcast.22, f32[1,2048]{1,0:T(1,128)} %bitcast.23, bf16[2048,512]{1,0:T(8,128)(2,1)} %wq_ref.1, bf16[2048,256]{1,0:T(8,128)(2,1)} %wkv_ref.1), custom_call_target="tpu_custom_call" | custom-call | tf_op jit(solution)/shard_map/pallas_call | solution.py:218
  44.5 5.1 %shard_map.114 = (bf16[2048,256]{1,0:T(8,128)(2,1)}, bf16[128,2048]{1,0:T(8,128)(2,1)}, bf16[64,8,256]{2,1,0:T(8,128)(2,1)}) custom-call(s32[1]{0:T(128)S(6)} %copy.14.held_ref.lens_ref, s32[1]{0:T(128)} %copy.13.span_ref, s32[64]{0:T(128)} %bitcast.24, s32[64]{0:T(128)} %bitcast.25, bf16[64,32,256]{2,1,0:T(8,128)(2,1)} %bitcast.20, ...), custom_call_target="tpu_custom_call" | custom-call | tf_op jit(solution)/shard_map/pallas_call | solution.py:404
  49.6 0.0 copy-start
  49.6 36.8 %shard_map.115 = (bf16[4,512,512]{2,1,0:T(8,128)(2,1)}, bf16[8,8,8,256]{3,2,1,0:T(8,128)(2,1)}) custom-call(s32[1]{0:T(128)S(6)} %copy.14.held_ref.lens_ref, bf16[512,512]{1,0:T(8,128)(2,1)} %get-tuple-element.10.q_ref, bf16[2048,256]{1,0:T(8,128)(2,1)} %get-tuple-element.13.fresh, bf16[128,2048]{1,0:T(8,128)(2,1)} %get-tuple-element.14.kt, ...), custom_call_target="tpu_custom_call" | custom-call | tf_op jit(solution)/shard_map/pallas_call | solution.py:507
  86.3 0.0 copy-start.1
  86.3 0.0 copy-done
  86.3 2.7 %fusion.1 = bf16[512,512]{1,0:T(8,128)(2,1)} fusion(bf16[512,512]{1,0:T(8,128)(2,1)S(1)} %copy-done, bf16[4,512,512]{2,1,0:T(8,128)(2,1)} %get-tuple-element.16, pred[512]{0:T(512)(128)(4,1)S(1)} %iota_compare_fusion), kind=kLoop, calls=%fused_computation.2 | loop fusion | flops 2883584 | bytes 3146240 | tf_op jit(solution)/shard_map/convert_element_type | solution.py:566
  89.1 0.0 copy-done.1
  89.1 0.7 copy.15
  (1 shorter events, 0.0 us)
Async XLA Ops:
  49.6 36.8 %copy-start = (bf16[512,512]{1,0:T(8,128)(2,1)S(1)}, bf16[512,512]{1,0:T(8,128)(2,1)}, u32[]{:S(2)}) copy-start(bf16[512,512]{1,0:T(8,128)(2,1)} %tok_ref.1) | copy-start | bytes 1572868
  86.3 2.7 %copy-start.1 = (bf16[8,8,8,256]{3,2,1,0:T(8,128)(2,1)S(1)}, bf16[8,8,8,256]{3,2,1,0:T(8,128)(2,1)}, u32[]{:S(2)}) copy-start(bf16[8,8,8,256]{3,2,1,0:T(8,128)(2,1)} %get-tuple-element.17) | copy-start | bytes 786436

commit v16 on v15

--- a/solution.py
+++ b/solution.py
@@ -496,7 +496,7 @@
 
 
 def attend_and_scatter(query, cache, keyval, held, span, holders, targets, w_out, na, nb, ntp,
-                       chunk=128):
+                       chunk=256):
     rows, qcols = query.shape
     blocks, block_rows, width = cache.shape
     share = block_rows // ntp

time: 89.9 us -> 90.8 us (1.010)
  no operation moved by 1% of the time
where the time goes in v16:
time: 90.8 us; the launch traced here: 90.6 us
  Pallas kernels  85.2 us (94%)
  other arithmetic  2.72 us (3%)
  between operations  1.96 us (2%)
    pallas_call x1, Pallas kernels, gather_inputs(): pl.pallas_call(functools.partial(_in_kernel, na, nb, ntp), out_shape=(jax...  42.5 us
    pallas_call x1, Pallas kernels, attend_and_scatter(): pl.pallas_call(functools.partial(_tail_kernel, na, nb, ntp, (width // 2)...  37.6 us
    pallas_call x1, Pallas kernels, prepare(): pl.pallas_call(functools.partial(_prep_kernel, ntp), out_shape=(jax.Shape...  5.1 us
    convert_element_type x1, other arithmetic, body(): jnp.where(row_pos < span_len, total, jnp.zeros_like(total))  2.72 us

profile of v16, /device:TPU:1, one launch (start us, length us, event | category | flops | bytes accessed | tf_op | source)
XLA Modules:
  0.0 90.6 jit_solution(8101110739101722920)
XLA Ops:
  1.9 42.5 %shard_map.113 = (bf16[512,512]{1,0:T(8,128)(2,1)}, bf16[512,256]{1,0:T(8,128)(2,1)}, bf16[8,8,4,8,256]{4,3,2,1,0:T(8,128)(2,1)}) custom-call(bf16[512,512]{1,0:T(8,128)(2,1)} %tok_ref.1, bf16[8,8,8,256]{3,2,1,0:T(8,128)(2,1)} %bitcast.22, f32[1,2048]{1,0:T(1,128)} %bitcast.23, bf16[2048,512]{1,0:T(8,128)(2,1)} %wq_ref.1, bf16[2048,256]{1,0:T(8,128)(2,1)} %wkv_ref.1), custom_call_target="tpu_custom_call" | custom-call | tf_op jit(solution)/shard_map/pallas_call | solution.py:218
  44.5 5.1 %shard_map.114 = (bf16[2048,256]{1,0:T(8,128)(2,1)}, bf16[128,2048]{1,0:T(8,128)(2,1)}, bf16[64,8,256]{2,1,0:T(8,128)(2,1)}) custom-call(s32[1]{0:T(128)S(6)} %copy.14.held_ref.lens_ref, s32[1]{0:T(128)} %copy.13.span_ref, s32[64]{0:T(128)} %bitcast.24, s32[64]{0:T(128)} %bitcast.25, bf16[64,32,256]{2,1,0:T(8,128)(2,1)} %bitcast.20, ...), custom_call_target="tpu_custom_call" | custom-call | tf_op jit(solution)/shard_map/pallas_call | solution.py:404
  49.6 0.0 copy-start
  49.6 37.6 %shard_map.115 = (bf16[4,512,512]{2,1,0:T(8,128)(2,1)}, bf16[8,8,8,256]{3,2,1,0:T(8,128)(2,1)}) custom-call(s32[1]{0:T(128)S(6)} %copy.14.held_ref.lens_ref, bf16[512,512]{1,0:T(8,128)(2,1)} %get-tuple-element.10.q_ref, bf16[2048,256]{1,0:T(8,128)(2,1)} %get-tuple-element.13.fresh, bf16[128,2048]{1,0:T(8,128)(2,1)} %get-tuple-element.14.kt, ...), custom_call_target="tpu_custom_call" | custom-call | tf_op jit(solution)/shard_map/pallas_call | solution.py:507
  87.2 0.0 copy-start.1
  87.2 0.0 copy-done
  87.2 2.7 %fusion.1 = bf16[512,512]{1,0:T(8,128)(2,1)} fusion(bf16[512,512]{1,0:T(8,128)(2,1)S(1)} %copy-done, bf16[4,512,512]{2,1,0:T(8,128)(2,1)} %get-tuple-element.16, pred[512]{0:T(512)(128)(4,1)S(1)} %iota_compare_fusion), kind=kLoop, calls=%fused_computation.2 | loop fusion | flops 2883584 | bytes 3146240 | tf_op jit(solution)/shard_map/convert_element_type | solution.py:566
  89.9 0.0 copy-done.1
  89.9 0.7 copy.15
  (1 shorter events, 0.0 us)
Async XLA Ops:
  49.6 37.7 %copy-start = (bf16[512,512]{1,0:T(8,128)(2,1)S(1)}, bf16[512,512]{1,0:T(8,128)(2,1)}, u32[]{:S(2)}) copy-start(bf16[512,512]{1,0:T(8,128)(2,1)} %tok_ref.1) | copy-start | bytes 1572868
  87.2 2.7 %copy-start.1 = (bf16[8,8,8,256]{3,2,1,0:T(8,128)(2,1)S(1)}, bf16[8,8,8,256]{3,2,1,0:T(8,128)(2,1)}, u32[]{:S(2)}) copy-start(bf16[8,8,8,256]{3,2,1,0:T(8,128)(2,1)} %get-tuple-element.17) | copy-start | bytes 786436

commit v17 on v15

--- a/solution.py
+++ b/solution.py
@@ -369,14 +369,14 @@
         sources_ref[targets_ref[b]] = b
         return carry
 
-    lax.fori_loop(0, targets_ref.shape[0], invert, 0)
+    lax.fori_loop(0, targets_ref.shape[0], invert, 0, unroll=8)
 
     def place(b, carry):
         fresh32[pl.ds(pl.multiple_of(b * block_rows, block_rows), block_rows), :] = (
             cache_ref[holders_ref[b]].astype(jnp.float32))
         return carry
 
-    lax.fori_loop(0, capacity // block_rows, place, 0)
+    lax.fori_loop(0, capacity // block_rows, place, 0, unroll=8)
     padded = jnp.concatenate(
         [kv_ref[...].astype(jnp.float32),
          jnp.zeros((capacity - kv_ref.shape[0], width), jnp.float32)], axis=0)
@@ -393,7 +393,7 @@
         share_buf[d] = fresh32[pl.ds(start, share), :].astype(share_buf.dtype)
         return carry
 
-    lax.fori_loop(0, share_buf.shape[0], pick, 0)
+    lax.fori_loop(0, share_buf.shape[0], pick, 0, unroll=8)
 
 
 def prepare(cache, keyval, held, span, holders, targets, ntp):

time: 89.9 us -> 88.8 us (0.988)
  Pallas kernels: 84.4 us -> 83.2 us
    pallas_call x1, Pallas kernels: 5.1 us -> 3.93 us  [prepare(): pl.pallas_call(functools.partial(_prep_kernel, ntp), out_shape=(jax.Shape...]
where the time goes in v17:
time: 88.8 us; the launch traced here: 88.6 us
  Pallas kernels  83.2 us (94%)
  other arithmetic  2.72 us (3%)
  between operations  1.96 us (2%)
    pallas_call x1, Pallas kernels, gather_inputs(): pl.pallas_call(functools.partial(_in_kernel, na, nb, ntp), out_shape=(jax...  42.5 us
    pallas_call x1, Pallas kernels, attend_and_scatter(): pl.pallas_call(functools.partial(_tail_kernel, na, nb, ntp, (width // 2)...  36.8 us
    pallas_call x1, Pallas kernels, prepare(): pl.pallas_call(functools.partial(_prep_kernel, ntp), out_shape=(jax.Shape...  3.93 us
    convert_element_type x1, other arithmetic, body(): jnp.where(row_pos < span_len, total, jnp.zeros_like(total))  2.72 us

profile of v17, /device:TPU:1, one launch (start us, length us, event | category | flops | bytes accessed | tf_op | source)
XLA Modules:
  0.0 88.6 jit_solution(16589573438316451878)
XLA Ops:
  1.9 42.5 %shard_map.113 = (bf16[512,512]{1,0:T(8,128)(2,1)}, bf16[512,256]{1,0:T(8,128)(2,1)}, bf16[8,8,4,8,256]{4,3,2,1,0:T(8,128)(2,1)}) custom-call(bf16[512,512]{1,0:T(8,128)(2,1)} %tok_ref.1, bf16[8,8,8,256]{3,2,1,0:T(8,128)(2,1)} %bitcast.22, f32[1,2048]{1,0:T(1,128)} %bitcast.23, bf16[2048,512]{1,0:T(8,128)(2,1)} %wq_ref.1, bf16[2048,256]{1,0:T(8,128)(2,1)} %wkv_ref.1), custom_call_target="tpu_custom_call" | custom-call | tf_op jit(solution)/shard_map/pallas_call | solution.py:218
  44.5 3.9 %shard_map.114 = (bf16[2048,256]{1,0:T(8,128)(2,1)}, bf16[128,2048]{1,0:T(8,128)(2,1)}, bf16[64,8,256]{2,1,0:T(8,128)(2,1)}) custom-call(s32[1]{0:T(128)S(6)} %copy.14.held_ref.lens_ref, s32[1]{0:T(128)} %copy.13.span_ref, s32[64]{0:T(128)} %bitcast.24, s32[64]{0:T(128)} %bitcast.25, bf16[64,32,256]{2,1,0:T(8,128)(2,1)} %bitcast.20, ...), custom_call_target="tpu_custom_call" | custom-call | tf_op jit(solution)/shard_map/pallas_call | solution.py:404
  48.4 0.0 copy-start
  48.4 36.8 %shard_map.115 = (bf16[4,512,512]{2,1,0:T(8,128)(2,1)}, bf16[8,8,8,256]{3,2,1,0:T(8,128)(2,1)}) custom-call(s32[1]{0:T(128)S(6)} %copy.14.held_ref.lens_ref, bf16[512,512]{1,0:T(8,128)(2,1)} %get-tuple-element.10.q_ref, bf16[2048,256]{1,0:T(8,128)(2,1)} %get-tuple-element.13.fresh, bf16[128,2048]{1,0:T(8,128)(2,1)} %get-tuple-element.14.kt, ...), custom_call_target="tpu_custom_call" | custom-call | tf_op jit(solution)/shard_map/pallas_call | solution.py:507
  85.2 0.0 copy-start.1
  85.2 0.0 copy-done
  85.2 2.7 %fusion.1 = bf16[512,512]{1,0:T(8,128)(2,1)} fusion(bf16[512,512]{1,0:T(8,128)(2,1)S(1)} %copy-done, bf16[4,512,512]{2,1,0:T(8,128)(2,1)} %get-tuple-element.16, pred[512]{0:T(512)(128)(4,1)S(1)} %iota_compare_fusion), kind=kLoop, calls=%fused_computation.2 | loop fusion | flops 2883584 | bytes 3146240 | tf_op jit(solution)/shard_map/convert_element_type | solution.py:566
  87.9 0.0 copy-done.1
  87.9 0.7 copy.15
  (1 shorter events, 0.0 us)
Async XLA Ops:
  48.4 36.8 %copy-start = (bf16[512,512]{1,0:T(8,128)(2,1)S(1)}, bf16[512,512]{1,0:T(8,128)(2,1)}, u32[]{:S(2)}) copy-start(bf16[512,512]{1,0:T(8,128)(2,1)} %tok_ref.1) | copy-start | bytes 1572868
  85.2 2.7 %copy-start.1 = (bf16[8,8,8,256]{3,2,1,0:T(8,128)(2,1)S(1)}, bf16[8,8,8,256]{3,2,1,0:T(8,128)(2,1)}, u32[]{:S(2)}) copy-start(bf16[8,8,8,256]{3,2,1,0:T(8,128)(2,1)} %get-tuple-element.17) | copy-start | bytes 786436

commit v18 on v17

--- a/solution.py
+++ b/solution.py
@@ -369,14 +369,14 @@
         sources_ref[targets_ref[b]] = b
         return carry
 
-    lax.fori_loop(0, targets_ref.shape[0], invert, 0, unroll=8)
+    lax.fori_loop(0, targets_ref.shape[0], invert, 0, unroll=True)
 
     def place(b, carry):
         fresh32[pl.ds(pl.multiple_of(b * block_rows, block_rows), block_rows), :] = (
             cache_ref[holders_ref[b]].astype(jnp.float32))
         return carry
 
-    lax.fori_loop(0, capacity // block_rows, place, 0, unroll=8)
+    lax.fori_loop(0, capacity // block_rows, place, 0, unroll=True)
     padded = jnp.concatenate(
         [kv_ref[...].astype(jnp.float32),
          jnp.zeros((capacity - kv_ref.shape[0], width), jnp.float32)], axis=0)
@@ -393,7 +393,7 @@
         share_buf[d] = fresh32[pl.ds(start, share), :].astype(share_buf.dtype)
         return carry
 
-    lax.fori_loop(0, share_buf.shape[0], pick, 0, unroll=8)
+    lax.fori_loop(0, share_buf.shape[0], pick, 0, unroll=True)
 
 
 def prepare(cache, keyval, held, span, holders, targets, ntp):

time: 88.8 us -> 88.3 us (level)
  no operation moved by 1% of the time
where the time goes in v18:
time: 88.3 us; the launch traced here: 88.1 us
  Pallas kernels  82.7 us (94%)
  other arithmetic  2.72 us (3%)
  between operations  1.96 us (2%)
    pallas_call x1, Pallas kernels, gather_inputs(): pl.pallas_call(functools.partial(_in_kernel, na, nb, ntp), out_shape=(jax...  42.5 us
    pallas_call x1, Pallas kernels, attend_and_scatter(): pl.pallas_call(functools.partial(_tail_kernel, na, nb, ntp, (width // 2)...  36.8 us
    pallas_call x1, Pallas kernels, prepare(): pl.pallas_call(functools.partial(_prep_kernel, ntp), out_shape=(jax.Shape...  3.45 us
    convert_element_type x1, other arithmetic, body(): jnp.where(row_pos < span_len, total, jnp.zeros_like(total))  2.72 us

profile of v18, /device:TPU:1, one launch (start us, length us, event | category | flops | bytes accessed | tf_op | source)
XLA Modules:
  0.0 88.1 jit_solution(12014634379219775825)
XLA Ops:
  1.9 42.5 %shard_map.113 = (bf16[512,512]{1,0:T(8,128)(2,1)}, bf16[512,256]{1,0:T(8,128)(2,1)}, bf16[8,8,4,8,256]{4,3,2,1,0:T(8,128)(2,1)}) custom-call(bf16[512,512]{1,0:T(8,128)(2,1)} %tok_ref.1, bf16[8,8,8,256]{3,2,1,0:T(8,128)(2,1)} %bitcast.22, f32[1,2048]{1,0:T(1,128)} %bitcast.23, bf16[2048,512]{1,0:T(8,128)(2,1)} %wq_ref.1, bf16[2048,256]{1,0:T(8,128)(2,1)} %wkv_ref.1), custom_call_target="tpu_custom_call" | custom-call | tf_op jit(solution)/shard_map/pallas_call | solution.py:218
  44.5 3.4 %shard_map.114 = (bf16[2048,256]{1,0:T(8,128)(2,1)}, bf16[128,2048]{1,0:T(8,128)(2,1)}, bf16[64,8,256]{2,1,0:T(8,128)(2,1)}) custom-call(s32[1]{0:T(128)S(6)} %copy.14.held_ref.lens_ref, s32[1]{0:T(128)} %copy.13.span_ref, s32[64]{0:T(128)} %bitcast.24, s32[64]{0:T(128)} %bitcast.25, bf16[64,32,256]{2,1,0:T(8,128)(2,1)} %bitcast.20, ...), custom_call_target="tpu_custom_call" | custom-call | tf_op jit(solution)/shard_map/pallas_call | solution.py:404
  47.9 0.0 copy-start
  47.9 36.8 %shard_map.115 = (bf16[4,512,512]{2,1,0:T(8,128)(2,1)}, bf16[8,8,8,256]{3,2,1,0:T(8,128)(2,1)}) custom-call(s32[1]{0:T(128)S(6)} %copy.14.held_ref.lens_ref, bf16[512,512]{1,0:T(8,128)(2,1)} %get-tuple-element.10.q_ref, bf16[2048,256]{1,0:T(8,128)(2,1)} %get-tuple-element.13.fresh, bf16[128,2048]{1,0:T(8,128)(2,1)} %get-tuple-element.14.kt, ...), custom_call_target="tpu_custom_call" | custom-call | tf_op jit(solution)/shard_map/pallas_call | solution.py:507
  84.7 0.0 copy-start.1
  84.7 0.0 copy-done
  84.7 2.7 %fusion.1 = bf16[512,512]{1,0:T(8,128)(2,1)} fusion(bf16[512,512]{1,0:T(8,128)(2,1)S(1)} %copy-done, bf16[4,512,512]{2,1,0:T(8,128)(2,1)} %get-tuple-element.16, pred[512]{0:T(512)(128)(4,1)S(1)} %iota_compare_fusion), kind=kLoop, calls=%fused_computation.2 | loop fusion | flops 2883584 | bytes 3146240 | tf_op jit(solution)/shard_map/convert_element_type | solution.py:566
  87.4 0.0 copy-done.1
  87.4 0.7 copy.15
  (1 shorter events, 0.0 us)
Async XLA Ops:
  47.9 36.8 %copy-start = (bf16[512,512]{1,0:T(8,128)(2,1)S(1)}, bf16[512,512]{1,0:T(8,128)(2,1)}, u32[]{:S(2)}) copy-start(bf16[512,512]{1,0:T(8,128)(2,1)} %tok_ref.1) | copy-start | bytes 1572868
  84.7 2.7 %copy-start.1 = (bf16[8,8,8,256]{3,2,1,0:T(8,128)(2,1)S(1)}, bf16[8,8,8,256]{3,2,1,0:T(8,128)(2,1)}, u32[]{:S(2)}) copy-start(bf16[8,8,8,256]{3,2,1,0:T(8,128)(2,1)} %get-tuple-element.17) | copy-start | bytes 786436

commit v19 on v18

--- a/solution.py
+++ b/solution.py
@@ -43,8 +43,8 @@
                             device_id_type=MESH)
         return carry
 
-    lax.fori_loop(1, nb, one_b, 0)
-    lax.fori_loop(1, na, one_a, 0)
+    lax.fori_loop(1, nb, one_b, 0, unroll=True)
+    lax.fori_loop(1, na, one_a, 0, unroll=True)
     for p in tp_peers:
         pl.semaphore_signal(barrier, inc=1, device_id={"seq": s, "tp": p}, device_id_type=MESH)
     pl.semaphore_wait(barrier, na + nb - 2 + len(tp_peers))
@@ -119,7 +119,7 @@
         fn(k)
         return carry
 
-    lax.fori_loop(1, n, step, 0)
+    lax.fori_loop(1, n, step, 0, unroll=True)
 
 
 def _in_kernel(na, nb, ntp, tok_ref, cache_ref, gain_ref, wq_ref, wkv_ref, q_out, kv_out,

time: 88.3 us -> 88.2 us (level)
  no operation moved by 1% of the time
where the time goes in v19:
time: 88.2 us; the launch traced here: 88 us
  Pallas kernels  82.6 us (94%)
  other arithmetic  2.72 us (3%)
  between operations  1.96 us (2%)
    pallas_call x1, Pallas kernels, gather_inputs(): pl.pallas_call(functools.partial(_in_kernel, na, nb, ntp), out_shape=(jax...  42.5 us
    pallas_call x1, Pallas kernels, attend_and_scatter(): pl.pallas_call(functools.partial(_tail_kernel, na, nb, ntp, (width // 2)...  36.7 us
    pallas_call x1, Pallas kernels, prepare(): pl.pallas_call(functools.partial(_prep_kernel, ntp), out_shape=(jax.Shape...  3.45 us
    convert_element_type x1, other arithmetic, body(): jnp.where(row_pos < span_len, total, jnp.zeros_like(total))  2.72 us

profile of v19, /device:TPU:1, one launch (start us, length us, event | category | flops | bytes accessed | tf_op | source)
XLA Modules:
  0.0 88.0 jit_solution(10566188541876481970)
XLA Ops:
  1.9 42.5 %shard_map.113 = (bf16[512,512]{1,0:T(8,128)(2,1)}, bf16[512,256]{1,0:T(8,128)(2,1)}, bf16[8,8,4,8,256]{4,3,2,1,0:T(8,128)(2,1)}) custom-call(bf16[512,512]{1,0:T(8,128)(2,1)} %tok_ref.1, bf16[8,8,8,256]{3,2,1,0:T(8,128)(2,1)} %bitcast.22, f32[1,2048]{1,0:T(1,128)} %bitcast.23, bf16[2048,512]{1,0:T(8,128)(2,1)} %wq_ref.1, bf16[2048,256]{1,0:T(8,128)(2,1)} %wkv_ref.1), custom_call_target="tpu_custom_call" | custom-call | tf_op jit(solution)/shard_map/pallas_call | solution.py:218
  44.4 3.4 %shard_map.114 = (bf16[2048,256]{1,0:T(8,128)(2,1)}, bf16[128,2048]{1,0:T(8,128)(2,1)}, bf16[64,8,256]{2,1,0:T(8,128)(2,1)}) custom-call(s32[1]{0:T(128)S(6)} %copy.14.held_ref.lens_ref, s32[1]{0:T(128)} %copy.13.span_ref, s32[64]{0:T(128)} %bitcast.24, s32[64]{0:T(128)} %bitcast.25, bf16[64,32,256]{2,1,0:T(8,128)(2,1)} %bitcast.20, ...), custom_call_target="tpu_custom_call" | custom-call | tf_op jit(solution)/shard_map/pallas_call | solution.py:404
  47.8 0.0 copy-start
  47.8 36.7 %shard_map.115 = (bf16[4,512,512]{2,1,0:T(8,128)(2,1)}, bf16[8,8,8,256]{3,2,1,0:T(8,128)(2,1)}) custom-call(s32[1]{0:T(128)S(6)} %copy.14.held_ref.lens_ref, bf16[512,512]{1,0:T(8,128)(2,1)} %get-tuple-element.10.q_ref, bf16[2048,256]{1,0:T(8,128)(2,1)} %get-tuple-element.13.fresh, bf16[128,2048]{1,0:T(8,128)(2,1)} %get-tuple-element.14.kt, ...), custom_call_target="tpu_custom_call" | custom-call | tf_op jit(solution)/shard_map/pallas_call | solution.py:507
  84.6 0.0 copy-start.1
  84.6 0.0 copy-done
  84.6 2.7 %fusion.1 = bf16[512,512]{1,0:T(8,128)(2,1)} fusion(bf16[512,512]{1,0:T(8,128)(2,1)S(1)} %copy-done, bf16[4,512,512]{2,1,0:T(8,128)(2,1)} %get-tuple-element.16, pred[512]{0:T(512)(128)(4,1)S(1)} %iota_compare_fusion), kind=kLoop, calls=%fused_computation.2 | loop fusion | flops 2883584 | bytes 3146240 | tf_op jit(solution)/shard_map/convert_element_type | solution.py:566
  87.3 0.0 copy-done.1
  87.3 0.7 copy.15
  (1 shorter events, 0.0 us)
Async XLA Ops:
  47.8 36.7 %copy-start = (bf16[512,512]{1,0:T(8,128)(2,1)S(1)}, bf16[512,512]{1,0:T(8,128)(2,1)}, u32[]{:S(2)}) copy-start(bf16[512,512]{1,0:T(8,128)(2,1)} %tok_ref.1) | copy-start | bytes 1572868
  84.6 2.7 %copy-start.1 = (bf16[8,8,8,256]{3,2,1,0:T(8,128)(2,1)S(1)}, bf16[8,8,8,256]{3,2,1,0:T(8,128)(2,1)}, u32[]{:S(2)}) copy-start(bf16[8,8,8,256]{3,2,1,0:T(8,128)(2,1)} %get-tuple-element.17) | copy-start | bytes 786436

commit v20 on v18

--- a/solution.py
+++ b/solution.py
@@ -183,7 +183,7 @@
             tsend.at[3], trecv.at[3], rdev).wait_recv()
     own_tok.wait()
 
-    chunk = min(rows, 256)
+    chunk = rows
 
     def project(c, carry):
         first = pl.multiple_of(c * chunk, chunk)

time: 88.3 us -> 88.3 us (level)
  no operation moved by 1% of the time
where the time goes in v20:
time: 88.3 us; the launch traced here: 88.1 us
  Pallas kernels  82.7 us (94%)
  other arithmetic  2.72 us (3%)
  between operations  1.96 us (2%)
    pallas_call x1, Pallas kernels, gather_inputs(): pl.pallas_call(functools.partial(_in_kernel, na, nb, ntp), out_shape=(jax...  42.5 us
    pallas_call x1, Pallas kernels, attend_and_scatter(): pl.pallas_call(functools.partial(_tail_kernel, na, nb, ntp, (width // 2)...  36.8 us
    pallas_call x1, Pallas kernels, prepare(): pl.pallas_call(functools.partial(_prep_kernel, ntp), out_shape=(jax.Shape...  3.45 us
    convert_element_type x1, other arithmetic, body(): jnp.where(row_pos < span_len, total, jnp.zeros_like(total))  2.72 us

profile of v20, /device:TPU:1, one launch (start us, length us, event | category | flops | bytes accessed | tf_op | source)
XLA Modules:
  0.0 88.1 jit_solution(4423896645791003812)
XLA Ops:
  1.9 42.5 %shard_map.113 = (bf16[512,512]{1,0:T(8,128)(2,1)}, bf16[512,256]{1,0:T(8,128)(2,1)}, bf16[8,8,4,8,256]{4,3,2,1,0:T(8,128)(2,1)}) custom-call(bf16[512,512]{1,0:T(8,128)(2,1)} %tok_ref.1, bf16[8,8,8,256]{3,2,1,0:T(8,128)(2,1)} %bitcast.22, f32[1,2048]{1,0:T(1,128)} %bitcast.23, bf16[2048,512]{1,0:T(8,128)(2,1)} %wq_ref.1, bf16[2048,256]{1,0:T(8,128)(2,1)} %wkv_ref.1), custom_call_target="tpu_custom_call" | custom-call | tf_op jit(solution)/shard_map/pallas_call | solution.py:218
  44.5 3.4 %shard_map.114 = (bf16[2048,256]{1,0:T(8,128)(2,1)}, bf16[128,2048]{1,0:T(8,128)(2,1)}, bf16[64,8,256]{2,1,0:T(8,128)(2,1)}) custom-call(s32[1]{0:T(128)S(6)} %copy.14.held_ref.lens_ref, s32[1]{0:T(128)} %copy.13.span_ref, s32[64]{0:T(128)} %bitcast.24, s32[64]{0:T(128)} %bitcast.25, bf16[64,32,256]{2,1,0:T(8,128)(2,1)} %bitcast.20, ...), custom_call_target="tpu_custom_call" | custom-call | tf_op jit(solution)/shard_map/pallas_call | solution.py:404
  47.9 0.0 copy-start
  47.9 36.8 %shard_map.115 = (bf16[4,512,512]{2,1,0:T(8,128)(2,1)}, bf16[8,8,8,256]{3,2,1,0:T(8,128)(2,1)}) custom-call(s32[1]{0:T(128)S(6)} %copy.14.held_ref.lens_ref, bf16[512,512]{1,0:T(8,128)(2,1)} %get-tuple-element.10.q_ref, bf16[2048,256]{1,0:T(8,128)(2,1)} %get-tuple-element.13.fresh, bf16[128,2048]{1,0:T(8,128)(2,1)} %get-tuple-element.14.kt, ...), custom_call_target="tpu_custom_call" | custom-call | tf_op jit(solution)/shard_map/pallas_call | solution.py:507
  84.7 0.0 copy-start.1
  84.7 0.0 copy-done
  84.7 2.7 %fusion.1 = bf16[512,512]{1,0:T(8,128)(2,1)} fusion(bf16[512,512]{1,0:T(8,128)(2,1)S(1)} %copy-done, bf16[4,512,512]{2,1,0:T(8,128)(2,1)} %get-tuple-element.16, pred[512]{0:T(512)(128)(4,1)S(1)} %iota_compare_fusion), kind=kLoop, calls=%fused_computation.2 | loop fusion | flops 2883584 | bytes 3146240 | tf_op jit(solution)/shard_map/convert_element_type | solution.py:566
  87.4 0.0 copy-done.1
  87.4 0.7 copy.15
  (1 shorter events, 0.0 us)
Async XLA Ops:
  47.9 36.8 %copy-start = (bf16[512,512]{1,0:T(8,128)(2,1)S(1)}, bf16[512,512]{1,0:T(8,128)(2,1)}, u32[]{:S(2)}) copy-start(bf16[512,512]{1,0:T(8,128)(2,1)} %tok_ref.1) | copy-start | bytes 1572868
  84.7 2.7 %copy-start.1 = (bf16[8,8,8,256]{3,2,1,0:T(8,128)(2,1)S(1)}, bf16[8,8,8,256]{3,2,1,0:T(8,128)(2,1)}, u32[]{:S(2)}) copy-start(bf16[8,8,8,256]{3,2,1,0:T(8,128)(2,1)} %get-tuple-element.17) | copy-start | bytes 786436

commit v21 on v18

--- a/solution.py
+++ b/solution.py
@@ -481,7 +481,7 @@
         do_chunk(c)
         return carry
 
-    lax.fori_loop(1, chunks, rest, 0)
+    lax.fori_loop(1, chunks, rest, 0, unroll=True)
     a2a.arrived()
 
     def drain(c, carry):

time: 88.3 us -> 88.5 us (level)
  no operation moved by 1% of the time
where the time goes in v21:
time: 88.5 us; the launch traced here: 88.3 us
  Pallas kernels  82.9 us (94%)
  other arithmetic  2.72 us (3%)
  between operations  1.96 us (2%)
    pallas_call x1, Pallas kernels, gather_inputs(): pl.pallas_call(functools.partial(_in_kernel, na, nb, ntp), out_shape=(jax...  42.5 us
    pallas_call x1, Pallas kernels, attend_and_scatter(): pl.pallas_call(functools.partial(_tail_kernel, na, nb, ntp, (width // 2)...  36.9 us
    pallas_call x1, Pallas kernels, prepare(): pl.pallas_call(functools.partial(_prep_kernel, ntp), out_shape=(jax.Shape...  3.45 us
    convert_element_type x1, other arithmetic, body(): jnp.where(row_pos < span_len, total, jnp.zeros_like(total))  2.72 us

profile of v21, /device:TPU:1, one launch (start us, length us, event | category | flops | bytes accessed | tf_op | source)
XLA Modules:
  0.0 88.3 jit_solution(3651001959602808929)
XLA Ops:
  1.9 42.5 %shard_map.113 = (bf16[512,512]{1,0:T(8,128)(2,1)}, bf16[512,256]{1,0:T(8,128)(2,1)}, bf16[8,8,4,8,256]{4,3,2,1,0:T(8,128)(2,1)}) custom-call(bf16[512,512]{1,0:T(8,128)(2,1)} %tok_ref.1, bf16[8,8,8,256]{3,2,1,0:T(8,128)(2,1)} %bitcast.22, f32[1,2048]{1,0:T(1,128)} %bitcast.23, bf16[2048,512]{1,0:T(8,128)(2,1)} %wq_ref.1, bf16[2048,256]{1,0:T(8,128)(2,1)} %wkv_ref.1), custom_call_target="tpu_custom_call" | custom-call | tf_op jit(solution)/shard_map/pallas_call | solution.py:218
  44.5 3.4 %shard_map.114 = (bf16[2048,256]{1,0:T(8,128)(2,1)}, bf16[128,2048]{1,0:T(8,128)(2,1)}, bf16[64,8,256]{2,1,0:T(8,128)(2,1)}) custom-call(s32[1]{0:T(128)S(6)} %copy.14.held_ref.lens_ref, s32[1]{0:T(128)} %copy.13.span_ref, s32[64]{0:T(128)} %bitcast.24, s32[64]{0:T(128)} %bitcast.25, bf16[64,32,256]{2,1,0:T(8,128)(2,1)} %bitcast.20, ...), custom_call_target="tpu_custom_call" | custom-call | tf_op jit(solution)/shard_map/pallas_call | solution.py:404
  47.9 0.0 copy-start
  47.9 36.9 %shard_map.115 = (bf16[4,512,512]{2,1,0:T(8,128)(2,1)}, bf16[8,8,8,256]{3,2,1,0:T(8,128)(2,1)}) custom-call(s32[1]{0:T(128)S(6)} %copy.14.held_ref.lens_ref, bf16[512,512]{1,0:T(8,128)(2,1)} %get-tuple-element.10.q_ref, bf16[2048,256]{1,0:T(8,128)(2,1)} %get-tuple-element.13.fresh, bf16[128,2048]{1,0:T(8,128)(2,1)} %get-tuple-element.14.kt, ...), custom_call_target="tpu_custom_call" | custom-call | tf_op jit(solution)/shard_map/pallas_call | solution.py:507
  84.8 0.0 copy-start.1
  84.9 0.0 copy-done
  84.9 2.7 %fusion.1 = bf16[512,512]{1,0:T(8,128)(2,1)} fusion(bf16[512,512]{1,0:T(8,128)(2,1)S(1)} %copy-done, bf16[4,512,512]{2,1,0:T(8,128)(2,1)} %get-tuple-element.16, pred[512]{0:T(512)(128)(4,1)S(1)} %iota_compare_fusion), kind=kLoop, calls=%fused_computation.2 | loop fusion | flops 2883584 | bytes 3146240 | tf_op jit(solution)/shard_map/convert_element_type | solution.py:566
  87.6 0.0 copy-done.1
  87.6 0.7 copy.15
  (1 shorter events, 0.0 us)
Async XLA Ops:
  47.9 37.0 %copy-start = (bf16[512,512]{1,0:T(8,128)(2,1)S(1)}, bf16[512,512]{1,0:T(8,128)(2,1)}, u32[]{:S(2)}) copy-start(bf16[512,512]{1,0:T(8,128)(2,1)} %tok_ref.1) | copy-start | bytes 1572868
  84.8 2.7 %copy-start.1 = (bf16[8,8,8,256]{3,2,1,0:T(8,128)(2,1)S(1)}, bf16[8,8,8,256]{3,2,1,0:T(8,128)(2,1)}, u32[]{:S(2)}) copy-start(bf16[8,8,8,256]{3,2,1,0:T(8,128)(2,1)} %get-tuple-element.17) | copy-start | bytes 786436
